TPU v7x, 512 devices: a whole 4x4x16 slice. The times are simulated.
512 devices in a mesh: space: 128 (over z, y, x_lo), shot: 4 (over x_hi, core).
Axes of the slice: x: 4 (x_hi: 2, x_lo: 2; x = x_hi * 2 + x_lo), y: 4, z: 16, core: 2. Of those that a mesh axis runs over, the one named last changes fastest.
Arguments:
- velocity: float32 [1024, 192, 128], P('space'), may hold values from 1.5 to 4.5
- wave_now: float32 [4, 1024, 192, 128], P('shot', 'space'), may hold values from -6 to 6
- wave_prev: float32 [4, 1024, 192, 128], P('shot', 'space'), may hold values from -6 to 6
- adjoint_now: float32 [4, 1024, 192, 128], P('shot', 'space'), may hold values from -6 to 6
- adjoint_prev: float32 [4, 1024, 192, 128], P('shot', 'space'), may hold values from -6 to 6
- source_cells: int32 [4, 128], P('shot'), may hold values from 0 to 25165823, as said below
- wavelet: float32 [4, 10, 128], P('shot'), may hold values from -24 to 24
- receiver_cells: int32 [65536], P('space'), may hold values from 0 to 196607, as said below
- receiver_counts: int32 [128], P('space'), may hold values from 128 to 512, as said below
- observed: float32 [4, 10, 65536], P('shot', None, 'space'), may hold values from -24 to 24
Outputs:
- gradient: float32 [1024, 192, 128], P('space', 'shot')
Inputs may be any that keep to these rules, and one draw needn't show every extreme that they name: `source_cells`: flat indices into the whole grid (first dimension slowest); the 128 cells of one shot group are distinct. `receiver_cells`: flat indices within one device's block of 8 x 192 x 128 cells (first dimension slowest); the 512 cells of one block are distinct. `receiver_counts`: the live slots of a block come first.
All inputs are finite; a program needn't handle non-finite values.
Results may differ from a plain program's by a relative error of at most 0.00002.
Values sent between devices are 32-bit elements; how exact they have to be, the bound alone decides.
No kernel may reach another device: no remote copies, remote signals or barrier semaphores. Data moves between devices by JAX's collectives and lax.ppermute only.
A program may use at most 64 MiB of HBM per device.

v0:
```python
import jax
import jax.numpy as jnp
from jax import lax
from jax.sharding import PartitionSpec as P

TAPS = (-205.0 / 72.0, 8.0 / 5.0, -1.0 / 5.0, 8.0 / 315.0, -1.0 / 560.0)
COURANT = 0.09
RADIUS = 4


def exchange_edges(block):
    count = lax.axis_size("space")
    forward = [(i, i + 1) for i in range(count - 1)]
    backward = [(target, source) for source, target in forward]
    low = lax.ppermute(block[block.shape[0] - RADIUS :], "space", forward)
    high = lax.ppermute(block[:RADIUS], "space", backward)
    return low, high


def inner_laplace(block):
    length_x, extent_y, extent_z = block.shape
    padded = jnp.pad(block, ((4, 4), (4, 4), (4, 4)))
    result = 3.0 * TAPS[0] * block
    for distance in range(1, 5):
        beside_all = (
            padded[4 + distance : 4 + distance + length_x, 4 : 4 + extent_y, 4 : 4 + extent_z]
            + padded[4 - distance : 4 - distance + length_x, 4 : 4 + extent_y, 4 : 4 + extent_z]
        )
        beside_all = (
            beside_all
            + padded[4 : 4 + length_x, 4 + distance : 4 + distance + extent_y, 4 : 4 + extent_z]
            + padded[4 : 4 + length_x, 4 - distance : 4 - distance + extent_y, 4 : 4 + extent_z]
        )
        beside_all = (
            beside_all
            + padded[4 : 4 + length_x, 4 : 4 + extent_y, 4 + distance : 4 + distance + extent_z]
            + padded[4 : 4 + length_x, 4 : 4 + extent_y, 4 - distance : 4 - distance + extent_z]
        )
        result = result + TAPS[distance] * beside_all
    return result


def edge_terms(low, high, length_x):
    middle = jnp.zeros((length_x,) + low.shape[1:], low.dtype)
    widened = jnp.concatenate([low, middle, high], axis=0)
    result = None
    for distance in range(1, 5):
        beside = (
            widened[4 + distance : 4 + distance + length_x]
            + widened[4 - distance : 4 - distance + length_x]
        )
        term = TAPS[distance] * beside
        result = term if result is None else result + term
    return result


def sample_cells(field, cells):
    lanes = field.shape[-1]
    rows = field.reshape(-1, lanes)[cells // lanes]
    chosen = lax.broadcasted_iota(jnp.int32, rows.shape, 1) == (cells % lanes)[:, None]
    return jnp.sum(jnp.where(chosen, rows, 0.0), axis=1)


def place_cells(shape, cells, amounts):
    lanes = shape[-1]
    chosen = lax.broadcasted_iota(jnp.int32, (cells.shape[0], lanes), 1) == (cells % lanes)[:, None]
    rows = jnp.where(chosen, amounts[:, None], 0.0)
    size = 1
    for extent in shape:
        size *= extent
    flat = jnp.zeros((size // lanes, lanes), jnp.float32).at[cells // lanes].add(rows)
    return flat.reshape(shape)


def step(current, former, courant_sq, injected):
    low, high = exchange_edges(current)
    interior = lax.optimization_barrier(inner_laplace(current))
    lap = interior + edge_terms(low, high, current.shape[0])
    return lax.optimization_barrier(2.0 * current - former + courant_sq * lap + injected)


def per_device(
    velocity,
    wave_now,
    wave_prev,
    adjoint_now,
    adjoint_prev,
    source_cells,
    wavelet,
    receiver_cells,
    receiver_counts,
    observed,
):
    extent_x, extent_y, extent_z = velocity.shape
    block_cells = extent_x * extent_y * extent_z
    steps = wavelet.shape[1]
    courant_sq = (COURANT * velocity) ** 2
    position = lax.axis_index("space")
    local_sources = source_cells[0] - position * block_cells
    inside = (local_sources >= 0) & (local_sources < block_cells)
    source_index = jnp.where(inside, local_sources, 0)
    pulses = wavelet[0]

    current, former = wave_now[0], wave_prev[0]
    accelerations = []
    traces = []
    for t in range(steps):
        injected = place_cells(velocity.shape, source_index, jnp.where(inside, pulses[t], 0.0))
        latest = step(current, former, courant_sq, injected)
        accelerations.append(lax.optimization_barrier(latest - 2.0 * current + former))
        traces.append(sample_cells(latest, receiver_cells))
        current, former = latest, current

    live_slots = (jnp.arange(receiver_cells.shape[0], dtype=jnp.int32) < receiver_counts[0]).astype(
        jnp.float32
    )
    misfit = [(traces[t] - observed[0, t]) * live_slots for t in range(steps)]

    following, furthest = adjoint_now[0], adjoint_prev[0]
    imaging = jnp.zeros_like(velocity)
    for t in reversed(range(steps)):
        injected = place_cells(velocity.shape, receiver_cells, misfit[t])
        earlier = step(following, furthest, courant_sq, injected)
        imaging = lax.optimization_barrier(imaging + earlier * accelerations[t])
        following, furthest = earlier, following

    shots = lax.axis_size("shot")
    shot = lax.axis_index("shot")
    band_rows = extent_y // shots
    core = shot % 2
    half = shot // 2
    banded = imaging.reshape(extent_x, 2, 2, band_rows, extent_z)
    kept = lax.dynamic_index_in_dim(banded, core, axis=2, keepdims=False)
    sent = lax.dynamic_index_in_dim(banded, 1 - core, axis=2, keepdims=False)
    summed = kept + lax.ppermute(sent, "shot", [(s, s ^ 1) for s in range(shots)])
    kept = lax.dynamic_index_in_dim(summed, half, axis=1, keepdims=False)
    sent = lax.dynamic_index_in_dim(summed, 1 - half, axis=1, keepdims=False)
    own_band = kept + lax.ppermute(sent, "shot", [(s, s ^ 2) for s in range(shots)])

    offset = shot * band_rows
    factor = lax.dynamic_slice_in_dim(-2.0 / velocity**3, offset, band_rows, 1)
    return factor * own_band


def solution(mesh):
    in_specs = (
        P("space", None, None),
        P("shot", "space", None, None),
        P("shot", "space", None, None),
        P("shot", "space", None, None),
        P("shot", "space", None, None),
        P("shot", None),
        P("shot", None, None),
        P("space"),
        P("space"),
        P("shot", None, "space"),
    )
    out_specs = P("space", "shot", None)
    return jax.shard_map(
        per_device, mesh=mesh, in_specs=in_specs, out_specs=out_specs, check_vma=False
    )
```

profile of v0, /device:TPU:160, one launch (start us, length us, event | category | flops | bytes accessed | tf_op | source)
XLA Modules:
  0.0 540.7 jit_solution(14476006756844071155)
XLA Ops:
  1.3 5.4 collective-permute-start.2
  16.2 8.6 %collective-permute-done.3 = f32[4,192,128]{2,1,0:T(8,128)} collective-permute-done((f32[4,192,128]{2,1,0:T(8,128)S(1)}, f32[4,192,128]{2,1,0:T(8,128)}, u32[]{:S(2)}, u32[]{:S(2)}) %collective-permute-start.3) | collective-permute-done | bytes 393248 | tf_op jit(solution)/shard_map/ppermute | solution.py:15
  41.3 6.2 %collective-permute-done.5 = f32[4,192,128]{2,1,0:T(8,128)} collective-permute-done((f32[4,192,128]{2,1,0:T(8,128)S(1)}, f32[4,192,128]{2,1,0:T(8,128)}, u32[]{:S(2)}, u32[]{:S(2)}) %collective-permute-start.5) | collective-permute-done | bytes 393248 | tf_op jit(solution)/shard_map/ppermute | solution.py:15
  52.4 3.4 collective-permute-start.7
  63.7 6.1 %collective-permute-done.7 = f32[4,192,128]{2,1,0:T(8,128)} collective-permute-done((f32[4,192,128]{2,1,0:T(8,128)S(1)}, f32[4,192,128]{2,1,0:T(8,128)}, u32[]{:S(2)}, u32[]{:S(2)}) %collective-permute-start.7) | collective-permute-done | bytes 393248 | tf_op jit(solution)/shard_map/ppermute | solution.py:15
  74.4 4.5 collective-permute-start.9
  87.2 7.2 %collective-permute-done.9 = f32[4,192,128]{2,1,0:T(8,128)} collective-permute-done((f32[4,192,128]{2,1,0:T(8,128)S(1)}, f32[4,192,128]{2,1,0:T(8,128)}, u32[]{:S(2)}, u32[]{:S(2)}) %collective-permute-start.9) | collective-permute-done | bytes 393248 | tf_op jit(solution)/shard_map/ppermute | solution.py:15
  97.6 5.4 collective-permute-start.10
  107.6 12.2 %fusion.449 = f32[8,192,128]{2,1,0:T(8,128)S(1)} fusion(f32[8,192,128]{2,1,0:T(8,128)} %copy-done.1), kind=kLoop, calls=%fused_computation.1119 | loop fusion | flops 5701632 | bytes 1572864 | tf_op jit(solution)/shard_map/add | solution.py:39
  123.0 6.9 %collective-permute-start.12 = (f32[4,192,128]{2,1,0:T(8,128)}, f32[4,192,128]{2,1,0:T(8,128)}, u32[]{:S(2)}, u32[]{:S(2)}) collective-permute-start(f32[4,192,128]{2,1,0:T(8,128)} %get-tuple-element.76), channel_id=1, source_target_pairs={{4,0},{8,4},{12,8},{16,12},{20,16},{24,20},{28,24},{32,28},{36,32}... | collective-permute-start | bytes 1179656 | tf_op jit(solution)/shard_map/ppermute | solution.py:16
  132.9 6.9 %collective-permute-start = (f32[4,192,128]{2,1,0:T(8,128)}, f32[4,192,128]{2,1,0:T(8,128)}, u32[]{:S(2)}, u32[]{:S(2)}) collective-permute-start(f32[4,192,128]{2,1,0:T(8,128)} %get-tuple-element.66), channel_id=1, source_target_pairs={{4,0},{8,4},{12,8},{16,12},{20,16},{24,20},{28,24},{32,28},{36,32}... | collective-permute-start | bytes 1179656 | tf_op jit(solution)/shard_map/ppermute | solution.py:16
  144.3 10.9 %fusion.477 = f32[8,192,128]{2,1,0:T(8,128)S(1)} fusion(f32[8,192,128]{2,1,0:T(8,128)} %copy-done.5), kind=kLoop, calls=%fused_computation.1147 | loop fusion | flops 5701632 | bytes 1572864 | tf_op jit(solution)/shard_map/add | solution.py:39
  158.5 6.9 %collective-permute-start.14 = (f32[4,192,128]{2,1,0:T(8,128)}, f32[4,192,128]{2,1,0:T(8,128)}, u32[]{:S(2)}, u32[]{:S(2)}) collective-permute-start(f32[4,192,128]{2,1,0:T(8,128)} %get-tuple-element.74), channel_id=1, source_target_pairs={{4,0},{8,4},{12,8},{16,12},{20,16},{24,20},{28,24},{32,28},{36,32}... | collective-permute-start | bytes 1179656 | tf_op jit(solution)/shard_map/ppermute | solution.py:16
  167.4 3.3 fusion.309
  173.3 10.9 %fusion.505 = f32[8,192,128]{2,1,0:T(8,128)S(1)} fusion(f32[8,192,128]{2,1,0:T(8,128)} %copy-done.9), kind=kLoop, calls=%fused_computation.1175 | loop fusion | flops 5701632 | bytes 1572864 | tf_op jit(solution)/shard_map/add | solution.py:39
  187.6 6.9 %collective-permute-start.16 = (f32[4,192,128]{2,1,0:T(8,128)}, f32[4,192,128]{2,1,0:T(8,128)}, u32[]{:S(2)}, u32[]{:S(2)}) collective-permute-start(f32[4,192,128]{2,1,0:T(8,128)} %get-tuple-element.72), channel_id=1, source_target_pairs={{4,0},{8,4},{12,8},{16,12},{20,16},{24,20},{28,24},{32,28},{36,32}... | collective-permute-start | bytes 1179656 | tf_op jit(solution)/shard_map/ppermute | solution.py:16
  199.9 10.8 %fusion.533 = f32[8,192,128]{2,1,0:T(8,128)S(1)} fusion(f32[8,192,128]{2,1,0:T(8,128)} %copy-done.13), kind=kLoop, calls=%fused_computation.1203 | loop fusion | flops 5701632 | bytes 1572864 | tf_op jit(solution)/shard_map/add | solution.py:39
  214.1 6.9 %collective-permute-start.18 = (f32[4,192,128]{2,1,0:T(8,128)}, f32[4,192,128]{2,1,0:T(8,128)}, u32[]{:S(2)}, u32[]{:S(2)}) collective-permute-start(f32[4,192,128]{2,1,0:T(8,128)} %get-tuple-element.70), channel_id=1, source_target_pairs={{4,0},{8,4},{12,8},{16,12},{20,16},{24,20},{28,24},{32,28},{36,32}... | collective-permute-start | bytes 1179656 | tf_op jit(solution)/shard_map/ppermute | solution.py:16
  225.5 11.1 %fusion.561 = f32[8,192,128]{2,1,0:T(8,128)S(1)} fusion(f32[8,192,128]{2,1,0:T(8,128)} %copy-done.17), kind=kLoop, calls=%fused_computation.1231 | loop fusion | flops 5701632 | bytes 1572864 | tf_op jit(solution)/shard_map/add | solution.py:39
  240.1 6.9 %collective-permute-start.20 = (f32[4,192,128]{2,1,0:T(8,128)}, f32[4,192,128]{2,1,0:T(8,128)}, u32[]{:S(2)}, u32[]{:S(2)}) collective-permute-start(f32[4,192,128]{2,1,0:T(8,128)} %get-tuple-element.68), channel_id=1, source_target_pairs={{4,0},{8,4},{12,8},{16,12},{20,16},{24,20},{28,24},{32,28},{36,32}... | collective-permute-start | bytes 1179656 | tf_op jit(solution)/shard_map/ppermute | solution.py:16
  270.8 11.9 %fusion.589 = f32[8,192,128]{2,1,0:T(8,128)} fusion(f32[8,192,128]{2,1,0:T(8,128)} %copy-done.20), kind=kLoop, calls=%fused_computation.1259 | loop fusion | flops 5701632 | bytes 1572864 | tf_op jit(solution)/shard_map/add | solution.py:39
  285.4 3.8 fusion.158
  295.1 3.3 scatter_custom_fusion.10
  302.5 7.0 %collective-permute-start.22 = (f32[4,192,128]{2,1,0:T(8,128)}, f32[4,192,128]{2,1,0:T(8,128)S(1)}, u32[]{:S(2)}, u32[]{:S(2)}) collective-permute-start(f32[4,192,128]{2,1,0:T(8,128)} %get-tuple-element.64), channel_id=1, source_target_pairs={{4,0},{8,4},{12,8},{16,12},{20,16},{24,20},{28,24},{32,28},{36,32}... | collective-permute-start | bytes 1179656 | tf_op jit(solution)/shard_map/ppermute | solution.py:16
  311.8 3.8 bitcast_add_fusion
  315.5 3.3 fusion.617
  326.0 6.5 %collective-permute-start.24 = (f32[4,192,128]{2,1,0:T(8,128)S(1)}, f32[4,192,128]{2,1,0:T(8,128)S(1)}, u32[]{:S(2)}, u32[]{:S(2)}) collective-permute-start(f32[4,192,128]{2,1,0:T(8,128)S(1)} %get-tuple-element.60), channel_id=1, source_target_pairs={{4,0},{8,4},{12,8},{16,12},{20,16},{24,20},{28,24},{32,28},{36,32}... | collective-permute-start | bytes 1179656 | tf_op jit(solution)/shard_map/ppermute | solution.py:16
  334.5 3.3 scatter_custom_fusion.12
  340.5 5.0 collective-permute-done.25
  350.5 3.9 collective-permute-start.27
  354.4 3.6 scatter_custom_fusion.13
  368.7 3.6 collective-permute-start.29
  372.4 3.3 scatter_custom_fusion.14
  385.1 9.7 %collective-permute-start.30 = (f32[4,192,128]{2,1,0:T(8,128)S(1)}, f32[4,192,128]{2,1,0:T(8,128)S(1)}, u32[]{:S(2)}, u32[]{:S(2)}) collective-permute-start(f32[4,192,128]{2,1,0:T(8,128)S(1)} %get-tuple-element.48), channel_id=1, source_target_pairs={{4,0},{8,4},{12,8},{16,12},{20,16},{24,20},{28,24},{32,28},{36,32}... | collective-permute-start | bytes 1179656 | tf_op jit(solution)/shard_map/ppermute | solution.py:16
  396.8 3.3 scatter_custom_fusion.15
  402.7 5.1 collective-permute-done.31
  411.0 5.9 %collective-permute-start.32 = (f32[4,192,128]{2,1,0:T(8,128)S(1)}, f32[4,192,128]{2,1,0:T(8,128)S(1)}, u32[]{:S(2)}, u32[]{:S(2)}) collective-permute-start(f32[4,192,128]{2,1,0:T(8,128)S(1)} %get-tuple-element.44), channel_id=1, source_target_pairs={{4,0},{8,4},{12,8},{16,12},{20,16},{24,20},{28,24},{32,28},{36,32}... | collective-permute-start | bytes 1179656 | tf_op jit(solution)/shard_map/ppermute | solution.py:16
  424.6 5.3 collective-permute-done.33
  433.0 30.5 %collective-permute-start.34 = (f32[4,192,128]{2,1,0:T(8,128)S(1)}, f32[4,192,128]{2,1,0:T(8,128)S(1)}, u32[]{:S(2)}, u32[]{:S(2)}) collective-permute-start(f32[4,192,128]{2,1,0:T(8,128)S(1)} %get-tuple-element.40), channel_id=1, source_target_pairs={{4,0},{8,4},{12,8},{16,12},{20,16},{24,20},{28,24},{32,28},{36,32}... | collective-permute-start | bytes 1179656 | tf_op jit(solution)/shard_map/ppermute | solution.py:16
  465.4 3.4 scatter_custom_fusion.17
  471.3 7.1 %collective-permute-done.35 = f32[4,192,128]{2,1,0:T(8,128)} collective-permute-done((f32[4,192,128]{2,1,0:T(8,128)S(1)}, f32[4,192,128]{2,1,0:T(8,128)}, u32[]{:S(2)}, u32[]{:S(2)}) %collective-permute-start.35) | collective-permute-done | bytes 393248 | tf_op jit(solution)/shard_map/ppermute | solution.py:15
  481.6 5.0 collective-permute-start.36
  488.6 3.5 scatter_custom_fusion.18
  495.5 4.2 collective-permute-done.37
  502.9 7.6 %collective-permute-start.38 = (f32[4,192,128]{2,1,0:T(8,128)S(1)}, f32[4,192,128]{2,1,0:T(8,128)S(1)}, u32[]{:S(2)}, u32[]{:S(2)}) collective-permute-start(f32[4,192,128]{2,1,0:T(8,128)S(1)} %get-tuple-element.32), channel_id=1, source_target_pairs={{4,0},{8,4},{12,8},{16,12},{20,16},{24,20},{28,24},{32,28},{36,32}... | collective-permute-start | bytes 1179656 | tf_op jit(solution)/shard_map/ppermute | solution.py:16
  518.3 4.9 collective-permute-done.39
  529.5 4.6 collective-permute-start.41
  534.2 5.7 %collective-permute-done.41 = f32[8,48,128]{2,1,0:T(8,128)S(1)} collective-permute-done((f32[8,48,128]{2,1,0:T(8,128)S(1)}, f32[8,48,128]{2,1,0:T(8,128)S(1)}, u32[]{:S(2)}, u32[]{:S(2)}) %collective-permute-start.41) | collective-permute-done | bytes 196640 | tf_op jit(solution)/shard_map/ppermute | solution.py:138
  (314 shorter events, 222.4 us)
Async XLA Ops:
  1.3 14.9 %collective-permute-start.2 = (f32[4,192,128]{2,1,0:T(8,128)S(1)}, f32[4,192,128]{2,1,0:T(8,128)S(1)}, u32[]{:S(2)}, u32[]{:S(2)}) collective-permute-start(f32[4,192,128]{2,1,0:T(8,128)S(1)} %get-tuple-element.86), channel_id=1, source_target_pairs={{4,0},{8,4},{12,8},{16,12},{20,16},{24,20},{28,24},{32,28},{36,32}... | collective-permute-start | bytes 1179656 | tf_op jit(solution)/shard_map/ppermute | solution.py:16
  6.7 18.1 %collective-permute-start.3 = (f32[4,192,128]{2,1,0:T(8,128)S(1)}, f32[4,192,128]{2,1,0:T(8,128)}, u32[]{:S(2)}, u32[]{:S(2)}) collective-permute-start(f32[4,192,128]{2,1,0:T(8,128)S(1)} %get-tuple-element.85), channel_id=1, source_target_pairs={{0,4},{4,8},{8,12},{12,16},{16,20},{20,24},{24,28},{28,32},{32,36}... | collective-permute-start | bytes 1179656 | tf_op jit(solution)/shard_map/ppermute | solution.py:15
  9.1 15.7 %copy-start.33 = (f32[1,8,192,128]{3,2,1,0:T(8,128)S(1)}, f32[1,8,192,128]{3,2,1,0:T(8,128)}, u32[]{:S(2)}) copy-start(f32[1,8,192,128]{3,2,1,0:T(8,128)} %param.12) | copy-start | bytes 2359300
  26.9 14.4 %collective-permute-start.4 = (f32[4,192,128]{2,1,0:T(8,128)S(1)}, f32[4,192,128]{2,1,0:T(8,128)S(1)}, u32[]{:S(2)}, u32[]{:S(2)}) collective-permute-start(f32[4,192,128]{2,1,0:T(8,128)S(1)} %get-tuple-element.84), channel_id=1, source_target_pairs={{4,0},{8,4},{12,8},{16,12},{20,16},{24,20},{28,24},{32,28},{36,32}... | collective-permute-start | bytes 1179656 | tf_op jit(solution)/shard_map/ppermute | solution.py:16
  30.2 17.3 %collective-permute-start.5 = (f32[4,192,128]{2,1,0:T(8,128)S(1)}, f32[4,192,128]{2,1,0:T(8,128)}, u32[]{:S(2)}, u32[]{:S(2)}) collective-permute-start(f32[4,192,128]{2,1,0:T(8,128)S(1)} %get-tuple-element.83), channel_id=1, source_target_pairs={{0,4},{4,8},{8,12},{12,16},{16,20},{20,24},{24,28},{28,32},{32,36}... | collective-permute-start | bytes 1179656 | tf_op jit(solution)/shard_map/ppermute | solution.py:15
  49.3 14.4 %collective-permute-start.6 = (f32[4,192,128]{2,1,0:T(8,128)S(1)}, f32[4,192,128]{2,1,0:T(8,128)S(1)}, u32[]{:S(2)}, u32[]{:S(2)}) collective-permute-start(f32[4,192,128]{2,1,0:T(8,128)S(1)} %get-tuple-element.82), channel_id=1, source_target_pairs={{4,0},{8,4},{12,8},{16,12},{20,16},{24,20},{28,24},{32,28},{36,32}... | collective-permute-start | bytes 1179656 | tf_op jit(solution)/shard_map/ppermute | solution.py:16
  52.4 17.5 %collective-permute-start.7 = (f32[4,192,128]{2,1,0:T(8,128)S(1)}, f32[4,192,128]{2,1,0:T(8,128)}, u32[]{:S(2)}, u32[]{:S(2)}) collective-permute-start(f32[4,192,128]{2,1,0:T(8,128)S(1)} %get-tuple-element.81), channel_id=1, source_target_pairs={{0,4},{4,8},{8,12},{12,16},{16,20},{20,24},{24,28},{28,32},{32,36}... | collective-permute-start | bytes 1179656 | tf_op jit(solution)/shard_map/ppermute | solution.py:15
  72.5 14.7 %collective-permute-start.8 = (f32[4,192,128]{2,1,0:T(8,128)}, f32[4,192,128]{2,1,0:T(8,128)}, u32[]{:S(2)}, u32[]{:S(2)}) collective-permute-start(f32[4,192,128]{2,1,0:T(8,128)} %get-tuple-element.80), channel_id=1, source_target_pairs={{4,0},{8,4},{12,8},{16,12},{20,16},{24,20},{28,24},{32,28},{36,32}... | collective-permute-start | bytes 1179656 | tf_op jit(solution)/shard_map/ppermute | solution.py:16
  74.4 20.0 %collective-permute-start.9 = (f32[4,192,128]{2,1,0:T(8,128)S(1)}, f32[4,192,128]{2,1,0:T(8,128)}, u32[]{:S(2)}, u32[]{:S(2)}) collective-permute-start(f32[4,192,128]{2,1,0:T(8,128)S(1)} %get-tuple-element.79), channel_id=1, source_target_pairs={{0,4},{4,8},{8,12},{12,16},{16,20},{20,24},{24,28},{28,32},{32,36}... | collective-permute-start | bytes 1179656 | tf_op jit(solution)/shard_map/ppermute | solution.py:15
  97.6 22.3 %collective-permute-start.10 = (f32[4,192,128]{2,1,0:T(8,128)}, f32[4,192,128]{2,1,0:T(8,128)}, u32[]{:S(2)}, u32[]{:S(2)}) collective-permute-start(f32[4,192,128]{2,1,0:T(8,128)} %get-tuple-element.78), channel_id=1, source_target_pairs={{4,0},{8,4},{12,8},{16,12},{20,16},{24,20},{28,24},{32,28},{36,32}... | collective-permute-start | bytes 1179656 | tf_op jit(solution)/shard_map/ppermute | solution.py:16
  102.9 16.9 %collective-permute-start.11 = (f32[4,192,128]{2,1,0:T(8,128)S(1)}, f32[4,192,128]{2,1,0:T(8,128)}, u32[]{:S(2)}, u32[]{:S(2)}) collective-permute-start(f32[4,192,128]{2,1,0:T(8,128)S(1)} %get-tuple-element.77), channel_id=1, source_target_pairs={{0,4},{4,8},{8,12},{12,16},{16,20},{20,24},{24,28},{28,32},{32,36}... | collective-permute-start | bytes 1179656 | tf_op jit(solution)/shard_map/ppermute | solution.py:15
  123.0 32.2 %collective-permute-start.12 = (f32[4,192,128]{2,1,0:T(8,128)}, f32[4,192,128]{2,1,0:T(8,128)}, u32[]{:S(2)}, u32[]{:S(2)}) collective-permute-start(f32[4,192,128]{2,1,0:T(8,128)} %get-tuple-element.76), channel_id=1, source_target_pairs={{4,0},{8,4},{12,8},{16,12},{20,16},{24,20},{28,24},{32,28},{36,32}... | collective-permute-start | bytes 1179656 | tf_op jit(solution)/shard_map/ppermute | solution.py:16
  130.0 25.2 %collective-permute-start.13 = (f32[4,192,128]{2,1,0:T(8,128)S(1)}, f32[4,192,128]{2,1,0:T(8,128)}, u32[]{:S(2)}, u32[]{:S(2)}) collective-permute-start(f32[4,192,128]{2,1,0:T(8,128)S(1)} %get-tuple-element.75), channel_id=1, source_target_pairs={{0,4},{4,8},{8,12},{12,16},{16,20},{20,24},{24,28},{28,32},{32,36}... | collective-permute-start | bytes 1179656 | tf_op jit(solution)/shard_map/ppermute | solution.py:15
  132.9 165.6 %collective-permute-start = (f32[4,192,128]{2,1,0:T(8,128)}, f32[4,192,128]{2,1,0:T(8,128)}, u32[]{:S(2)}, u32[]{:S(2)}) collective-permute-start(f32[4,192,128]{2,1,0:T(8,128)} %get-tuple-element.66), channel_id=1, source_target_pairs={{4,0},{8,4},{12,8},{16,12},{20,16},{24,20},{28,24},{32,28},{36,32}... | collective-permute-start | bytes 1179656 | tf_op jit(solution)/shard_map/ppermute | solution.py:16
  139.8 158.6 %collective-permute-start.1 = (f32[4,192,128]{2,1,0:T(8,128)}, f32[4,192,128]{2,1,0:T(8,128)}, u32[]{:S(2)}, u32[]{:S(2)}) collective-permute-start(f32[4,192,128]{2,1,0:T(8,128)} %get-tuple-element.65), channel_id=1, source_target_pairs={{0,4},{4,8},{8,12},{12,16},{16,20},{20,24},{24,28},{28,32},{32,36}... | collective-permute-start | bytes 1179656 | tf_op jit(solution)/shard_map/ppermute | solution.py:15
  158.5 25.7 %collective-permute-start.14 = (f32[4,192,128]{2,1,0:T(8,128)}, f32[4,192,128]{2,1,0:T(8,128)}, u32[]{:S(2)}, u32[]{:S(2)}) collective-permute-start(f32[4,192,128]{2,1,0:T(8,128)} %get-tuple-element.74), channel_id=1, source_target_pairs={{4,0},{8,4},{12,8},{16,12},{20,16},{24,20},{28,24},{32,28},{36,32}... | collective-permute-start | bytes 1179656 | tf_op jit(solution)/shard_map/ppermute | solution.py:16
  165.4 18.8 %collective-permute-start.15 = (f32[4,192,128]{2,1,0:T(8,128)S(1)}, f32[4,192,128]{2,1,0:T(8,128)}, u32[]{:S(2)}, u32[]{:S(2)}) collective-permute-start(f32[4,192,128]{2,1,0:T(8,128)S(1)} %get-tuple-element.73), channel_id=1, source_target_pairs={{0,4},{4,8},{8,12},{12,16},{16,20},{20,24},{24,28},{28,32},{32,36}... | collective-permute-start | bytes 1179656 | tf_op jit(solution)/shard_map/ppermute | solution.py:15
  187.6 23.1 %collective-permute-start.16 = (f32[4,192,128]{2,1,0:T(8,128)}, f32[4,192,128]{2,1,0:T(8,128)}, u32[]{:S(2)}, u32[]{:S(2)}) collective-permute-start(f32[4,192,128]{2,1,0:T(8,128)} %get-tuple-element.72), channel_id=1, source_target_pairs={{4,0},{8,4},{12,8},{16,12},{20,16},{24,20},{28,24},{32,28},{36,32}... | collective-permute-start | bytes 1179656 | tf_op jit(solution)/shard_map/ppermute | solution.py:16
  194.5 16.2 %collective-permute-start.17 = (f32[4,192,128]{2,1,0:T(8,128)S(1)}, f32[4,192,128]{2,1,0:T(8,128)}, u32[]{:S(2)}, u32[]{:S(2)}) collective-permute-start(f32[4,192,128]{2,1,0:T(8,128)S(1)} %get-tuple-element.71), channel_id=1, source_target_pairs={{0,4},{4,8},{8,12},{12,16},{16,20},{20,24},{24,28},{28,32},{32,36}... | collective-permute-start | bytes 1179656 | tf_op jit(solution)/shard_map/ppermute | solution.py:15
  214.1 22.5 %collective-permute-start.18 = (f32[4,192,128]{2,1,0:T(8,128)}, f32[4,192,128]{2,1,0:T(8,128)}, u32[]{:S(2)}, u32[]{:S(2)}) collective-permute-start(f32[4,192,128]{2,1,0:T(8,128)} %get-tuple-element.70), channel_id=1, source_target_pairs={{4,0},{8,4},{12,8},{16,12},{20,16},{24,20},{28,24},{32,28},{36,32}... | collective-permute-start | bytes 1179656 | tf_op jit(solution)/shard_map/ppermute | solution.py:16
  221.0 15.6 %collective-permute-start.19 = (f32[4,192,128]{2,1,0:T(8,128)S(1)}, f32[4,192,128]{2,1,0:T(8,128)}, u32[]{:S(2)}, u32[]{:S(2)}) collective-permute-start(f32[4,192,128]{2,1,0:T(8,128)S(1)} %get-tuple-element.69), channel_id=1, source_target_pairs={{0,4},{4,8},{8,12},{12,16},{16,20},{20,24},{24,28},{28,32},{32,36}... | collective-permute-start | bytes 1179656 | tf_op jit(solution)/shard_map/ppermute | solution.py:15
  240.1 45.3 %collective-permute-start.20 = (f32[4,192,128]{2,1,0:T(8,128)}, f32[4,192,128]{2,1,0:T(8,128)}, u32[]{:S(2)}, u32[]{:S(2)}) collective-permute-start(f32[4,192,128]{2,1,0:T(8,128)} %get-tuple-element.68), channel_id=1, source_target_pairs={{4,0},{8,4},{12,8},{16,12},{20,16},{24,20},{28,24},{32,28},{36,32}... | collective-permute-start | bytes 1179656 | tf_op jit(solution)/shard_map/ppermute | solution.py:16
  247.0 38.4 %collective-permute-start.21 = (f32[4,192,128]{2,1,0:T(8,128)}, f32[4,192,128]{2,1,0:T(8,128)}, u32[]{:S(2)}, u32[]{:S(2)}) collective-permute-start(f32[4,192,128]{2,1,0:T(8,128)} %get-tuple-element.67), channel_id=1, source_target_pairs={{0,4},{4,8},{8,12},{12,16},{16,20},{20,24},{24,28},{28,32},{32,36}... | collective-permute-start | bytes 1179656 | tf_op jit(solution)/shard_map/ppermute | solution.py:15
  298.4 13.2 %copy-start.16 = (f32[8,192,128]{2,1,0:T(8,128)S(1)}, f32[8,192,128]{2,1,0:T(8,128)}, u32[]{:S(2)}) copy-start(f32[8,192,128]{2,1,0:T(8,128)} %copy-done.13) | copy-start | bytes 2359300
  298.4 13.2 %copy-start.19 = (f32[8,192,128]{2,1,0:T(8,128)S(1)}, f32[8,192,128]{2,1,0:T(8,128)}, u32[]{:S(2)}) copy-start(f32[8,192,128]{2,1,0:T(8,128)} %copy-done.17) | copy-start | bytes 2359300
  298.5 13.2 %copy-start.21 = (f32[8,192,128]{2,1,0:T(8,128)S(1)}, f32[8,192,128]{2,1,0:T(8,128)}, u32[]{:S(2)}) copy-start(f32[8,192,128]{2,1,0:T(8,128)} %copy-done.20) | copy-start | bytes 2359300
  301.5 14.0 %copy-start.24 = (f32[8,192,128]{2,1,0:T(8,128)}, f32[8,192,128]{2,1,0:T(8,128)S(1)}, u32[]{:S(2)}) copy-start(f32[8,192,128]{2,1,0:T(8,128)S(1)} %fusion.8) | copy-start | bytes 2359300
  302.5 19.7 %collective-permute-start.22 = (f32[4,192,128]{2,1,0:T(8,128)}, f32[4,192,128]{2,1,0:T(8,128)S(1)}, u32[]{:S(2)}, u32[]{:S(2)}) collective-permute-start(f32[4,192,128]{2,1,0:T(8,128)} %get-tuple-element.64), channel_id=1, source_target_pairs={{4,0},{8,4},{12,8},{16,12},{20,16},{24,20},{28,24},{32,28},{36,32}... | collective-permute-start | bytes 1179656 | tf_op jit(solution)/shard_map/ppermute | solution.py:16
  309.6 13.1 %collective-permute-start.23 = (f32[4,192,128]{2,1,0:T(8,128)}, f32[4,192,128]{2,1,0:T(8,128)}, u32[]{:S(2)}, u32[]{:S(2)}) collective-permute-start(f32[4,192,128]{2,1,0:T(8,128)} %get-tuple-element.63), channel_id=1, source_target_pairs={{0,4},{4,8},{8,12},{12,16},{16,20},{20,24},{24,28},{28,32},{32,36}... | collective-permute-start | bytes 1179656 | tf_op jit(solution)/shard_map/ppermute | solution.py:15
  326.0 14.4 %collective-permute-start.24 = (f32[4,192,128]{2,1,0:T(8,128)S(1)}, f32[4,192,128]{2,1,0:T(8,128)S(1)}, u32[]{:S(2)}, u32[]{:S(2)}) collective-permute-start(f32[4,192,128]{2,1,0:T(8,128)S(1)} %get-tuple-element.60), channel_id=1, source_target_pairs={{4,0},{8,4},{12,8},{16,12},{20,16},{24,20},{28,24},{32,28},{36,32}... | collective-permute-start | bytes 1179656 | tf_op jit(solution)/shard_map/ppermute | solution.py:16
  332.6 12.9 %collective-permute-start.25 = (f32[4,192,128]{2,1,0:T(8,128)S(1)}, f32[4,192,128]{2,1,0:T(8,128)}, u32[]{:S(2)}, u32[]{:S(2)}) collective-permute-start(f32[4,192,128]{2,1,0:T(8,128)S(1)} %get-tuple-element.59), channel_id=1, source_target_pairs={{0,4},{4,8},{8,12},{12,16},{16,20},{20,24},{24,28},{28,32},{32,36}... | collective-permute-start | bytes 1179656 | tf_op jit(solution)/shard_map/ppermute | solution.py:15
  348.5 12.3 %collective-permute-start.26 = (f32[4,192,128]{2,1,0:T(8,128)S(1)}, f32[4,192,128]{2,1,0:T(8,128)S(1)}, u32[]{:S(2)}, u32[]{:S(2)}) collective-permute-start(f32[4,192,128]{2,1,0:T(8,128)S(1)} %get-tuple-element.56), channel_id=1, source_target_pairs={{4,0},{8,4},{12,8},{16,12},{20,16},{24,20},{28,24},{32,28},{36,32}... | collective-permute-start | bytes 1179656 | tf_op jit(solution)/shard_map/ppermute | solution.py:16
  350.5 12.9 %collective-permute-start.27 = (f32[4,192,128]{2,1,0:T(8,128)S(1)}, f32[4,192,128]{2,1,0:T(8,128)}, u32[]{:S(2)}, u32[]{:S(2)}) collective-permute-start(f32[4,192,128]{2,1,0:T(8,128)S(1)} %get-tuple-element.55), channel_id=1, source_target_pairs={{0,4},{4,8},{8,12},{12,16},{16,20},{20,24},{24,28},{28,32},{32,36}... | collective-permute-start | bytes 1179656 | tf_op jit(solution)/shard_map/ppermute | solution.py:15
  366.5 13.0 %collective-permute-start.28 = (f32[4,192,128]{2,1,0:T(8,128)S(1)}, f32[4,192,128]{2,1,0:T(8,128)S(1)}, u32[]{:S(2)}, u32[]{:S(2)}) collective-permute-start(f32[4,192,128]{2,1,0:T(8,128)S(1)} %get-tuple-element.52), channel_id=1, source_target_pairs={{4,0},{8,4},{12,8},{16,12},{20,16},{24,20},{28,24},{32,28},{36,32}... | collective-permute-start | bytes 1179656 | tf_op jit(solution)/shard_map/ppermute | solution.py:16
  368.7 13.3 %collective-permute-start.29 = (f32[4,192,128]{2,1,0:T(8,128)S(1)}, f32[4,192,128]{2,1,0:T(8,128)}, u32[]{:S(2)}, u32[]{:S(2)}) collective-permute-start(f32[4,192,128]{2,1,0:T(8,128)S(1)} %get-tuple-element.51), channel_id=1, source_target_pairs={{0,4},{4,8},{8,12},{12,16},{16,20},{20,24},{24,28},{28,32},{32,36}... | collective-permute-start | bytes 1179656 | tf_op jit(solution)/shard_map/ppermute | solution.py:15
  385.1 22.7 %copy-start.26 = (f32[8,192,128]{2,1,0:T(8,128)}, f32[8,192,128]{2,1,0:T(8,128)S(1)}, u32[]{:S(2)}) copy-start(f32[8,192,128]{2,1,0:T(8,128)S(1)} %get-tuple-element.49) | copy-start | bytes 2359300
  385.1 17.5 %collective-permute-start.30 = (f32[4,192,128]{2,1,0:T(8,128)S(1)}, f32[4,192,128]{2,1,0:T(8,128)S(1)}, u32[]{:S(2)}, u32[]{:S(2)}) collective-permute-start(f32[4,192,128]{2,1,0:T(8,128)S(1)} %get-tuple-element.48), channel_id=1, source_target_pairs={{4,0},{8,4},{12,8},{16,12},{20,16},{24,20},{28,24},{32,28},{36,32}... | collective-permute-start | bytes 1179656 | tf_op jit(solution)/shard_map/ppermute | solution.py:16
  394.8 12.9 %collective-permute-start.31 = (f32[4,192,128]{2,1,0:T(8,128)S(1)}, f32[4,192,128]{2,1,0:T(8,128)}, u32[]{:S(2)}, u32[]{:S(2)}) collective-permute-start(f32[4,192,128]{2,1,0:T(8,128)S(1)} %get-tuple-element.47), channel_id=1, source_target_pairs={{0,4},{4,8},{8,12},{12,16},{16,20},{20,24},{24,28},{28,32},{32,36}... | collective-permute-start | bytes 1179656 | tf_op jit(solution)/shard_map/ppermute | solution.py:15
  411.0 13.6 %collective-permute-start.32 = (f32[4,192,128]{2,1,0:T(8,128)S(1)}, f32[4,192,128]{2,1,0:T(8,128)S(1)}, u32[]{:S(2)}, u32[]{:S(2)}) collective-permute-start(f32[4,192,128]{2,1,0:T(8,128)S(1)} %get-tuple-element.44), channel_id=1, source_target_pairs={{4,0},{8,4},{12,8},{16,12},{20,16},{24,20},{28,24},{32,28},{36,32}... | collective-permute-start | bytes 1179656 | tf_op jit(solution)/shard_map/ppermute | solution.py:16
  416.9 12.9 %collective-permute-start.33 = (f32[4,192,128]{2,1,0:T(8,128)S(1)}, f32[4,192,128]{2,1,0:T(8,128)}, u32[]{:S(2)}, u32[]{:S(2)}) collective-permute-start(f32[4,192,128]{2,1,0:T(8,128)S(1)} %get-tuple-element.43), channel_id=1, source_target_pairs={{0,4},{4,8},{8,12},{12,16},{16,20},{20,24},{24,28},{28,32},{32,36}... | collective-permute-start | bytes 1179656 | tf_op jit(solution)/shard_map/ppermute | solution.py:15
  433.0 38.3 %collective-permute-start.34 = (f32[4,192,128]{2,1,0:T(8,128)S(1)}, f32[4,192,128]{2,1,0:T(8,128)S(1)}, u32[]{:S(2)}, u32[]{:S(2)}) collective-permute-start(f32[4,192,128]{2,1,0:T(8,128)S(1)} %get-tuple-element.40), channel_id=1, source_target_pairs={{4,0},{8,4},{12,8},{16,12},{20,16},{24,20},{28,24},{32,28},{36,32}... | collective-permute-start | bytes 1179656 | tf_op jit(solution)/shard_map/ppermute | solution.py:16
  463.4 15.0 %collective-permute-start.35 = (f32[4,192,128]{2,1,0:T(8,128)S(1)}, f32[4,192,128]{2,1,0:T(8,128)}, u32[]{:S(2)}, u32[]{:S(2)}) collective-permute-start(f32[4,192,128]{2,1,0:T(8,128)S(1)} %get-tuple-element.39), channel_id=1, source_target_pairs={{0,4},{4,8},{8,12},{12,16},{16,20},{20,24},{24,28},{28,32},{32,36}... | collective-permute-start | bytes 1179656 | tf_op jit(solution)/shard_map/ppermute | solution.py:15
  481.6 13.9 %collective-permute-start.36 = (f32[4,192,128]{2,1,0:T(8,128)S(1)}, f32[4,192,128]{2,1,0:T(8,128)S(1)}, u32[]{:S(2)}, u32[]{:S(2)}) collective-permute-start(f32[4,192,128]{2,1,0:T(8,128)S(1)} %get-tuple-element.36), channel_id=1, source_target_pairs={{4,0},{8,4},{12,8},{16,12},{20,16},{24,20},{28,24},{32,28},{36,32}... | collective-permute-start | bytes 1179656 | tf_op jit(solution)/shard_map/ppermute | solution.py:16
  486.6 13.2 %collective-permute-start.37 = (f32[4,192,128]{2,1,0:T(8,128)S(1)}, f32[4,192,128]{2,1,0:T(8,128)}, u32[]{:S(2)}, u32[]{:S(2)}) collective-permute-start(f32[4,192,128]{2,1,0:T(8,128)S(1)} %get-tuple-element.35), channel_id=1, source_target_pairs={{0,4},{4,8},{8,12},{12,16},{16,20},{20,24},{24,28},{28,32},{32,36}... | collective-permute-start | bytes 1179656 | tf_op jit(solution)/shard_map/ppermute | solution.py:15
  502.9 15.5 %collective-permute-start.38 = (f32[4,192,128]{2,1,0:T(8,128)S(1)}, f32[4,192,128]{2,1,0:T(8,128)S(1)}, u32[]{:S(2)}, u32[]{:S(2)}) collective-permute-start(f32[4,192,128]{2,1,0:T(8,128)S(1)} %get-tuple-element.32), channel_id=1, source_target_pairs={{4,0},{8,4},{12,8},{16,12},{20,16},{24,20},{28,24},{32,28},{36,32}... | collective-permute-start | bytes 1179656 | tf_op jit(solution)/shard_map/ppermute | solution.py:16
  510.5 12.8 %collective-permute-start.39 = (f32[4,192,128]{2,1,0:T(8,128)S(1)}, f32[4,192,128]{2,1,0:T(8,128)}, u32[]{:S(2)}, u32[]{:S(2)}) collective-permute-start(f32[4,192,128]{2,1,0:T(8,128)S(1)} %get-tuple-element.31), channel_id=1, source_target_pairs={{0,4},{4,8},{8,12},{12,16},{16,20},{20,24},{24,28},{28,32},{32,36}... | collective-permute-start | bytes 1179656 | tf_op jit(solution)/shard_map/ppermute | solution.py:15
  525.8 3.6 collective-permute-start.40
  529.5 10.3 %collective-permute-start.41 = (f32[8,48,128]{2,1,0:T(8,128)S(1)}, f32[8,48,128]{2,1,0:T(8,128)S(1)}, u32[]{:S(2)}, u32[]{:S(2)}) collective-permute-start(f32[8,48,128]{2,1,0:T(8,128)S(1)} %dynamic-slice_bitcast_fusion), channel_id=1, source_target_pairs={{0,2},{1,3},{2,0},{3,1},{4,6},{5,7},{6,4},{7,5},{8,10},{9,11},{10,... | collective-permute-start | bytes 589832 | tf_op jit(solution)/shard_map/ppermute | solution.py:138
  (78 other events, 628.2 us)
where the time goes:
time: 551 us; the launch traced here: 541 us
  other arithmetic  228 us (41%)
  starting transfers between devices  191 us (35%)
  waiting for transfers between devices  83.7 us (15%)
  local copies, waits for them, and re-layouts  35.4 us (6%)
    ppermute x20, starting transfers between devices, exchange_edges(): high = lax.ppermute(block[:RADIUS], 'space', backward)  137 us
    add x20, other arithmetic, inner_laplace(): result = result + TAPS[distance] * beside_all  106 us
    ppermute x20, waiting for transfers between devices, exchange_edges(): low = lax.ppermute(block[block.shape[0] - RADIUS:], 'space', forward)  65.2 us
    scatter-add x20, other arithmetic, place_cells(): jnp.zeros((size // lanes, lanes), jnp.float32).at[cells // lanes].add(rows)  59.7 us
    add x20, other arithmetic, step(): 2.0 * current - former + courant_sq * lap + injected  52.9 us
    ppermute x20, starting transfers between devices, exchange_edges(): low = lax.ppermute(block[block.shape[0] - RADIUS:], 'space', forward)  47.9 us
    gather x10, local copies, waits for them, and re-layouts, sample_cells(): rows = field.reshape(-1, lanes)[cells // lanes]  23.7 us
    ppermute x20, waiting for transfers between devices, exchange_edges(): high = lax.ppermute(block[:RADIUS], 'space', backward)  11.1 us
  transfers between devices with their start and end apart: 42, of which 21 were waited for; matrix products, arithmetic and copies ran while one was open for 40% of the time, Pallas kernels for 0%

commit v1 on v0

--- a/solution.py
+++ b/solution.py
@@ -74,9 +74,10 @@
 
 def step(current, former, courant_sq, injected):
     low, high = exchange_edges(current)
-    interior = lax.optimization_barrier(inner_laplace(current))
-    lap = interior + edge_terms(low, high, current.shape[0])
-    return lax.optimization_barrier(2.0 * current - former + courant_sq * lap + injected)
+    base = lax.optimization_barrier(
+        2.0 * current - former + courant_sq * inner_laplace(current) + injected
+    )
+    return lax.optimization_barrier(base + courant_sq * edge_terms(low, high, current.shape[0]))
 
 
 def per_device(

time: 551 us -> 529 us (0.960)
  the two profiles are of different devices: /device:TPU:160 before, /device:TPU:454 now
where the time goes in v1:
time: 529 us; the launch traced here: 519 us
  waiting for transfers between devices  188 us (36%)
  other arithmetic  151 us (29%)
  starting transfers between devices  147 us (28%)
  local copies, waits for them, and re-layouts  30.7 us (6%)
    ppermute x20, waiting for transfers between devices, exchange_edges(): low = lax.ppermute(block[block.shape[0] - RADIUS:], 'space', forward)  110 us
    ppermute x20, starting transfers between devices, exchange_edges(): low = lax.ppermute(block[block.shape[0] - RADIUS:], 'space', forward)  95.6 us
    ppermute x20, waiting for transfers between devices, exchange_edges(): high = lax.ppermute(block[:RADIUS], 'space', backward)  69 us
    scatter-add x20, other arithmetic, place_cells(): jnp.zeros((size // lanes, lanes), jnp.float32).at[cells // lanes].add(rows)  54.9 us
    ppermute x20, starting transfers between devices, exchange_edges(): high = lax.ppermute(block[:RADIUS], 'space', backward)  46.4 us
    add x10, other arithmetic, per_device(): latest - 2.0 * current + former  34 us
    add x11, other arithmetic, step(): 2.0 * current - former + courant_sq * inner_laplace(current) + injected  32.8 us
    add x20, other arithmetic, step(): base + courant_sq * edge_terms(low, high, current.shape[0])  25 us
  transfers between devices with their start and end apart: 42, of which 36 were waited for; matrix products, arithmetic and copies ran while one was open for 33% of the time, Pallas kernels for 0%

profile of v1, /device:TPU:454, one launch (start us, length us, event | category | flops | bytes accessed | tf_op | source)
XLA Modules:
  0.0 519.2 jit_solution(6583075528150588036)
XLA Ops:
  5.0 4.0 collective-permute-start.1
  9.9 4.0 collective-permute-start.20
  49.3 6.0 %collective-permute-start.2 = (f32[4,192,128]{2,1,0:T(8,128)}, f32[4,192,128]{2,1,0:T(8,128)}, u32[]{:S(2)}, u32[]{:S(2)}) collective-permute-start(f32[4,192,128]{2,1,0:T(8,128)} %get-tuple-element.90), channel_id=1, source_target_pairs={{4,0},{8,4},{12,8},{16,12},{20,16},{24,20},{28,24},{32,28},{36,32}... | collective-permute-start | bytes 1179656 | tf_op jit(solution)/shard_map/ppermute | solution.py:16
  57.3 3.7 bitcast_add_fusion
  65.2 12.0 %collective-permute-done.3 = f32[4,192,128]{2,1,0:T(8,128)} collective-permute-done((f32[4,192,128]{2,1,0:T(8,128)}, f32[4,192,128]{2,1,0:T(8,128)}, u32[]{:S(2)}, u32[]{:S(2)}) %collective-permute-start.3) | collective-permute-done | bytes 393248 | tf_op jit(solution)/shard_map/ppermute | solution.py:15
  82.1 5.0 collective-permute-start.5
  87.1 3.7 subtract_add_fusion
  95.3 4.4 collective-permute-done.5
  104.6 5.3 %collective-permute-start.7 = (f32[4,192,128]{2,1,0:T(8,128)}, f32[4,192,128]{2,1,0:T(8,128)}, u32[]{:S(2)}, u32[]{:S(2)}) collective-permute-start(f32[4,192,128]{2,1,0:T(8,128)} %get-tuple-element.85), channel_id=1, source_target_pairs={{0,4},{4,8},{8,12},{12,16},{16,20},{20,24},{24,28},{28,32},{32,36}... | collective-permute-start | bytes 1179656 | tf_op jit(solution)/shard_map/ppermute | solution.py:15
  109.9 3.7 subtract_add_fusion.1
  126.5 5.3 %collective-permute-start.9 = (f32[4,192,128]{2,1,0:T(8,128)}, f32[4,192,128]{2,1,0:T(8,128)}, u32[]{:S(2)}, u32[]{:S(2)}) collective-permute-start(f32[4,192,128]{2,1,0:T(8,128)} %get-tuple-element.83), channel_id=1, source_target_pairs={{0,4},{4,8},{8,12},{12,16},{16,20},{20,24},{24,28},{28,32},{32,36}... | collective-permute-start | bytes 1179656 | tf_op jit(solution)/shard_map/ppermute | solution.py:15
  147.8 5.3 %collective-permute-start.11 = (f32[4,192,128]{2,1,0:T(8,128)}, f32[4,192,128]{2,1,0:T(8,128)}, u32[]{:S(2)}, u32[]{:S(2)}) collective-permute-start(f32[4,192,128]{2,1,0:T(8,128)} %get-tuple-element.81), channel_id=1, source_target_pairs={{0,4},{4,8},{8,12},{12,16},{16,20},{20,24},{24,28},{28,32},{32,36}... | collective-permute-start | bytes 1179656 | tf_op jit(solution)/shard_map/ppermute | solution.py:15
  161.5 12.3 %collective-permute-done.11 = f32[4,192,128]{2,1,0:T(8,128)} collective-permute-done((f32[4,192,128]{2,1,0:T(8,128)}, f32[4,192,128]{2,1,0:T(8,128)}, u32[]{:S(2)}, u32[]{:S(2)}) %collective-permute-start.11) | collective-permute-done | bytes 393248 | tf_op jit(solution)/shard_map/ppermute | solution.py:15
  178.5 4.8 collective-permute-start.13
  191.7 4.4 collective-permute-done.13
  201.0 5.5 %collective-permute-start.15 = (f32[4,192,128]{2,1,0:T(8,128)}, f32[4,192,128]{2,1,0:T(8,128)}, u32[]{:S(2)}, u32[]{:S(2)}) collective-permute-start(f32[4,192,128]{2,1,0:T(8,128)} %get-tuple-element.77), channel_id=1, source_target_pairs={{0,4},{4,8},{8,12},{12,16},{16,20},{20,24},{24,28},{28,32},{32,36}... | collective-permute-start | bytes 1179656 | tf_op jit(solution)/shard_map/ppermute | solution.py:15
  206.5 3.7 subtract_add_fusion.5
  222.5 5.3 %collective-permute-start.17 = (f32[4,192,128]{2,1,0:T(8,128)S(1)}, f32[4,192,128]{2,1,0:T(8,128)}, u32[]{:S(2)}, u32[]{:S(2)}) collective-permute-start(f32[4,192,128]{2,1,0:T(8,128)S(1)} %get-tuple-element.75), channel_id=1, source_target_pairs={{0,4},{4,8},{8,12},{12,16},{16,20},{20,24},{24,28},{28,32},{32,36}... | collective-permute-start | bytes 1179656 | tf_op jit(solution)/shard_map/ppermute | solution.py:15
  227.9 3.7 subtract_add_fusion.6
  243.9 5.4 %collective-permute-start.19 = (f32[4,192,128]{2,1,0:T(8,128)}, f32[4,192,128]{2,1,0:T(8,128)}, u32[]{:S(2)}, u32[]{:S(2)}) collective-permute-start(f32[4,192,128]{2,1,0:T(8,128)} %get-tuple-element.73), channel_id=1, source_target_pairs={{0,4},{4,8},{8,12},{12,16},{16,20},{20,24},{24,28},{28,32},{32,36}... | collective-permute-start | bytes 1179656 | tf_op jit(solution)/shard_map/ppermute | solution.py:15
  249.3 3.6 subtract_add_fusion.7
  257.7 12.3 %collective-permute-done.19 = f32[4,192,128]{2,1,0:T(8,128)} collective-permute-done((f32[4,192,128]{2,1,0:T(8,128)}, f32[4,192,128]{2,1,0:T(8,128)}, u32[]{:S(2)}, u32[]{:S(2)}) %collective-permute-start.19) | collective-permute-done | bytes 393248 | tf_op jit(solution)/shard_map/ppermute | solution.py:15
  280.0 3.7 fusion.272
  288.4 5.2 %collective-permute-start.23 = (f32[4,192,128]{2,1,0:T(8,128)}, f32[4,192,128]{2,1,0:T(8,128)}, u32[]{:S(2)}, u32[]{:S(2)}) collective-permute-start(f32[4,192,128]{2,1,0:T(8,128)} %get-tuple-element.69), channel_id=1, source_target_pairs={{0,4},{4,8},{8,12},{12,16},{16,20},{20,24},{24,28},{28,32},{32,36}... | collective-permute-start | bytes 1179656 | tf_op jit(solution)/shard_map/ppermute | solution.py:15
  329.4 4.8 collective-permute-start.25
  337.0 5.3 %collective-permute-done.24 = f32[4,192,128]{2,1,0:T(8,128)S(1)} collective-permute-done((f32[4,192,128]{2,1,0:T(8,128)S(1)}, f32[4,192,128]{2,1,0:T(8,128)S(1)}, u32[]{:S(2)}, u32[]{:S(2)}) %collective-permute-start.24) | collective-permute-done | bytes 393248 | tf_op jit(solution)/shard_map/ppermute | solution.py:16
  342.3 13.7 %collective-permute-done.25 = f32[4,192,128]{2,1,0:T(8,128)S(1)} collective-permute-done((f32[4,192,128]{2,1,0:T(8,128)S(1)}, f32[4,192,128]{2,1,0:T(8,128)S(1)}, u32[]{:S(2)}, u32[]{:S(2)}) %collective-permute-start.25) | collective-permute-done | bytes 393248 | tf_op jit(solution)/shard_map/ppermute | solution.py:15
  358.3 5.0 collective-permute-start.27
  366.2 5.0 collective-permute-done.26
  371.2 5.7 %collective-permute-done.27 = f32[4,192,128]{2,1,0:T(8,128)S(1)} collective-permute-done((f32[4,192,128]{2,1,0:T(8,128)S(1)}, f32[4,192,128]{2,1,0:T(8,128)S(1)}, u32[]{:S(2)}, u32[]{:S(2)}) %collective-permute-start.27) | collective-permute-done | bytes 393248 | tf_op jit(solution)/shard_map/ppermute | solution.py:15
  379.3 4.8 collective-permute-start.29
  387.0 5.2 %collective-permute-done.28 = f32[4,192,128]{2,1,0:T(8,128)S(1)} collective-permute-done((f32[4,192,128]{2,1,0:T(8,128)S(1)}, f32[4,192,128]{2,1,0:T(8,128)S(1)}, u32[]{:S(2)}, u32[]{:S(2)}) %collective-permute-start.28) | collective-permute-done | bytes 393248 | tf_op jit(solution)/shard_map/ppermute | solution.py:16
  392.2 4.4 collective-permute-done.29
  399.0 5.3 %collective-permute-start.31 = (f32[4,192,128]{2,1,0:T(8,128)S(1)}, f32[4,192,128]{2,1,0:T(8,128)S(1)}, u32[]{:S(2)}, u32[]{:S(2)}) collective-permute-start(f32[4,192,128]{2,1,0:T(8,128)S(1)} %get-tuple-element.53), channel_id=1, source_target_pairs={{0,4},{4,8},{8,12},{12,16},{16,20},{20,24},{24,28},{28,32},{32,36}... | collective-permute-start | bytes 1179656 | tf_op jit(solution)/shard_map/ppermute | solution.py:15
  407.1 5.2 %collective-permute-done.30 = f32[4,192,128]{2,1,0:T(8,128)S(1)} collective-permute-done((f32[4,192,128]{2,1,0:T(8,128)S(1)}, f32[4,192,128]{2,1,0:T(8,128)S(1)}, u32[]{:S(2)}, u32[]{:S(2)}) %collective-permute-start.30) | collective-permute-done | bytes 393248 | tf_op jit(solution)/shard_map/ppermute | solution.py:16
  418.1 5.3 %collective-permute-start.33 = (f32[4,192,128]{2,1,0:T(8,128)S(1)}, f32[4,192,128]{2,1,0:T(8,128)S(1)}, u32[]{:S(2)}, u32[]{:S(2)}) collective-permute-start(f32[4,192,128]{2,1,0:T(8,128)S(1)} %get-tuple-element.49), channel_id=1, source_target_pairs={{0,4},{4,8},{8,12},{12,16},{16,20},{20,24},{24,28},{28,32},{32,36}... | collective-permute-start | bytes 1179656 | tf_op jit(solution)/shard_map/ppermute | solution.py:15
  426.2 5.3 %collective-permute-done.32 = f32[4,192,128]{2,1,0:T(8,128)S(1)} collective-permute-done((f32[4,192,128]{2,1,0:T(8,128)S(1)}, f32[4,192,128]{2,1,0:T(8,128)S(1)}, u32[]{:S(2)}, u32[]{:S(2)}) %collective-permute-start.32) | collective-permute-done | bytes 393248 | tf_op jit(solution)/shard_map/ppermute | solution.py:16
  431.5 6.8 %collective-permute-done.33 = f32[4,192,128]{2,1,0:T(8,128)S(1)} collective-permute-done((f32[4,192,128]{2,1,0:T(8,128)S(1)}, f32[4,192,128]{2,1,0:T(8,128)S(1)}, u32[]{:S(2)}, u32[]{:S(2)}) %collective-permute-start.33) | collective-permute-done | bytes 393248 | tf_op jit(solution)/shard_map/ppermute | solution.py:15
  440.8 4.8 collective-permute-start.35
  448.4 5.3 %collective-permute-done.34 = f32[4,192,128]{2,1,0:T(8,128)S(1)} collective-permute-done((f32[4,192,128]{2,1,0:T(8,128)S(1)}, f32[4,192,128]{2,1,0:T(8,128)S(1)}, u32[]{:S(2)}, u32[]{:S(2)}) %collective-permute-start.34) | collective-permute-done | bytes 393248 | tf_op jit(solution)/shard_map/ppermute | solution.py:16
  453.7 6.4 %collective-permute-done.35 = f32[4,192,128]{2,1,0:T(8,128)S(1)} collective-permute-done((f32[4,192,128]{2,1,0:T(8,128)S(1)}, f32[4,192,128]{2,1,0:T(8,128)S(1)}, u32[]{:S(2)}, u32[]{:S(2)}) %collective-permute-start.35) | collective-permute-done | bytes 393248 | tf_op jit(solution)/shard_map/ppermute | solution.py:15
  462.5 4.8 collective-permute-start.37
  470.1 5.3 %collective-permute-done.36 = f32[4,192,128]{2,1,0:T(8,128)S(1)} collective-permute-done((f32[4,192,128]{2,1,0:T(8,128)S(1)}, f32[4,192,128]{2,1,0:T(8,128)S(1)}, u32[]{:S(2)}, u32[]{:S(2)}) %collective-permute-start.36) | collective-permute-done | bytes 393248 | tf_op jit(solution)/shard_map/ppermute | solution.py:16
  475.4 6.2 %collective-permute-done.37 = f32[4,192,128]{2,1,0:T(8,128)S(1)} collective-permute-done((f32[4,192,128]{2,1,0:T(8,128)S(1)}, f32[4,192,128]{2,1,0:T(8,128)S(1)}, u32[]{:S(2)}, u32[]{:S(2)}) %collective-permute-start.37) | collective-permute-done | bytes 393248 | tf_op jit(solution)/shard_map/ppermute | solution.py:15
  483.9 4.8 collective-permute-start.39
  491.8 5.1 collective-permute-done.38
  496.9 6.9 %collective-permute-done.39 = f32[4,192,128]{2,1,0:T(8,128)S(1)} collective-permute-done((f32[4,192,128]{2,1,0:T(8,128)S(1)}, f32[4,192,128]{2,1,0:T(8,128)S(1)}, u32[]{:S(2)}, u32[]{:S(2)}) %collective-permute-start.39) | collective-permute-done | bytes 393248 | tf_op jit(solution)/shard_map/ppermute | solution.py:15
  511.3 7.0 %collective-permute-done.41 = f32[8,48,128]{2,1,0:T(8,128)S(1)} collective-permute-done((f32[8,48,128]{2,1,0:T(8,128)S(1)}, f32[8,48,128]{2,1,0:T(8,128)S(1)}, u32[]{:S(2)}, u32[]{:S(2)}) %collective-permute-start.41) | collective-permute-done | bytes 196640 | tf_op jit(solution)/shard_map/ppermute | solution.py:139
  (285 shorter events, 246.1 us)
Async XLA Ops:
  2.2 44.4 %collective-permute-start = (f32[4,192,128]{2,1,0:T(8,128)}, f32[4,192,128]{2,1,0:T(8,128)S(1)}, u32[]{:S(2)}, u32[]{:S(2)}) collective-permute-start(f32[4,192,128]{2,1,0:T(8,128)} %get-tuple-element.92), channel_id=1, source_target_pairs={{4,0},{8,4},{12,8},{16,12},{20,16},{24,20},{28,24},{32,28},{36,32}... | collective-permute-start | bytes 1179656 | tf_op jit(solution)/shard_map/ppermute | solution.py:16
  4.9 11.9 %copy-start.58 = (f32[1,10,128]{2,0,1:T(1,128)S(1)}, f32[1,10,128]{2,0,1:T(1,128)}, u32[]{:S(2)}) copy-start(f32[1,10,128]{2,0,1:T(1,128)} %param.16) | copy-start | bytes 15364
  4.9 11.9 %copy-start.67 = (s32[1,128]{1,0:T(1,128)S(1)}, s32[1,128]{1,0:T(1,128)}, u32[]{:S(2)}) copy-start(s32[1,128]{1,0:T(1,128)} %param.15) | copy-start | bytes 1540
  5.0 41.6 %collective-permute-start.1 = (f32[4,192,128]{2,1,0:T(8,128)}, f32[4,192,128]{2,1,0:T(8,128)}, u32[]{:S(2)}, u32[]{:S(2)}) collective-permute-start(f32[4,192,128]{2,1,0:T(8,128)} %get-tuple-element.91), channel_id=1, source_target_pairs={{0,4},{4,8},{8,12},{12,16},{16,20},{20,24},{24,28},{28,32},{32,36}... | collective-permute-start | bytes 1179656 | tf_op jit(solution)/shard_map/ppermute | solution.py:15
  9.0 10.3 %copy-start.3 = (f32[1,8,192,128]{3,2,1,0:T(8,128)S(1)}, f32[1,8,192,128]{3,2,1,0:T(8,128)}, u32[]{:S(2)}) copy-start(f32[1,8,192,128]{3,2,1,0:T(8,128)} %param.11) | copy-start | bytes 2359300
  9.0 10.3 %copy-start.31 = (f32[1,8,192,128]{3,2,1,0:T(8,128)S(1)}, f32[1,8,192,128]{3,2,1,0:T(8,128)}, u32[]{:S(2)}) copy-start(f32[1,8,192,128]{3,2,1,0:T(8,128)} %param.12) | copy-start | bytes 2359300
  9.9 273.8 %collective-permute-start.20 = (f32[4,192,128]{2,1,0:T(8,128)}, f32[4,192,128]{2,1,0:T(8,128)}, u32[]{:S(2)}, u32[]{:S(2)}) collective-permute-start(f32[4,192,128]{2,1,0:T(8,128)} %get-tuple-element.72), channel_id=1, source_target_pairs={{4,0},{8,4},{12,8},{16,12},{20,16},{24,20},{28,24},{32,28},{36,32}... | collective-permute-start | bytes 1179656 | tf_op jit(solution)/shard_map/ppermute | solution.py:16
  14.0 269.7 %collective-permute-start.21 = (f32[4,192,128]{2,1,0:T(8,128)}, f32[4,192,128]{2,1,0:T(8,128)}, u32[]{:S(2)}, u32[]{:S(2)}) collective-permute-start(f32[4,192,128]{2,1,0:T(8,128)} %get-tuple-element.71), channel_id=1, source_target_pairs={{0,4},{4,8},{8,12},{12,16},{16,20},{20,24},{24,28},{28,32},{32,36}... | collective-permute-start | bytes 1179656 | tf_op jit(solution)/shard_map/ppermute | solution.py:15
  49.3 15.9 %collective-permute-start.2 = (f32[4,192,128]{2,1,0:T(8,128)}, f32[4,192,128]{2,1,0:T(8,128)}, u32[]{:S(2)}, u32[]{:S(2)}) collective-permute-start(f32[4,192,128]{2,1,0:T(8,128)} %get-tuple-element.90), channel_id=1, source_target_pairs={{4,0},{8,4},{12,8},{16,12},{20,16},{24,20},{28,24},{32,28},{36,32}... | collective-permute-start | bytes 1179656 | tf_op jit(solution)/shard_map/ppermute | solution.py:16
  55.3 21.9 %collective-permute-start.3 = (f32[4,192,128]{2,1,0:T(8,128)}, f32[4,192,128]{2,1,0:T(8,128)}, u32[]{:S(2)}, u32[]{:S(2)}) collective-permute-start(f32[4,192,128]{2,1,0:T(8,128)} %get-tuple-element.89), channel_id=1, source_target_pairs={{0,4},{4,8},{8,12},{12,16},{16,20},{20,24},{24,28},{28,32},{32,36}... | collective-permute-start | bytes 1179656 | tf_op jit(solution)/shard_map/ppermute | solution.py:15
  80.2 15.1 %collective-permute-start.4 = (f32[4,192,128]{2,1,0:T(8,128)}, f32[4,192,128]{2,1,0:T(8,128)}, u32[]{:S(2)}, u32[]{:S(2)}) collective-permute-start(f32[4,192,128]{2,1,0:T(8,128)} %get-tuple-element.88), channel_id=1, source_target_pairs={{4,0},{8,4},{12,8},{16,12},{20,16},{24,20},{28,24},{32,28},{36,32}... | collective-permute-start | bytes 1179656 | tf_op jit(solution)/shard_map/ppermute | solution.py:16
  82.1 17.6 %collective-permute-start.5 = (f32[4,192,128]{2,1,0:T(8,128)}, f32[4,192,128]{2,1,0:T(8,128)}, u32[]{:S(2)}, u32[]{:S(2)}) collective-permute-start(f32[4,192,128]{2,1,0:T(8,128)} %get-tuple-element.87), channel_id=1, source_target_pairs={{0,4},{4,8},{8,12},{12,16},{16,20},{20,24},{24,28},{28,32},{32,36}... | collective-permute-start | bytes 1179656 | tf_op jit(solution)/shard_map/ppermute | solution.py:15
  102.6 15.6 %collective-permute-start.6 = (f32[4,192,128]{2,1,0:T(8,128)}, f32[4,192,128]{2,1,0:T(8,128)}, u32[]{:S(2)}, u32[]{:S(2)}) collective-permute-start(f32[4,192,128]{2,1,0:T(8,128)} %get-tuple-element.86), channel_id=1, source_target_pairs={{4,0},{8,4},{12,8},{16,12},{20,16},{24,20},{28,24},{32,28},{36,32}... | collective-permute-start | bytes 1179656 | tf_op jit(solution)/shard_map/ppermute | solution.py:16
  104.6 17.0 %collective-permute-start.7 = (f32[4,192,128]{2,1,0:T(8,128)}, f32[4,192,128]{2,1,0:T(8,128)}, u32[]{:S(2)}, u32[]{:S(2)}) collective-permute-start(f32[4,192,128]{2,1,0:T(8,128)} %get-tuple-element.85), channel_id=1, source_target_pairs={{0,4},{4,8},{8,12},{12,16},{16,20},{20,24},{24,28},{28,32},{32,36}... | collective-permute-start | bytes 1179656 | tf_op jit(solution)/shard_map/ppermute | solution.py:15
  124.5 15.6 %collective-permute-start.8 = (f32[4,192,128]{2,1,0:T(8,128)}, f32[4,192,128]{2,1,0:T(8,128)}, u32[]{:S(2)}, u32[]{:S(2)}) collective-permute-start(f32[4,192,128]{2,1,0:T(8,128)} %get-tuple-element.84), channel_id=1, source_target_pairs={{4,0},{8,4},{12,8},{16,12},{20,16},{24,20},{28,24},{32,28},{36,32}... | collective-permute-start | bytes 1179656 | tf_op jit(solution)/shard_map/ppermute | solution.py:16
  126.5 16.4 %collective-permute-start.9 = (f32[4,192,128]{2,1,0:T(8,128)}, f32[4,192,128]{2,1,0:T(8,128)}, u32[]{:S(2)}, u32[]{:S(2)}) collective-permute-start(f32[4,192,128]{2,1,0:T(8,128)} %get-tuple-element.83), channel_id=1, source_target_pairs={{0,4},{4,8},{8,12},{12,16},{16,20},{20,24},{24,28},{28,32},{32,36}... | collective-permute-start | bytes 1179656 | tf_op jit(solution)/shard_map/ppermute | solution.py:15
  145.8 15.6 %collective-permute-start.10 = (f32[4,192,128]{2,1,0:T(8,128)}, f32[4,192,128]{2,1,0:T(8,128)}, u32[]{:S(2)}, u32[]{:S(2)}) collective-permute-start(f32[4,192,128]{2,1,0:T(8,128)} %get-tuple-element.82), channel_id=1, source_target_pairs={{4,0},{8,4},{12,8},{16,12},{20,16},{24,20},{28,24},{32,28},{36,32}... | collective-permute-start | bytes 1179656 | tf_op jit(solution)/shard_map/ppermute | solution.py:16
  147.8 26.0 %collective-permute-start.11 = (f32[4,192,128]{2,1,0:T(8,128)}, f32[4,192,128]{2,1,0:T(8,128)}, u32[]{:S(2)}, u32[]{:S(2)}) collective-permute-start(f32[4,192,128]{2,1,0:T(8,128)} %get-tuple-element.81), channel_id=1, source_target_pairs={{0,4},{4,8},{8,12},{12,16},{16,20},{20,24},{24,28},{28,32},{32,36}... | collective-permute-start | bytes 1179656 | tf_op jit(solution)/shard_map/ppermute | solution.py:15
  175.7 30.8 %copy-start.1 = (f32[8,192,128]{2,1,0:T(8,128)}, f32[8,192,128]{2,1,0:T(8,128)S(1)}, u32[]{:S(2)}) copy-start(f32[8,192,128]{2,1,0:T(8,128)S(1)} %fusion.71) | copy-start | bytes 2359300
  176.6 15.1 %collective-permute-start.12 = (f32[4,192,128]{2,1,0:T(8,128)}, f32[4,192,128]{2,1,0:T(8,128)}, u32[]{:S(2)}, u32[]{:S(2)}) collective-permute-start(f32[4,192,128]{2,1,0:T(8,128)} %get-tuple-element.80), channel_id=1, source_target_pairs={{4,0},{8,4},{12,8},{16,12},{20,16},{24,20},{28,24},{32,28},{36,32}... | collective-permute-start | bytes 1179656 | tf_op jit(solution)/shard_map/ppermute | solution.py:16
  178.5 17.6 %collective-permute-start.13 = (f32[4,192,128]{2,1,0:T(8,128)}, f32[4,192,128]{2,1,0:T(8,128)}, u32[]{:S(2)}, u32[]{:S(2)}) collective-permute-start(f32[4,192,128]{2,1,0:T(8,128)} %get-tuple-element.79), channel_id=1, source_target_pairs={{0,4},{4,8},{8,12},{12,16},{16,20},{20,24},{24,28},{28,32},{32,36}... | collective-permute-start | bytes 1179656 | tf_op jit(solution)/shard_map/ppermute | solution.py:15
  199.1 15.6 %collective-permute-start.14 = (f32[4,192,128]{2,1,0:T(8,128)}, f32[4,192,128]{2,1,0:T(8,128)}, u32[]{:S(2)}, u32[]{:S(2)}) collective-permute-start(f32[4,192,128]{2,1,0:T(8,128)} %get-tuple-element.78), channel_id=1, source_target_pairs={{4,0},{8,4},{12,8},{16,12},{20,16},{24,20},{28,24},{32,28},{36,32}... | collective-permute-start | bytes 1179656 | tf_op jit(solution)/shard_map/ppermute | solution.py:16
  201.0 17.0 %collective-permute-start.15 = (f32[4,192,128]{2,1,0:T(8,128)}, f32[4,192,128]{2,1,0:T(8,128)}, u32[]{:S(2)}, u32[]{:S(2)}) collective-permute-start(f32[4,192,128]{2,1,0:T(8,128)} %get-tuple-element.77), channel_id=1, source_target_pairs={{0,4},{4,8},{8,12},{12,16},{16,20},{20,24},{24,28},{28,32},{32,36}... | collective-permute-start | bytes 1179656 | tf_op jit(solution)/shard_map/ppermute | solution.py:15
  220.6 15.5 %collective-permute-start.16 = (f32[4,192,128]{2,1,0:T(8,128)}, f32[4,192,128]{2,1,0:T(8,128)S(1)}, u32[]{:S(2)}, u32[]{:S(2)}) collective-permute-start(f32[4,192,128]{2,1,0:T(8,128)} %get-tuple-element.76), channel_id=1, source_target_pairs={{4,0},{8,4},{12,8},{16,12},{20,16},{24,20},{28,24},{32,28},{36,32}... | collective-permute-start | bytes 1179656 | tf_op jit(solution)/shard_map/ppermute | solution.py:16
  222.5 16.3 %collective-permute-start.17 = (f32[4,192,128]{2,1,0:T(8,128)S(1)}, f32[4,192,128]{2,1,0:T(8,128)}, u32[]{:S(2)}, u32[]{:S(2)}) collective-permute-start(f32[4,192,128]{2,1,0:T(8,128)S(1)} %get-tuple-element.75), channel_id=1, source_target_pairs={{0,4},{4,8},{8,12},{12,16},{16,20},{20,24},{24,28},{28,32},{32,36}... | collective-permute-start | bytes 1179656 | tf_op jit(solution)/shard_map/ppermute | solution.py:15
  242.0 15.7 %collective-permute-start.18 = (f32[4,192,128]{2,1,0:T(8,128)}, f32[4,192,128]{2,1,0:T(8,128)}, u32[]{:S(2)}, u32[]{:S(2)}) collective-permute-start(f32[4,192,128]{2,1,0:T(8,128)} %get-tuple-element.74), channel_id=1, source_target_pairs={{4,0},{8,4},{12,8},{16,12},{20,16},{24,20},{28,24},{32,28},{36,32}... | collective-permute-start | bytes 1179656 | tf_op jit(solution)/shard_map/ppermute | solution.py:16
  243.9 26.1 %collective-permute-start.19 = (f32[4,192,128]{2,1,0:T(8,128)}, f32[4,192,128]{2,1,0:T(8,128)}, u32[]{:S(2)}, u32[]{:S(2)}) collective-permute-start(f32[4,192,128]{2,1,0:T(8,128)} %get-tuple-element.73), channel_id=1, source_target_pairs={{0,4},{4,8},{8,12},{12,16},{16,20},{20,24},{24,28},{28,32},{32,36}... | collective-permute-start | bytes 1179656 | tf_op jit(solution)/shard_map/ppermute | solution.py:15
  286.5 38.9 %collective-permute-start.22 = (f32[4,192,128]{2,1,0:T(8,128)}, f32[4,192,128]{2,1,0:T(8,128)S(1)}, u32[]{:S(2)}, u32[]{:S(2)}) collective-permute-start(f32[4,192,128]{2,1,0:T(8,128)} %get-tuple-element.70), channel_id=1, source_target_pairs={{4,0},{8,4},{12,8},{16,12},{20,16},{24,20},{28,24},{32,28},{36,32}... | collective-permute-start | bytes 1179656 | tf_op jit(solution)/shard_map/ppermute | solution.py:16
  288.4 37.0 %collective-permute-start.23 = (f32[4,192,128]{2,1,0:T(8,128)}, f32[4,192,128]{2,1,0:T(8,128)}, u32[]{:S(2)}, u32[]{:S(2)}) collective-permute-start(f32[4,192,128]{2,1,0:T(8,128)} %get-tuple-element.69), channel_id=1, source_target_pairs={{0,4},{4,8},{8,12},{12,16},{16,20},{20,24},{24,28},{28,32},{32,36}... | collective-permute-start | bytes 1179656 | tf_op jit(solution)/shard_map/ppermute | solution.py:15
  327.3 15.0 %collective-permute-start.24 = (f32[4,192,128]{2,1,0:T(8,128)S(1)}, f32[4,192,128]{2,1,0:T(8,128)S(1)}, u32[]{:S(2)}, u32[]{:S(2)}) collective-permute-start(f32[4,192,128]{2,1,0:T(8,128)S(1)} %get-tuple-element.66), channel_id=1, source_target_pairs={{4,0},{8,4},{12,8},{16,12},{20,16},{24,20},{28,24},{32,28},{36,32}... | collective-permute-start | bytes 1179656 | tf_op jit(solution)/shard_map/ppermute | solution.py:16
  329.4 26.6 %collective-permute-start.25 = (f32[4,192,128]{2,1,0:T(8,128)S(1)}, f32[4,192,128]{2,1,0:T(8,128)S(1)}, u32[]{:S(2)}, u32[]{:S(2)}) collective-permute-start(f32[4,192,128]{2,1,0:T(8,128)S(1)} %get-tuple-element.65), channel_id=1, source_target_pairs={{0,4},{4,8},{8,12},{12,16},{16,20},{20,24},{24,28},{28,32},{32,36}... | collective-permute-start | bytes 1179656 | tf_op jit(solution)/shard_map/ppermute | solution.py:15
  356.3 14.9 %collective-permute-start.26 = (f32[4,192,128]{2,1,0:T(8,128)S(1)}, f32[4,192,128]{2,1,0:T(8,128)S(1)}, u32[]{:S(2)}, u32[]{:S(2)}) collective-permute-start(f32[4,192,128]{2,1,0:T(8,128)S(1)} %get-tuple-element.62), channel_id=1, source_target_pairs={{4,0},{8,4},{12,8},{16,12},{20,16},{24,20},{28,24},{32,28},{36,32}... | collective-permute-start | bytes 1179656 | tf_op jit(solution)/shard_map/ppermute | solution.py:16
  358.3 18.6 %collective-permute-start.27 = (f32[4,192,128]{2,1,0:T(8,128)S(1)}, f32[4,192,128]{2,1,0:T(8,128)S(1)}, u32[]{:S(2)}, u32[]{:S(2)}) collective-permute-start(f32[4,192,128]{2,1,0:T(8,128)S(1)} %get-tuple-element.61), channel_id=1, source_target_pairs={{0,4},{4,8},{8,12},{12,16},{16,20},{20,24},{24,28},{28,32},{32,36}... | collective-permute-start | bytes 1179656 | tf_op jit(solution)/shard_map/ppermute | solution.py:15
  377.3 14.9 %collective-permute-start.28 = (f32[4,192,128]{2,1,0:T(8,128)S(1)}, f32[4,192,128]{2,1,0:T(8,128)S(1)}, u32[]{:S(2)}, u32[]{:S(2)}) collective-permute-start(f32[4,192,128]{2,1,0:T(8,128)S(1)} %get-tuple-element.58), channel_id=1, source_target_pairs={{4,0},{8,4},{12,8},{16,12},{20,16},{24,20},{28,24},{32,28},{36,32}... | collective-permute-start | bytes 1179656 | tf_op jit(solution)/shard_map/ppermute | solution.py:16
  379.3 17.2 %collective-permute-start.29 = (f32[4,192,128]{2,1,0:T(8,128)S(1)}, f32[4,192,128]{2,1,0:T(8,128)S(1)}, u32[]{:S(2)}, u32[]{:S(2)}) collective-permute-start(f32[4,192,128]{2,1,0:T(8,128)S(1)} %get-tuple-element.57), channel_id=1, source_target_pairs={{0,4},{4,8},{8,12},{12,16},{16,20},{20,24},{24,28},{28,32},{32,36}... | collective-permute-start | bytes 1179656 | tf_op jit(solution)/shard_map/ppermute | solution.py:15
  396.9 15.4 %collective-permute-start.30 = (f32[4,192,128]{2,1,0:T(8,128)S(1)}, f32[4,192,128]{2,1,0:T(8,128)S(1)}, u32[]{:S(2)}, u32[]{:S(2)}) collective-permute-start(f32[4,192,128]{2,1,0:T(8,128)S(1)} %get-tuple-element.54), channel_id=1, source_target_pairs={{4,0},{8,4},{12,8},{16,12},{20,16},{24,20},{28,24},{32,28},{36,32}... | collective-permute-start | bytes 1179656 | tf_op jit(solution)/shard_map/ppermute | solution.py:16
  399.0 16.7 %collective-permute-start.31 = (f32[4,192,128]{2,1,0:T(8,128)S(1)}, f32[4,192,128]{2,1,0:T(8,128)S(1)}, u32[]{:S(2)}, u32[]{:S(2)}) collective-permute-start(f32[4,192,128]{2,1,0:T(8,128)S(1)} %get-tuple-element.53), channel_id=1, source_target_pairs={{0,4},{4,8},{8,12},{12,16},{16,20},{20,24},{24,28},{28,32},{32,36}... | collective-permute-start | bytes 1179656 | tf_op jit(solution)/shard_map/ppermute | solution.py:15
  416.1 15.4 %collective-permute-start.32 = (f32[4,192,128]{2,1,0:T(8,128)S(1)}, f32[4,192,128]{2,1,0:T(8,128)S(1)}, u32[]{:S(2)}, u32[]{:S(2)}) collective-permute-start(f32[4,192,128]{2,1,0:T(8,128)S(1)} %get-tuple-element.50), channel_id=1, source_target_pairs={{4,0},{8,4},{12,8},{16,12},{20,16},{24,20},{28,24},{32,28},{36,32}... | collective-permute-start | bytes 1179656 | tf_op jit(solution)/shard_map/ppermute | solution.py:16
  418.1 20.2 %collective-permute-start.33 = (f32[4,192,128]{2,1,0:T(8,128)S(1)}, f32[4,192,128]{2,1,0:T(8,128)S(1)}, u32[]{:S(2)}, u32[]{:S(2)}) collective-permute-start(f32[4,192,128]{2,1,0:T(8,128)S(1)} %get-tuple-element.49), channel_id=1, source_target_pairs={{0,4},{4,8},{8,12},{12,16},{16,20},{20,24},{24,28},{28,32},{32,36}... | collective-permute-start | bytes 1179656 | tf_op jit(solution)/shard_map/ppermute | solution.py:15
  438.7 15.0 %collective-permute-start.34 = (f32[4,192,128]{2,1,0:T(8,128)S(1)}, f32[4,192,128]{2,1,0:T(8,128)S(1)}, u32[]{:S(2)}, u32[]{:S(2)}) collective-permute-start(f32[4,192,128]{2,1,0:T(8,128)S(1)} %get-tuple-element.46), channel_id=1, source_target_pairs={{4,0},{8,4},{12,8},{16,12},{20,16},{24,20},{28,24},{32,28},{36,32}... | collective-permute-start | bytes 1179656 | tf_op jit(solution)/shard_map/ppermute | solution.py:16
  440.8 19.3 %collective-permute-start.35 = (f32[4,192,128]{2,1,0:T(8,128)S(1)}, f32[4,192,128]{2,1,0:T(8,128)S(1)}, u32[]{:S(2)}, u32[]{:S(2)}) collective-permute-start(f32[4,192,128]{2,1,0:T(8,128)S(1)} %get-tuple-element.45), channel_id=1, source_target_pairs={{0,4},{4,8},{8,12},{12,16},{16,20},{20,24},{24,28},{28,32},{32,36}... | collective-permute-start | bytes 1179656 | tf_op jit(solution)/shard_map/ppermute | solution.py:15
  460.4 15.0 %collective-permute-start.36 = (f32[4,192,128]{2,1,0:T(8,128)S(1)}, f32[4,192,128]{2,1,0:T(8,128)S(1)}, u32[]{:S(2)}, u32[]{:S(2)}) collective-permute-start(f32[4,192,128]{2,1,0:T(8,128)S(1)} %get-tuple-element.42), channel_id=1, source_target_pairs={{4,0},{8,4},{12,8},{16,12},{20,16},{24,20},{28,24},{32,28},{36,32}... | collective-permute-start | bytes 1179656 | tf_op jit(solution)/shard_map/ppermute | solution.py:16
  462.5 19.1 %collective-permute-start.37 = (f32[4,192,128]{2,1,0:T(8,128)S(1)}, f32[4,192,128]{2,1,0:T(8,128)S(1)}, u32[]{:S(2)}, u32[]{:S(2)}) collective-permute-start(f32[4,192,128]{2,1,0:T(8,128)S(1)} %get-tuple-element.41), channel_id=1, source_target_pairs={{0,4},{4,8},{8,12},{12,16},{16,20},{20,24},{24,28},{28,32},{32,36}... | collective-permute-start | bytes 1179656 | tf_op jit(solution)/shard_map/ppermute | solution.py:15
  481.9 15.0 %collective-permute-start.38 = (f32[4,192,128]{2,1,0:T(8,128)S(1)}, f32[4,192,128]{2,1,0:T(8,128)S(1)}, u32[]{:S(2)}, u32[]{:S(2)}) collective-permute-start(f32[4,192,128]{2,1,0:T(8,128)S(1)} %get-tuple-element.38), channel_id=1, source_target_pairs={{4,0},{8,4},{12,8},{16,12},{20,16},{24,20},{28,24},{32,28},{36,32}... | collective-permute-start | bytes 1179656 | tf_op jit(solution)/shard_map/ppermute | solution.py:16
  483.9 19.8 %collective-permute-start.39 = (f32[4,192,128]{2,1,0:T(8,128)S(1)}, f32[4,192,128]{2,1,0:T(8,128)S(1)}, u32[]{:S(2)}, u32[]{:S(2)}) collective-permute-start(f32[4,192,128]{2,1,0:T(8,128)S(1)} %get-tuple-element.37), channel_id=1, source_target_pairs={{0,4},{4,8},{8,12},{12,16},{16,20},{20,24},{24,28},{28,32},{32,36}... | collective-permute-start | bytes 1179656 | tf_op jit(solution)/shard_map/ppermute | solution.py:15
  491.7 12.3 %copy-start.27 = (f32[8,192,128]{2,1,0:T(8,128)S(1)}, f32[8,192,128]{2,1,0:T(8,128)}, u32[]{:S(2)}) copy-start(f32[8,192,128]{2,1,0:T(8,128)} %get-tuple-element.17) | copy-start | bytes 2359300
  504.2 3.6 collective-permute-start.40
  507.9 10.3 %collective-permute-start.41 = (f32[8,48,128]{2,1,0:T(8,128)S(1)}, f32[8,48,128]{2,1,0:T(8,128)S(1)}, u32[]{:S(2)}, u32[]{:S(2)}) collective-permute-start(f32[8,48,128]{2,1,0:T(8,128)S(1)} %dynamic-slice_bitcast_fusion), channel_id=1, source_target_pairs={{0,2},{1,3},{2,0},{3,1},{4,6},{5,7},{6,4},{7,5},{8,10},{9,11},{10,... | collective-permute-start | bytes 589832 | tf_op jit(solution)/shard_map/ppermute | solution.py:139
  (63 other events, 360.8 us)

commit v2 on v1

--- a/solution.py
+++ b/solution.py
@@ -63,13 +63,15 @@
 
 def place_cells(shape, cells, amounts):
     lanes = shape[-1]
-    chosen = lax.broadcasted_iota(jnp.int32, (cells.shape[0], lanes), 1) == (cells % lanes)[:, None]
-    rows = jnp.where(chosen, amounts[:, None], 0.0)
     size = 1
     for extent in shape:
         size *= extent
-    flat = jnp.zeros((size // lanes, lanes), jnp.float32).at[cells // lanes].add(rows)
-    return flat.reshape(shape)
+    rows = lax.broadcasted_iota(jnp.int32, (size // lanes, cells.shape[0]), 0)
+    by_row = jnp.where(rows == (cells // lanes)[None, :], amounts[None, :], 0.0)
+    columns = lax.broadcasted_iota(jnp.int32, (cells.shape[0], lanes), 1)
+    by_lane = (columns == (cells % lanes)[:, None]).astype(jnp.float32)
+    placed = jnp.dot(by_row, by_lane, precision=lax.Precision.HIGHEST)
+    return placed.reshape(shape)
 
 
 def step(current, former, courant_sq, injected):

time: 529 us -> 500 us (0.945)
  other arithmetic: 151 us -> 93.2 us
  matrix products: 0 us -> 32.9 us
    scatter-add x20 -> x0, other arithmetic: 54.9 us -> none  [place_cells(): jnp.zeros((size // lanes, lanes), jnp.float32).at[cells // lanes].add(rows)]
    dot_general x0 -> x20, matrix products: none -> 32.9 us  [place_cells(): placed = jnp.dot(by_row, by_lane, precision=lax.Precision.HIGHEST)]
    ppermute x20, waiting for transfers between devices: 69 us -> 60.4 us  [exchange_edges(): high = lax.ppermute(block[:RADIUS], 'space', backward)]
    ppermute x20, waiting for transfers between devices: 110 us -> 117 us  [exchange_edges(): low = lax.ppermute(block[block.shape[0] - RADIUS:], 'space', forward)]
  transfers between devices with their start and end apart: 42 -> 42, of which waited for: 36 -> 36; matrix products, arithmetic and copies ran while one was open for 33% -> 30% of each run, Pallas kernels for 0% -> 0%
where the time goes in v2:
time: 500 us; the launch traced here: 491 us
  waiting for transfers between devices  186 us (37%)
  starting transfers between devices  147 us (29%)
  other arithmetic  93.2 us (19%)
  matrix products  32.9 us (7%)
  local copies, waits for them, and re-layouts  29.5 us (6%)
    ppermute x20, waiting for transfers between devices, exchange_edges(): low = lax.ppermute(block[block.shape[0] - RADIUS:], 'space', forward)  117 us
    ppermute x20, starting transfers between devices, exchange_edges(): low = lax.ppermute(block[block.shape[0] - RADIUS:], 'space', forward)  95.2 us
    ppermute x20, waiting for transfers between devices, exchange_edges(): high = lax.ppermute(block[:RADIUS], 'space', backward)  60.4 us
    ppermute x20, starting transfers between devices, exchange_edges(): high = lax.ppermute(block[:RADIUS], 'space', backward)  46.3 us
    add x10, other arithmetic, per_device(): latest - 2.0 * current + former  34 us
    dot_general x20, matrix products, place_cells(): placed = jnp.dot(by_row, by_lane, precision=lax.Precision.HIGHEST)  32.9 us
    add x11, other arithmetic, step(): 2.0 * current - former + courant_sq * inner_laplace(current) + injected  31.6 us
    add x20, other arithmetic, step(): base + courant_sq * edge_terms(low, high, current.shape[0])  23.5 us
  transfers between devices with their start and end apart: 42, of which 36 were waited for; matrix products, arithmetic and copies ran while one was open for 30% of the time, Pallas kernels for 0%

profile of v2, /device:TPU:454, one launch (start us, length us, event | category | flops | bytes accessed | tf_op | source)
XLA Modules:
  0.0 490.8 jit_solution(8932492669689613846)
XLA Ops:
  4.9 4.0 collective-permute-start.1
  9.8 3.9 collective-permute-start.20
  38.7 6.0 %collective-permute-start.2 = (f32[4,192,128]{2,1,0:T(8,128)}, f32[4,192,128]{2,1,0:T(8,128)}, u32[]{:S(2)}, u32[]{:S(2)}) collective-permute-start(f32[4,192,128]{2,1,0:T(8,128)} %get-tuple-element.92), channel_id=1, source_target_pairs={{4,0},{8,4},{12,8},{16,12},{20,16},{24,20},{28,24},{32,28},{36,32}... | collective-permute-start | bytes 1179656 | tf_op jit(solution)/shard_map/ppermute | solution.py:16
  46.6 3.7 bitcast_add_fusion
  54.6 12.0 %collective-permute-done.3 = f32[4,192,128]{2,1,0:T(8,128)} collective-permute-done((f32[4,192,128]{2,1,0:T(8,128)}, f32[4,192,128]{2,1,0:T(8,128)}, u32[]{:S(2)}, u32[]{:S(2)}) %collective-permute-start.3) | collective-permute-done | bytes 393248 | tf_op jit(solution)/shard_map/ppermute | solution.py:15
  71.5 5.0 %collective-permute-start.5 = (f32[4,192,128]{2,1,0:T(8,128)}, f32[4,192,128]{2,1,0:T(8,128)}, u32[]{:S(2)}, u32[]{:S(2)}) collective-permute-start(f32[4,192,128]{2,1,0:T(8,128)} %get-tuple-element.89), channel_id=1, source_target_pairs={{0,4},{4,8},{8,12},{12,16},{16,20},{20,24},{24,28},{28,32},{32,36}... | collective-permute-start | bytes 1179656 | tf_op jit(solution)/shard_map/ppermute | solution.py:15
  76.5 3.7 subtract_add_fusion
  84.6 4.4 collective-permute-done.5
  93.9 5.3 %collective-permute-start.7 = (f32[4,192,128]{2,1,0:T(8,128)}, f32[4,192,128]{2,1,0:T(8,128)}, u32[]{:S(2)}, u32[]{:S(2)}) collective-permute-start(f32[4,192,128]{2,1,0:T(8,128)} %get-tuple-element.87), channel_id=1, source_target_pairs={{0,4},{4,8},{8,12},{12,16},{16,20},{20,24},{24,28},{28,32},{32,36}... | collective-permute-start | bytes 1179656 | tf_op jit(solution)/shard_map/ppermute | solution.py:15
  99.2 3.7 subtract_add_fusion.1
  115.9 5.3 %collective-permute-start.9 = (f32[4,192,128]{2,1,0:T(8,128)}, f32[4,192,128]{2,1,0:T(8,128)}, u32[]{:S(2)}, u32[]{:S(2)}) collective-permute-start(f32[4,192,128]{2,1,0:T(8,128)} %get-tuple-element.85), channel_id=1, source_target_pairs={{0,4},{4,8},{8,12},{12,16},{16,20},{20,24},{24,28},{28,32},{32,36}... | collective-permute-start | bytes 1179656 | tf_op jit(solution)/shard_map/ppermute | solution.py:15
  121.2 3.6 subtract_add_fusion.2
  137.2 5.3 %collective-permute-start.11 = (f32[4,192,128]{2,1,0:T(8,128)}, f32[4,192,128]{2,1,0:T(8,128)}, u32[]{:S(2)}, u32[]{:S(2)}) collective-permute-start(f32[4,192,128]{2,1,0:T(8,128)} %get-tuple-element.83), channel_id=1, source_target_pairs={{0,4},{4,8},{8,12},{12,16},{16,20},{20,24},{24,28},{28,32},{32,36}... | collective-permute-start | bytes 1179656 | tf_op jit(solution)/shard_map/ppermute | solution.py:15
  142.5 3.7 subtract_add_fusion.3
  150.9 12.3 %collective-permute-done.11 = f32[4,192,128]{2,1,0:T(8,128)} collective-permute-done((f32[4,192,128]{2,1,0:T(8,128)}, f32[4,192,128]{2,1,0:T(8,128)}, u32[]{:S(2)}, u32[]{:S(2)}) %collective-permute-start.11) | collective-permute-done | bytes 393248 | tf_op jit(solution)/shard_map/ppermute | solution.py:15
  168.0 4.8 collective-permute-start.13
  172.9 3.7 subtract_add_fusion.4
  181.2 4.4 collective-permute-done.13
  190.6 5.7 %collective-permute-start.15 = (f32[4,192,128]{2,1,0:T(8,128)}, f32[4,192,128]{2,1,0:T(8,128)}, u32[]{:S(2)}, u32[]{:S(2)}) collective-permute-start(f32[4,192,128]{2,1,0:T(8,128)} %get-tuple-element.79), channel_id=1, source_target_pairs={{0,4},{4,8},{8,12},{12,16},{16,20},{20,24},{24,28},{28,32},{32,36}... | collective-permute-start | bytes 1179656 | tf_op jit(solution)/shard_map/ppermute | solution.py:15
  196.3 3.6 subtract_add_fusion.5
  212.1 5.3 %collective-permute-start.17 = (f32[4,192,128]{2,1,0:T(8,128)S(1)}, f32[4,192,128]{2,1,0:T(8,128)}, u32[]{:S(2)}, u32[]{:S(2)}) collective-permute-start(f32[4,192,128]{2,1,0:T(8,128)S(1)} %get-tuple-element.77), channel_id=1, source_target_pairs={{0,4},{4,8},{8,12},{12,16},{16,20},{20,24},{24,28},{28,32},{32,36}... | collective-permute-start | bytes 1179656 | tf_op jit(solution)/shard_map/ppermute | solution.py:15
  217.4 3.7 subtract_add_fusion.6
  233.3 5.4 %collective-permute-start.19 = (f32[4,192,128]{2,1,0:T(8,128)}, f32[4,192,128]{2,1,0:T(8,128)}, u32[]{:S(2)}, u32[]{:S(2)}) collective-permute-start(f32[4,192,128]{2,1,0:T(8,128)} %get-tuple-element.75), channel_id=1, source_target_pairs={{0,4},{4,8},{8,12},{12,16},{16,20},{20,24},{24,28},{28,32},{32,36}... | collective-permute-start | bytes 1179656 | tf_op jit(solution)/shard_map/ppermute | solution.py:15
  238.7 3.7 subtract_add_fusion.7
  247.1 12.3 %collective-permute-done.19 = f32[4,192,128]{2,1,0:T(8,128)} collective-permute-done((f32[4,192,128]{2,1,0:T(8,128)}, f32[4,192,128]{2,1,0:T(8,128)}, u32[]{:S(2)}, u32[]{:S(2)}) %collective-permute-start.19) | collective-permute-done | bytes 393248 | tf_op jit(solution)/shard_map/ppermute | solution.py:15
  274.7 4.8 collective-permute-start.23
  302.5 4.8 collective-permute-start.25
  310.1 5.3 %collective-permute-done.24 = f32[4,192,128]{2,1,0:T(8,128)S(1)} collective-permute-done((f32[4,192,128]{2,1,0:T(8,128)S(1)}, f32[4,192,128]{2,1,0:T(8,128)S(1)}, u32[]{:S(2)}, u32[]{:S(2)}) %collective-permute-start.24) | collective-permute-done | bytes 393248 | tf_op jit(solution)/shard_map/ppermute | solution.py:16
  315.4 13.7 %collective-permute-done.25 = f32[4,192,128]{2,1,0:T(8,128)S(1)} collective-permute-done((f32[4,192,128]{2,1,0:T(8,128)S(1)}, f32[4,192,128]{2,1,0:T(8,128)S(1)}, u32[]{:S(2)}, u32[]{:S(2)}) %collective-permute-start.25) | collective-permute-done | bytes 393248 | tf_op jit(solution)/shard_map/ppermute | solution.py:15
  331.4 4.8 collective-permute-start.27
  339.0 5.2 %collective-permute-done.26 = f32[4,192,128]{2,1,0:T(8,128)S(1)} collective-permute-done((f32[4,192,128]{2,1,0:T(8,128)S(1)}, f32[4,192,128]{2,1,0:T(8,128)S(1)}, u32[]{:S(2)}, u32[]{:S(2)}) %collective-permute-start.26) | collective-permute-done | bytes 393248 | tf_op jit(solution)/shard_map/ppermute | solution.py:16
  344.3 8.3 %collective-permute-done.27 = f32[4,192,128]{2,1,0:T(8,128)S(1)} collective-permute-done((f32[4,192,128]{2,1,0:T(8,128)S(1)}, f32[4,192,128]{2,1,0:T(8,128)S(1)}, u32[]{:S(2)}, u32[]{:S(2)}) %collective-permute-start.27) | collective-permute-done | bytes 393248 | tf_op jit(solution)/shard_map/ppermute | solution.py:15
  354.9 4.8 collective-permute-start.29
  362.6 5.3 %collective-permute-done.28 = f32[4,192,128]{2,1,0:T(8,128)S(1)} collective-permute-done((f32[4,192,128]{2,1,0:T(8,128)S(1)}, f32[4,192,128]{2,1,0:T(8,128)S(1)}, u32[]{:S(2)}, u32[]{:S(2)}) %collective-permute-start.28) | collective-permute-done | bytes 393248 | tf_op jit(solution)/shard_map/ppermute | solution.py:16
  367.9 7.3 %collective-permute-done.29 = f32[4,192,128]{2,1,0:T(8,128)S(1)} collective-permute-done((f32[4,192,128]{2,1,0:T(8,128)S(1)}, f32[4,192,128]{2,1,0:T(8,128)S(1)}, u32[]{:S(2)}, u32[]{:S(2)}) %collective-permute-start.29) | collective-permute-done | bytes 393248 | tf_op jit(solution)/shard_map/ppermute | solution.py:15
  377.6 4.8 collective-permute-start.31
  388.6 4.0 collective-permute-done.31
  395.0 5.3 %collective-permute-start.33 = (f32[4,192,128]{2,1,0:T(8,128)S(1)}, f32[4,192,128]{2,1,0:T(8,128)S(1)}, u32[]{:S(2)}, u32[]{:S(2)}) collective-permute-start(f32[4,192,128]{2,1,0:T(8,128)S(1)} %get-tuple-element.51), channel_id=1, source_target_pairs={{0,4},{4,8},{8,12},{12,16},{16,20},{20,24},{24,28},{28,32},{32,36}... | collective-permute-start | bytes 1179656 | tf_op jit(solution)/shard_map/ppermute | solution.py:15
  405.4 4.6 collective-permute-done.33
  412.4 5.3 %collective-permute-start.35 = (f32[4,192,128]{2,1,0:T(8,128)S(1)}, f32[4,192,128]{2,1,0:T(8,128)S(1)}, u32[]{:S(2)}, u32[]{:S(2)}) collective-permute-start(f32[4,192,128]{2,1,0:T(8,128)S(1)} %get-tuple-element.47), channel_id=1, source_target_pairs={{0,4},{4,8},{8,12},{12,16},{16,20},{20,24},{24,28},{28,32},{32,36}... | collective-permute-start | bytes 1179656 | tf_op jit(solution)/shard_map/ppermute | solution.py:15
  422.3 9.2 %collective-permute-done.35 = f32[4,192,128]{2,1,0:T(8,128)S(1)} collective-permute-done((f32[4,192,128]{2,1,0:T(8,128)S(1)}, f32[4,192,128]{2,1,0:T(8,128)S(1)}, u32[]{:S(2)}, u32[]{:S(2)}) %collective-permute-start.35) | collective-permute-done | bytes 393248 | tf_op jit(solution)/shard_map/ppermute | solution.py:15
  433.9 4.8 collective-permute-start.37
  441.5 5.3 %collective-permute-done.36 = f32[4,192,128]{2,1,0:T(8,128)S(1)} collective-permute-done((f32[4,192,128]{2,1,0:T(8,128)S(1)}, f32[4,192,128]{2,1,0:T(8,128)S(1)}, u32[]{:S(2)}, u32[]{:S(2)}) %collective-permute-start.36) | collective-permute-done | bytes 393248 | tf_op jit(solution)/shard_map/ppermute | solution.py:16
  446.8 6.4 %collective-permute-done.37 = f32[4,192,128]{2,1,0:T(8,128)S(1)} collective-permute-done((f32[4,192,128]{2,1,0:T(8,128)S(1)}, f32[4,192,128]{2,1,0:T(8,128)S(1)}, u32[]{:S(2)}, u32[]{:S(2)}) %collective-permute-start.37) | collective-permute-done | bytes 393248 | tf_op jit(solution)/shard_map/ppermute | solution.py:15
  455.6 4.8 collective-permute-start.39
  463.4 5.1 %collective-permute-done.38 = f32[4,192,128]{2,1,0:T(8,128)S(1)} collective-permute-done((f32[4,192,128]{2,1,0:T(8,128)S(1)}, f32[4,192,128]{2,1,0:T(8,128)S(1)}, u32[]{:S(2)}, u32[]{:S(2)}) %collective-permute-start.38) | collective-permute-done | bytes 393248 | tf_op jit(solution)/shard_map/ppermute | solution.py:16
  468.5 6.6 %collective-permute-done.39 = f32[4,192,128]{2,1,0:T(8,128)S(1)} collective-permute-done((f32[4,192,128]{2,1,0:T(8,128)S(1)}, f32[4,192,128]{2,1,0:T(8,128)S(1)}, u32[]{:S(2)}, u32[]{:S(2)}) %collective-permute-start.39) | collective-permute-done | bytes 393248 | tf_op jit(solution)/shard_map/ppermute | solution.py:15
  482.6 7.0 %collective-permute-done.41 = f32[8,48,128]{2,1,0:T(8,128)S(1)} collective-permute-done((f32[8,48,128]{2,1,0:T(8,128)S(1)}, f32[8,48,128]{2,1,0:T(8,128)S(1)}, u32[]{:S(2)}, u32[]{:S(2)}) %collective-permute-start.41) | collective-permute-done | bytes 196640 | tf_op jit(solution)/shard_map/ppermute | solution.py:141
  (249 shorter events, 216.3 us)
Async XLA Ops:
  0.0 8.9 %copy-start.4 = (f32[1,8,192,128]{3,2,1,0:T(8,128)S(1)}, f32[1,8,192,128]{3,2,1,0:T(8,128)}, u32[]{:S(2)}) copy-start(f32[1,8,192,128]{3,2,1,0:T(8,128)} %param.13) | copy-start | bytes 2359300
  2.1 34.0 %collective-permute-start = (f32[4,192,128]{2,1,0:T(8,128)}, f32[4,192,128]{2,1,0:T(8,128)S(1)}, u32[]{:S(2)}, u32[]{:S(2)}) collective-permute-start(f32[4,192,128]{2,1,0:T(8,128)} %get-tuple-element.94), channel_id=1, source_target_pairs={{4,0},{8,4},{12,8},{16,12},{20,16},{24,20},{28,24},{32,28},{36,32}... | collective-permute-start | bytes 1179656 | tf_op jit(solution)/shard_map/ppermute | solution.py:16
  4.8 11.7 %copy-start.47 = (f32[1,10,128]{2,0,1:T(1,128)S(1)}, f32[1,10,128]{2,0,1:T(1,128)}, u32[]{:S(2)}) copy-start(f32[1,10,128]{2,0,1:T(1,128)} %param.16) | copy-start | bytes 15364
  4.9 11.7 %copy-start.48 = (s32[1,128]{1,0:T(1,128)S(1)}, s32[1,128]{1,0:T(1,128)}, u32[]{:S(2)}) copy-start(s32[1,128]{1,0:T(1,128)} %param.15) | copy-start | bytes 1540
  4.9 31.2 %collective-permute-start.1 = (f32[4,192,128]{2,1,0:T(8,128)}, f32[4,192,128]{2,1,0:T(8,128)}, u32[]{:S(2)}, u32[]{:S(2)}) collective-permute-start(f32[4,192,128]{2,1,0:T(8,128)} %get-tuple-element.93), channel_id=1, source_target_pairs={{0,4},{4,8},{8,12},{12,16},{16,20},{20,24},{24,28},{28,32},{32,36}... | collective-permute-start | bytes 1179656 | tf_op jit(solution)/shard_map/ppermute | solution.py:15
  9.8 261.1 %collective-permute-start.20 = (f32[4,192,128]{2,1,0:T(8,128)}, f32[4,192,128]{2,1,0:T(8,128)}, u32[]{:S(2)}, u32[]{:S(2)}) collective-permute-start(f32[4,192,128]{2,1,0:T(8,128)} %get-tuple-element.74), channel_id=1, source_target_pairs={{4,0},{8,4},{12,8},{16,12},{20,16},{24,20},{28,24},{32,28},{36,32}... | collective-permute-start | bytes 1179656 | tf_op jit(solution)/shard_map/ppermute | solution.py:16
  13.8 257.2 %collective-permute-start.21 = (f32[4,192,128]{2,1,0:T(8,128)}, f32[4,192,128]{2,1,0:T(8,128)}, u32[]{:S(2)}, u32[]{:S(2)}) collective-permute-start(f32[4,192,128]{2,1,0:T(8,128)} %get-tuple-element.73), channel_id=1, source_target_pairs={{0,4},{4,8},{8,12},{12,16},{16,20},{20,24},{24,28},{28,32},{32,36}... | collective-permute-start | bytes 1179656 | tf_op jit(solution)/shard_map/ppermute | solution.py:15
  37.7 8.9 %copy-start.27 = (f32[1,8,192,128]{3,2,1,0:T(8,128)S(1)}, f32[1,8,192,128]{3,2,1,0:T(8,128)}, u32[]{:S(2)}) copy-start(f32[1,8,192,128]{3,2,1,0:T(8,128)} %param.12) | copy-start | bytes 2359300
  38.7 15.9 %collective-permute-start.2 = (f32[4,192,128]{2,1,0:T(8,128)}, f32[4,192,128]{2,1,0:T(8,128)}, u32[]{:S(2)}, u32[]{:S(2)}) collective-permute-start(f32[4,192,128]{2,1,0:T(8,128)} %get-tuple-element.92), channel_id=1, source_target_pairs={{4,0},{8,4},{12,8},{16,12},{20,16},{24,20},{28,24},{32,28},{36,32}... | collective-permute-start | bytes 1179656 | tf_op jit(solution)/shard_map/ppermute | solution.py:16
  44.7 21.9 %collective-permute-start.3 = (f32[4,192,128]{2,1,0:T(8,128)}, f32[4,192,128]{2,1,0:T(8,128)}, u32[]{:S(2)}, u32[]{:S(2)}) collective-permute-start(f32[4,192,128]{2,1,0:T(8,128)} %get-tuple-element.91), channel_id=1, source_target_pairs={{0,4},{4,8},{8,12},{12,16},{16,20},{20,24},{24,28},{28,32},{32,36}... | collective-permute-start | bytes 1179656 | tf_op jit(solution)/shard_map/ppermute | solution.py:15
  69.6 15.1 %collective-permute-start.4 = (f32[4,192,128]{2,1,0:T(8,128)}, f32[4,192,128]{2,1,0:T(8,128)}, u32[]{:S(2)}, u32[]{:S(2)}) collective-permute-start(f32[4,192,128]{2,1,0:T(8,128)} %get-tuple-element.90), channel_id=1, source_target_pairs={{4,0},{8,4},{12,8},{16,12},{20,16},{24,20},{28,24},{32,28},{36,32}... | collective-permute-start | bytes 1179656 | tf_op jit(solution)/shard_map/ppermute | solution.py:16
  71.5 17.6 %collective-permute-start.5 = (f32[4,192,128]{2,1,0:T(8,128)}, f32[4,192,128]{2,1,0:T(8,128)}, u32[]{:S(2)}, u32[]{:S(2)}) collective-permute-start(f32[4,192,128]{2,1,0:T(8,128)} %get-tuple-element.89), channel_id=1, source_target_pairs={{0,4},{4,8},{8,12},{12,16},{16,20},{20,24},{24,28},{28,32},{32,36}... | collective-permute-start | bytes 1179656 | tf_op jit(solution)/shard_map/ppermute | solution.py:15
  92.0 15.6 %collective-permute-start.6 = (f32[4,192,128]{2,1,0:T(8,128)}, f32[4,192,128]{2,1,0:T(8,128)}, u32[]{:S(2)}, u32[]{:S(2)}) collective-permute-start(f32[4,192,128]{2,1,0:T(8,128)} %get-tuple-element.88), channel_id=1, source_target_pairs={{4,0},{8,4},{12,8},{16,12},{20,16},{24,20},{28,24},{32,28},{36,32}... | collective-permute-start | bytes 1179656 | tf_op jit(solution)/shard_map/ppermute | solution.py:16
  93.9 17.0 %collective-permute-start.7 = (f32[4,192,128]{2,1,0:T(8,128)}, f32[4,192,128]{2,1,0:T(8,128)}, u32[]{:S(2)}, u32[]{:S(2)}) collective-permute-start(f32[4,192,128]{2,1,0:T(8,128)} %get-tuple-element.87), channel_id=1, source_target_pairs={{0,4},{4,8},{8,12},{12,16},{16,20},{20,24},{24,28},{28,32},{32,36}... | collective-permute-start | bytes 1179656 | tf_op jit(solution)/shard_map/ppermute | solution.py:15
  113.9 15.6 %collective-permute-start.8 = (f32[4,192,128]{2,1,0:T(8,128)}, f32[4,192,128]{2,1,0:T(8,128)}, u32[]{:S(2)}, u32[]{:S(2)}) collective-permute-start(f32[4,192,128]{2,1,0:T(8,128)} %get-tuple-element.86), channel_id=1, source_target_pairs={{4,0},{8,4},{12,8},{16,12},{20,16},{24,20},{28,24},{32,28},{36,32}... | collective-permute-start | bytes 1179656 | tf_op jit(solution)/shard_map/ppermute | solution.py:16
  115.9 16.4 %collective-permute-start.9 = (f32[4,192,128]{2,1,0:T(8,128)}, f32[4,192,128]{2,1,0:T(8,128)}, u32[]{:S(2)}, u32[]{:S(2)}) collective-permute-start(f32[4,192,128]{2,1,0:T(8,128)} %get-tuple-element.85), channel_id=1, source_target_pairs={{0,4},{4,8},{8,12},{12,16},{16,20},{20,24},{24,28},{28,32},{32,36}... | collective-permute-start | bytes 1179656 | tf_op jit(solution)/shard_map/ppermute | solution.py:15
  135.3 15.6 %collective-permute-start.10 = (f32[4,192,128]{2,1,0:T(8,128)}, f32[4,192,128]{2,1,0:T(8,128)}, u32[]{:S(2)}, u32[]{:S(2)}) collective-permute-start(f32[4,192,128]{2,1,0:T(8,128)} %get-tuple-element.84), channel_id=1, source_target_pairs={{4,0},{8,4},{12,8},{16,12},{20,16},{24,20},{28,24},{32,28},{36,32}... | collective-permute-start | bytes 1179656 | tf_op jit(solution)/shard_map/ppermute | solution.py:16
  137.2 26.0 %collective-permute-start.11 = (f32[4,192,128]{2,1,0:T(8,128)}, f32[4,192,128]{2,1,0:T(8,128)}, u32[]{:S(2)}, u32[]{:S(2)}) collective-permute-start(f32[4,192,128]{2,1,0:T(8,128)} %get-tuple-element.83), channel_id=1, source_target_pairs={{0,4},{4,8},{8,12},{12,16},{16,20},{20,24},{24,28},{28,32},{32,36}... | collective-permute-start | bytes 1179656 | tf_op jit(solution)/shard_map/ppermute | solution.py:15
  165.1 31.1 %copy-start.1 = (f32[8,192,128]{2,1,0:T(8,128)}, f32[8,192,128]{2,1,0:T(8,128)S(1)}, u32[]{:S(2)}) copy-start(f32[8,192,128]{2,1,0:T(8,128)S(1)} %fusion.121) | copy-start | bytes 2359300
  166.1 15.1 %collective-permute-start.12 = (f32[4,192,128]{2,1,0:T(8,128)}, f32[4,192,128]{2,1,0:T(8,128)}, u32[]{:S(2)}, u32[]{:S(2)}) collective-permute-start(f32[4,192,128]{2,1,0:T(8,128)} %get-tuple-element.82), channel_id=1, source_target_pairs={{4,0},{8,4},{12,8},{16,12},{20,16},{24,20},{28,24},{32,28},{36,32}... | collective-permute-start | bytes 1179656 | tf_op jit(solution)/shard_map/ppermute | solution.py:16
  168.0 17.6 %collective-permute-start.13 = (f32[4,192,128]{2,1,0:T(8,128)}, f32[4,192,128]{2,1,0:T(8,128)}, u32[]{:S(2)}, u32[]{:S(2)}) collective-permute-start(f32[4,192,128]{2,1,0:T(8,128)} %get-tuple-element.81), channel_id=1, source_target_pairs={{0,4},{4,8},{8,12},{12,16},{16,20},{20,24},{24,28},{28,32},{32,36}... | collective-permute-start | bytes 1179656 | tf_op jit(solution)/shard_map/ppermute | solution.py:15
  188.6 15.6 %collective-permute-start.14 = (f32[4,192,128]{2,1,0:T(8,128)}, f32[4,192,128]{2,1,0:T(8,128)}, u32[]{:S(2)}, u32[]{:S(2)}) collective-permute-start(f32[4,192,128]{2,1,0:T(8,128)} %get-tuple-element.80), channel_id=1, source_target_pairs={{4,0},{8,4},{12,8},{16,12},{20,16},{24,20},{28,24},{32,28},{36,32}... | collective-permute-start | bytes 1179656 | tf_op jit(solution)/shard_map/ppermute | solution.py:16
  190.6 17.0 %collective-permute-start.15 = (f32[4,192,128]{2,1,0:T(8,128)}, f32[4,192,128]{2,1,0:T(8,128)}, u32[]{:S(2)}, u32[]{:S(2)}) collective-permute-start(f32[4,192,128]{2,1,0:T(8,128)} %get-tuple-element.79), channel_id=1, source_target_pairs={{0,4},{4,8},{8,12},{12,16},{16,20},{20,24},{24,28},{28,32},{32,36}... | collective-permute-start | bytes 1179656 | tf_op jit(solution)/shard_map/ppermute | solution.py:15
  210.2 15.5 %collective-permute-start.16 = (f32[4,192,128]{2,1,0:T(8,128)}, f32[4,192,128]{2,1,0:T(8,128)S(1)}, u32[]{:S(2)}, u32[]{:S(2)}) collective-permute-start(f32[4,192,128]{2,1,0:T(8,128)} %get-tuple-element.78), channel_id=1, source_target_pairs={{4,0},{8,4},{12,8},{16,12},{20,16},{24,20},{28,24},{32,28},{36,32}... | collective-permute-start | bytes 1179656 | tf_op jit(solution)/shard_map/ppermute | solution.py:16
  212.1 16.3 %collective-permute-start.17 = (f32[4,192,128]{2,1,0:T(8,128)S(1)}, f32[4,192,128]{2,1,0:T(8,128)}, u32[]{:S(2)}, u32[]{:S(2)}) collective-permute-start(f32[4,192,128]{2,1,0:T(8,128)S(1)} %get-tuple-element.77), channel_id=1, source_target_pairs={{0,4},{4,8},{8,12},{12,16},{16,20},{20,24},{24,28},{28,32},{32,36}... | collective-permute-start | bytes 1179656 | tf_op jit(solution)/shard_map/ppermute | solution.py:15
  231.4 15.7 %collective-permute-start.18 = (f32[4,192,128]{2,1,0:T(8,128)}, f32[4,192,128]{2,1,0:T(8,128)}, u32[]{:S(2)}, u32[]{:S(2)}) collective-permute-start(f32[4,192,128]{2,1,0:T(8,128)} %get-tuple-element.76), channel_id=1, source_target_pairs={{4,0},{8,4},{12,8},{16,12},{20,16},{24,20},{28,24},{32,28},{36,32}... | collective-permute-start | bytes 1179656 | tf_op jit(solution)/shard_map/ppermute | solution.py:16
  233.3 26.1 %collective-permute-start.19 = (f32[4,192,128]{2,1,0:T(8,128)}, f32[4,192,128]{2,1,0:T(8,128)}, u32[]{:S(2)}, u32[]{:S(2)}) collective-permute-start(f32[4,192,128]{2,1,0:T(8,128)} %get-tuple-element.75), channel_id=1, source_target_pairs={{0,4},{4,8},{8,12},{12,16},{16,20},{20,24},{24,28},{28,32},{32,36}... | collective-permute-start | bytes 1179656 | tf_op jit(solution)/shard_map/ppermute | solution.py:15
  272.8 27.3 %collective-permute-start.22 = (f32[4,192,128]{2,1,0:T(8,128)S(1)}, f32[4,192,128]{2,1,0:T(8,128)S(1)}, u32[]{:S(2)}, u32[]{:S(2)}) collective-permute-start(f32[4,192,128]{2,1,0:T(8,128)S(1)} %get-tuple-element.72), channel_id=1, source_target_pairs={{4,0},{8,4},{12,8},{16,12},{20,16},{24,20},{28,24},{32,28},{36,32}... | collective-permute-start | bytes 1179656 | tf_op jit(solution)/shard_map/ppermute | solution.py:16
  274.7 25.4 %collective-permute-start.23 = (f32[4,192,128]{2,1,0:T(8,128)S(1)}, f32[4,192,128]{2,1,0:T(8,128)S(1)}, u32[]{:S(2)}, u32[]{:S(2)}) collective-permute-start(f32[4,192,128]{2,1,0:T(8,128)S(1)} %get-tuple-element.71), channel_id=1, source_target_pairs={{0,4},{4,8},{8,12},{12,16},{16,20},{20,24},{24,28},{28,32},{32,36}... | collective-permute-start | bytes 1179656 | tf_op jit(solution)/shard_map/ppermute | solution.py:15
  300.4 15.0 %collective-permute-start.24 = (f32[4,192,128]{2,1,0:T(8,128)S(1)}, f32[4,192,128]{2,1,0:T(8,128)S(1)}, u32[]{:S(2)}, u32[]{:S(2)}) collective-permute-start(f32[4,192,128]{2,1,0:T(8,128)S(1)} %get-tuple-element.68), channel_id=1, source_target_pairs={{4,0},{8,4},{12,8},{16,12},{20,16},{24,20},{28,24},{32,28},{36,32}... | collective-permute-start | bytes 1179656 | tf_op jit(solution)/shard_map/ppermute | solution.py:16
  302.5 26.6 %collective-permute-start.25 = (f32[4,192,128]{2,1,0:T(8,128)S(1)}, f32[4,192,128]{2,1,0:T(8,128)S(1)}, u32[]{:S(2)}, u32[]{:S(2)}) collective-permute-start(f32[4,192,128]{2,1,0:T(8,128)S(1)} %get-tuple-element.67), channel_id=1, source_target_pairs={{0,4},{4,8},{8,12},{12,16},{16,20},{20,24},{24,28},{28,32},{32,36}... | collective-permute-start | bytes 1179656 | tf_op jit(solution)/shard_map/ppermute | solution.py:15
  329.4 14.9 %collective-permute-start.26 = (f32[4,192,128]{2,1,0:T(8,128)S(1)}, f32[4,192,128]{2,1,0:T(8,128)S(1)}, u32[]{:S(2)}, u32[]{:S(2)}) collective-permute-start(f32[4,192,128]{2,1,0:T(8,128)S(1)} %get-tuple-element.64), channel_id=1, source_target_pairs={{4,0},{8,4},{12,8},{16,12},{20,16},{24,20},{28,24},{32,28},{36,32}... | collective-permute-start | bytes 1179656 | tf_op jit(solution)/shard_map/ppermute | solution.py:16
  331.4 21.1 %collective-permute-start.27 = (f32[4,192,128]{2,1,0:T(8,128)S(1)}, f32[4,192,128]{2,1,0:T(8,128)S(1)}, u32[]{:S(2)}, u32[]{:S(2)}) collective-permute-start(f32[4,192,128]{2,1,0:T(8,128)S(1)} %get-tuple-element.63), channel_id=1, source_target_pairs={{0,4},{4,8},{8,12},{12,16},{16,20},{20,24},{24,28},{28,32},{32,36}... | collective-permute-start | bytes 1179656 | tf_op jit(solution)/shard_map/ppermute | solution.py:15
  352.9 15.0 %collective-permute-start.28 = (f32[4,192,128]{2,1,0:T(8,128)S(1)}, f32[4,192,128]{2,1,0:T(8,128)S(1)}, u32[]{:S(2)}, u32[]{:S(2)}) collective-permute-start(f32[4,192,128]{2,1,0:T(8,128)S(1)} %get-tuple-element.60), channel_id=1, source_target_pairs={{4,0},{8,4},{12,8},{16,12},{20,16},{24,20},{28,24},{32,28},{36,32}... | collective-permute-start | bytes 1179656 | tf_op jit(solution)/shard_map/ppermute | solution.py:16
  354.9 20.2 %collective-permute-start.29 = (f32[4,192,128]{2,1,0:T(8,128)S(1)}, f32[4,192,128]{2,1,0:T(8,128)S(1)}, u32[]{:S(2)}, u32[]{:S(2)}) collective-permute-start(f32[4,192,128]{2,1,0:T(8,128)S(1)} %get-tuple-element.59), channel_id=1, source_target_pairs={{0,4},{4,8},{8,12},{12,16},{16,20},{20,24},{24,28},{28,32},{32,36}... | collective-permute-start | bytes 1179656 | tf_op jit(solution)/shard_map/ppermute | solution.py:15
  375.5 13.1 %collective-permute-start.30 = (f32[4,192,128]{2,1,0:T(8,128)S(1)}, f32[4,192,128]{2,1,0:T(8,128)S(1)}, u32[]{:S(2)}, u32[]{:S(2)}) collective-permute-start(f32[4,192,128]{2,1,0:T(8,128)S(1)} %get-tuple-element.56), channel_id=1, source_target_pairs={{4,0},{8,4},{12,8},{16,12},{20,16},{24,20},{28,24},{32,28},{36,32}... | collective-permute-start | bytes 1179656 | tf_op jit(solution)/shard_map/ppermute | solution.py:16
  377.6 15.0 %collective-permute-start.31 = (f32[4,192,128]{2,1,0:T(8,128)S(1)}, f32[4,192,128]{2,1,0:T(8,128)S(1)}, u32[]{:S(2)}, u32[]{:S(2)}) collective-permute-start(f32[4,192,128]{2,1,0:T(8,128)S(1)} %get-tuple-element.55), channel_id=1, source_target_pairs={{0,4},{4,8},{8,12},{12,16},{16,20},{20,24},{24,28},{28,32},{32,36}... | collective-permute-start | bytes 1179656 | tf_op jit(solution)/shard_map/ppermute | solution.py:15
  392.9 12.5 %collective-permute-start.32 = (f32[4,192,128]{2,1,0:T(8,128)S(1)}, f32[4,192,128]{2,1,0:T(8,128)S(1)}, u32[]{:S(2)}, u32[]{:S(2)}) collective-permute-start(f32[4,192,128]{2,1,0:T(8,128)S(1)} %get-tuple-element.52), channel_id=1, source_target_pairs={{4,0},{8,4},{12,8},{16,12},{20,16},{24,20},{28,24},{32,28},{36,32}... | collective-permute-start | bytes 1179656 | tf_op jit(solution)/shard_map/ppermute | solution.py:16
  395.0 15.0 %collective-permute-start.33 = (f32[4,192,128]{2,1,0:T(8,128)S(1)}, f32[4,192,128]{2,1,0:T(8,128)S(1)}, u32[]{:S(2)}, u32[]{:S(2)}) collective-permute-start(f32[4,192,128]{2,1,0:T(8,128)S(1)} %get-tuple-element.51), channel_id=1, source_target_pairs={{0,4},{4,8},{8,12},{12,16},{16,20},{20,24},{24,28},{28,32},{32,36}... | collective-permute-start | bytes 1179656 | tf_op jit(solution)/shard_map/ppermute | solution.py:15
  410.4 11.9 %collective-permute-start.34 = (f32[4,192,128]{2,1,0:T(8,128)S(1)}, f32[4,192,128]{2,1,0:T(8,128)S(1)}, u32[]{:S(2)}, u32[]{:S(2)}) collective-permute-start(f32[4,192,128]{2,1,0:T(8,128)S(1)} %get-tuple-element.48), channel_id=1, source_target_pairs={{4,0},{8,4},{12,8},{16,12},{20,16},{24,20},{28,24},{32,28},{36,32}... | collective-permute-start | bytes 1179656 | tf_op jit(solution)/shard_map/ppermute | solution.py:16
  412.4 19.0 %collective-permute-start.35 = (f32[4,192,128]{2,1,0:T(8,128)S(1)}, f32[4,192,128]{2,1,0:T(8,128)S(1)}, u32[]{:S(2)}, u32[]{:S(2)}) collective-permute-start(f32[4,192,128]{2,1,0:T(8,128)S(1)} %get-tuple-element.47), channel_id=1, source_target_pairs={{0,4},{4,8},{8,12},{12,16},{16,20},{20,24},{24,28},{28,32},{32,36}... | collective-permute-start | bytes 1179656 | tf_op jit(solution)/shard_map/ppermute | solution.py:15
  431.8 15.0 %collective-permute-start.36 = (f32[4,192,128]{2,1,0:T(8,128)S(1)}, f32[4,192,128]{2,1,0:T(8,128)S(1)}, u32[]{:S(2)}, u32[]{:S(2)}) collective-permute-start(f32[4,192,128]{2,1,0:T(8,128)S(1)} %get-tuple-element.44), channel_id=1, source_target_pairs={{4,0},{8,4},{12,8},{16,12},{20,16},{24,20},{28,24},{32,28},{36,32}... | collective-permute-start | bytes 1179656 | tf_op jit(solution)/shard_map/ppermute | solution.py:16
  433.9 19.3 %collective-permute-start.37 = (f32[4,192,128]{2,1,0:T(8,128)S(1)}, f32[4,192,128]{2,1,0:T(8,128)S(1)}, u32[]{:S(2)}, u32[]{:S(2)}) collective-permute-start(f32[4,192,128]{2,1,0:T(8,128)S(1)} %get-tuple-element.43), channel_id=1, source_target_pairs={{0,4},{4,8},{8,12},{12,16},{16,20},{20,24},{24,28},{28,32},{32,36}... | collective-permute-start | bytes 1179656 | tf_op jit(solution)/shard_map/ppermute | solution.py:15
  453.5 15.0 %collective-permute-start.38 = (f32[4,192,128]{2,1,0:T(8,128)S(1)}, f32[4,192,128]{2,1,0:T(8,128)S(1)}, u32[]{:S(2)}, u32[]{:S(2)}) collective-permute-start(f32[4,192,128]{2,1,0:T(8,128)S(1)} %get-tuple-element.40), channel_id=1, source_target_pairs={{4,0},{8,4},{12,8},{16,12},{20,16},{24,20},{28,24},{32,28},{36,32}... | collective-permute-start | bytes 1179656 | tf_op jit(solution)/shard_map/ppermute | solution.py:16
  455.6 19.5 %collective-permute-start.39 = (f32[4,192,128]{2,1,0:T(8,128)S(1)}, f32[4,192,128]{2,1,0:T(8,128)S(1)}, u32[]{:S(2)}, u32[]{:S(2)}) collective-permute-start(f32[4,192,128]{2,1,0:T(8,128)S(1)} %get-tuple-element.39), channel_id=1, source_target_pairs={{0,4},{4,8},{8,12},{12,16},{16,20},{20,24},{24,28},{28,32},{32,36}... | collective-permute-start | bytes 1179656 | tf_op jit(solution)/shard_map/ppermute | solution.py:15
  463.3 12.0 %copy-start.13 = (f32[8,192,128]{2,1,0:T(8,128)S(1)}, f32[8,192,128]{2,1,0:T(8,128)}, u32[]{:S(2)}) copy-start(f32[8,192,128]{2,1,0:T(8,128)} %get-tuple-element.19) | copy-start | bytes 2359300
  475.6 3.6 collective-permute-start.40
  479.3 10.3 %collective-permute-start.41 = (f32[8,48,128]{2,1,0:T(8,128)S(1)}, f32[8,48,128]{2,1,0:T(8,128)S(1)}, u32[]{:S(2)}, u32[]{:S(2)}) collective-permute-start(f32[8,48,128]{2,1,0:T(8,128)S(1)} %dynamic-slice_bitcast_fusion), channel_id=1, source_target_pairs={{0,2},{1,3},{2,0},{3,1},{4,6},{5,7},{6,4},{7,5},{8,10},{9,11},{10,... | collective-permute-start | bytes 589832 | tf_op jit(solution)/shard_map/ppermute | solution.py:141
  (45 other events, 199.1 us)

commit v3 on v2

--- a/solution.py
+++ b/solution.py
@@ -108,7 +108,8 @@
     accelerations = []
     traces = []
     for t in range(steps):
-        injected = place_cells(velocity.shape, source_index, jnp.where(inside, pulses[t], 0.0))
+        amounts, _ = lax.optimization_barrier((jnp.where(inside, pulses[t], 0.0), current))
+        injected = place_cells(velocity.shape, source_index, amounts)
         latest = step(current, former, courant_sq, injected)
         accelerations.append(lax.optimization_barrier(latest - 2.0 * current + former))
         traces.append(sample_cells(latest, receiver_cells))
@@ -122,7 +123,8 @@
     following, furthest = adjoint_now[0], adjoint_prev[0]
     imaging = jnp.zeros_like(velocity)
     for t in reversed(range(steps)):
-        injected = place_cells(velocity.shape, receiver_cells, misfit[t])
+        amounts, _ = lax.optimization_barrier((misfit[t], following))
+        injected = place_cells(velocity.shape, receiver_cells, amounts)
         earlier = step(following, furthest, courant_sq, injected)
         imaging = lax.optimization_barrier(imaging + earlier * accelerations[t])
         following, furthest = earlier, following

time: 500 us -> 513 us (1.026)
  the two profiles are of different devices: /device:TPU:454 before, /device:TPU:366 now
where the time goes in v3:
time: 513 us; the launch traced here: 504 us
  waiting for transfers between devices  226 us (44%)
  starting transfers between devices  141 us (27%)
  other arithmetic  76.6 us (15%)
  local copies, waits for them, and re-layouts  32.7 us (6%)
  matrix products  24.9 us (5%)
    ppermute x20, waiting for transfers between devices, exchange_edges(): low = lax.ppermute(block[block.shape[0] - RADIUS:], 'space', forward)  120 us
    ppermute x20, waiting for transfers between devices, exchange_edges(): high = lax.ppermute(block[:RADIUS], 'space', backward)  97.2 us
    ppermute x20, starting transfers between devices, exchange_edges(): low = lax.ppermute(block[block.shape[0] - RADIUS:], 'space', forward)  92.2 us
    ppermute x20, starting transfers between devices, exchange_edges(): high = lax.ppermute(block[:RADIUS], 'space', backward)  43.9 us
    add x10, other arithmetic, per_device(): latest - 2.0 * current + former  31.8 us
    add x11, other arithmetic, step(): 2.0 * current - former + courant_sq * inner_laplace(current) + injected  31.4 us
    dot_general x20, matrix products, place_cells(): placed = jnp.dot(by_row, by_lane, precision=lax.Precision.HIGHEST)  24.9 us
    gather x10, local copies, waits for them, and re-layouts, sample_cells(): rows = field.reshape(-1, lanes)[cells // lanes]  16.7 us
  transfers between devices with their start and end apart: 42, of which 39 were waited for; matrix products, arithmetic and copies ran while one was open for 20% of the time, Pallas kernels for 0%

profile of v3, /device:TPU:366, one launch (start us, length us, event | category | flops | bytes accessed | tf_op | source)
XLA Modules:
  0.0 504.2 jit_solution(15510489018245364296)
XLA Ops:
  12.0 4.8 collective-permute-start.21
  39.3 11.5 %collective-permute-done.2 = f32[4,192,128]{2,1,0:T(8,128)S(1)} collective-permute-done((f32[4,192,128]{2,1,0:T(8,128)}, f32[4,192,128]{2,1,0:T(8,128)S(1)}, u32[]{:S(2)}, u32[]{:S(2)}) %collective-permute-start.2) | collective-permute-done | bytes 393248 | tf_op jit(solution)/shard_map/ppermute | solution.py:16
  51.6 9.8 %collective-permute-done.3 = f32[4,192,128]{2,1,0:T(8,128)} collective-permute-done((f32[4,192,128]{2,1,0:T(8,128)S(1)}, f32[4,192,128]{2,1,0:T(8,128)}, u32[]{:S(2)}, u32[]{:S(2)}) %collective-permute-start.3) | collective-permute-done | bytes 393248 | tf_op jit(solution)/shard_map/ppermute | solution.py:15
  69.1 4.5 collective-permute-start.5
  77.1 4.6 collective-permute-done.4
  81.7 6.9 %collective-permute-done.5 = f32[4,192,128]{2,1,0:T(8,128)S(1)} collective-permute-done((f32[4,192,128]{2,1,0:T(8,128)S(1)}, f32[4,192,128]{2,1,0:T(8,128)S(1)}, u32[]{:S(2)}, u32[]{:S(2)}) %collective-permute-start.5) | collective-permute-done | bytes 393248 | tf_op jit(solution)/shard_map/ppermute | solution.py:15
  94.8 4.7 collective-permute-start.7
  107.4 5.6 %collective-permute-done.7 = f32[4,192,128]{2,1,0:T(8,128)S(1)} collective-permute-done((f32[4,192,128]{2,1,0:T(8,128)S(1)}, f32[4,192,128]{2,1,0:T(8,128)S(1)}, u32[]{:S(2)}, u32[]{:S(2)}) %collective-permute-start.7) | collective-permute-done | bytes 393248 | tf_op jit(solution)/shard_map/ppermute | solution.py:15
  119.2 4.5 collective-permute-start.9
  127.2 4.6 collective-permute-done.8
  131.8 4.5 collective-permute-done.9
  142.5 4.7 collective-permute-start.11
  150.7 4.6 collective-permute-done.10
  155.3 7.8 %collective-permute-done.11 = f32[4,192,128]{2,1,0:T(8,128)S(1)} collective-permute-done((f32[4,192,128]{2,1,0:T(8,128)S(1)}, f32[4,192,128]{2,1,0:T(8,128)S(1)}, u32[]{:S(2)}, u32[]{:S(2)}) %collective-permute-start.11) | collective-permute-done | bytes 393248 | tf_op jit(solution)/shard_map/ppermute | solution.py:15
  176.8 4.8 collective-permute-done.12
  181.6 7.3 %collective-permute-done.13 = f32[4,192,128]{2,1,0:T(8,128)S(1)} collective-permute-done((f32[4,192,128]{2,1,0:T(8,128)}, f32[4,192,128]{2,1,0:T(8,128)S(1)}, u32[]{:S(2)}, u32[]{:S(2)}) %collective-permute-start.13) | collective-permute-done | bytes 393248 | tf_op jit(solution)/shard_map/ppermute | solution.py:15
  195.0 4.9 collective-permute-start.15
  207.7 5.7 %collective-permute-done.15 = f32[4,192,128]{2,1,0:T(8,128)S(1)} collective-permute-done((f32[4,192,128]{2,1,0:T(8,128)S(1)}, f32[4,192,128]{2,1,0:T(8,128)S(1)}, u32[]{:S(2)}, u32[]{:S(2)}) %collective-permute-start.15) | collective-permute-done | bytes 393248 | tf_op jit(solution)/shard_map/ppermute | solution.py:15
  227.5 4.6 collective-permute-done.16
  232.1 4.5 collective-permute-done.17
  242.6 4.8 collective-permute-start.19
  255.5 7.6 %collective-permute-done.19 = f32[4,192,128]{2,1,0:T(8,128)S(1)} collective-permute-done((f32[4,192,128]{2,1,0:T(8,128)S(1)}, f32[4,192,128]{2,1,0:T(8,128)S(1)}, u32[]{:S(2)}, u32[]{:S(2)}) %collective-permute-start.19) | collective-permute-done | bytes 393248 | tf_op jit(solution)/shard_map/ppermute | solution.py:15
  281.0 4.7 collective-permute-start.23
  285.9 7.8 %collective-permute-done.22 = f32[4,192,128]{2,1,0:T(8,128)S(1)} collective-permute-done((f32[4,192,128]{2,1,0:T(8,128)S(1)}, f32[4,192,128]{2,1,0:T(8,128)S(1)}, u32[]{:S(2)}, u32[]{:S(2)}) %collective-permute-start.22) | collective-permute-done | bytes 393248 | tf_op jit(solution)/shard_map/ppermute | solution.py:16
  293.7 7.4 %collective-permute-done.23 = f32[4,192,128]{2,1,0:T(8,128)S(1)} collective-permute-done((f32[4,192,128]{2,1,0:T(8,128)S(1)}, f32[4,192,128]{2,1,0:T(8,128)S(1)}, u32[]{:S(2)}, u32[]{:S(2)}) %collective-permute-start.23) | collective-permute-done | bytes 393248 | tf_op jit(solution)/shard_map/ppermute | solution.py:15
  312.9 5.3 %collective-permute-done.24 = f32[4,192,128]{2,1,0:T(8,128)S(1)} collective-permute-done((f32[4,192,128]{2,1,0:T(8,128)S(1)}, f32[4,192,128]{2,1,0:T(8,128)S(1)}, u32[]{:S(2)}, u32[]{:S(2)}) %collective-permute-start.24) | collective-permute-done | bytes 393248 | tf_op jit(solution)/shard_map/ppermute | solution.py:16
  318.2 5.7 %collective-permute-done.25 = f32[4,192,128]{2,1,0:T(8,128)S(1)} collective-permute-done((f32[4,192,128]{2,1,0:T(8,128)S(1)}, f32[4,192,128]{2,1,0:T(8,128)S(1)}, u32[]{:S(2)}, u32[]{:S(2)}) %collective-permute-start.25) | collective-permute-done | bytes 393248 | tf_op jit(solution)/shard_map/ppermute | solution.py:15
  328.3 4.5 collective-permute-start.27
  335.7 5.3 %collective-permute-done.26 = f32[4,192,128]{2,1,0:T(8,128)S(1)} collective-permute-done((f32[4,192,128]{2,1,0:T(8,128)S(1)}, f32[4,192,128]{2,1,0:T(8,128)S(1)}, u32[]{:S(2)}, u32[]{:S(2)}) %collective-permute-start.26) | collective-permute-done | bytes 393248 | tf_op jit(solution)/shard_map/ppermute | solution.py:16
  340.9 4.5 collective-permute-done.27
  349.7 5.0 collective-permute-start.29
  357.5 5.1 %collective-permute-done.28 = f32[4,192,128]{2,1,0:T(8,128)S(1)} collective-permute-done((f32[4,192,128]{2,1,0:T(8,128)S(1)}, f32[4,192,128]{2,1,0:T(8,128)S(1)}, u32[]{:S(2)}, u32[]{:S(2)}) %collective-permute-start.28) | collective-permute-done | bytes 393248 | tf_op jit(solution)/shard_map/ppermute | solution.py:16
  362.6 7.4 %collective-permute-done.29 = f32[4,192,128]{2,1,0:T(8,128)S(1)} collective-permute-done((f32[4,192,128]{2,1,0:T(8,128)S(1)}, f32[4,192,128]{2,1,0:T(8,128)S(1)}, u32[]{:S(2)}, u32[]{:S(2)}) %collective-permute-start.29) | collective-permute-done | bytes 393248 | tf_op jit(solution)/shard_map/ppermute | solution.py:15
  374.4 4.5 collective-permute-start.31
  381.8 5.3 %collective-permute-done.30 = f32[4,192,128]{2,1,0:T(8,128)S(1)} collective-permute-done((f32[4,192,128]{2,1,0:T(8,128)S(1)}, f32[4,192,128]{2,1,0:T(8,128)S(1)}, u32[]{:S(2)}, u32[]{:S(2)}) %collective-permute-start.30) | collective-permute-done | bytes 393248 | tf_op jit(solution)/shard_map/ppermute | solution.py:16
  387.1 7.7 %collective-permute-done.31 = f32[4,192,128]{2,1,0:T(8,128)S(1)} collective-permute-done((f32[4,192,128]{2,1,0:T(8,128)S(1)}, f32[4,192,128]{2,1,0:T(8,128)S(1)}, u32[]{:S(2)}, u32[]{:S(2)}) %collective-permute-start.31) | collective-permute-done | bytes 393248 | tf_op jit(solution)/shard_map/ppermute | solution.py:15
  399.2 4.5 collective-permute-start.33
  406.6 5.3 %collective-permute-done.32 = f32[4,192,128]{2,1,0:T(8,128)S(1)} collective-permute-done((f32[4,192,128]{2,1,0:T(8,128)S(1)}, f32[4,192,128]{2,1,0:T(8,128)S(1)}, u32[]{:S(2)}, u32[]{:S(2)}) %collective-permute-start.32) | collective-permute-done | bytes 393248 | tf_op jit(solution)/shard_map/ppermute | solution.py:16
  411.8 5.7 %collective-permute-done.33 = f32[4,192,128]{2,1,0:T(8,128)S(1)} collective-permute-done((f32[4,192,128]{2,1,0:T(8,128)S(1)}, f32[4,192,128]{2,1,0:T(8,128)S(1)}, u32[]{:S(2)}, u32[]{:S(2)}) %collective-permute-start.33) | collective-permute-done | bytes 393248 | tf_op jit(solution)/shard_map/ppermute | solution.py:15
  422.0 4.8 collective-permute-start.35
  429.6 5.0 collective-permute-done.34
  434.7 4.5 collective-permute-done.35
  443.4 4.8 collective-permute-start.37
  451.0 5.3 %collective-permute-done.36 = f32[4,192,128]{2,1,0:T(8,128)S(1)} collective-permute-done((f32[4,192,128]{2,1,0:T(8,128)S(1)}, f32[4,192,128]{2,1,0:T(8,128)S(1)}, u32[]{:S(2)}, u32[]{:S(2)}) %collective-permute-start.36) | collective-permute-done | bytes 393248 | tf_op jit(solution)/shard_map/ppermute | solution.py:16
  456.3 7.3 %collective-permute-done.37 = f32[4,192,128]{2,1,0:T(8,128)S(1)} collective-permute-done((f32[4,192,128]{2,1,0:T(8,128)S(1)}, f32[4,192,128]{2,1,0:T(8,128)S(1)}, u32[]{:S(2)}, u32[]{:S(2)}) %collective-permute-start.37) | collective-permute-done | bytes 393248 | tf_op jit(solution)/shard_map/ppermute | solution.py:15
  475.7 5.1 %collective-permute-done.38 = f32[4,192,128]{2,1,0:T(8,128)S(1)} collective-permute-done((f32[4,192,128]{2,1,0:T(8,128)S(1)}, f32[4,192,128]{2,1,0:T(8,128)S(1)}, u32[]{:S(2)}, u32[]{:S(2)}) %collective-permute-start.38) | collective-permute-done | bytes 393248 | tf_op jit(solution)/shard_map/ppermute | solution.py:16
  480.8 7.7 %collective-permute-done.39 = f32[4,192,128]{2,1,0:T(8,128)S(1)} collective-permute-done((f32[4,192,128]{2,1,0:T(8,128)S(1)}, f32[4,192,128]{2,1,0:T(8,128)S(1)}, u32[]{:S(2)}, u32[]{:S(2)}) %collective-permute-start.39) | collective-permute-done | bytes 393248 | tf_op jit(solution)/shard_map/ppermute | solution.py:15
  496.0 7.0 %collective-permute-done.41 = f32[8,48,128]{2,1,0:T(8,128)S(1)} collective-permute-done((f32[8,48,128]{2,1,0:T(8,128)S(1)}, f32[8,48,128]{2,1,0:T(8,128)S(1)}, u32[]{:S(2)}, u32[]{:S(2)}) %collective-permute-start.41) | collective-permute-done | bytes 196640 | tf_op jit(solution)/shard_map/ppermute | solution.py:143
  (228 shorter events, 226.9 us)
Async XLA Ops:
  2.1 19.9 %collective-permute-start = (f32[4,192,128]{2,1,0:T(8,128)}, f32[4,192,128]{2,1,0:T(8,128)}, u32[]{:S(2)}, u32[]{:S(2)}) collective-permute-start(f32[4,192,128]{2,1,0:T(8,128)} %get-tuple-element.134), channel_id=1, source_target_pairs={{4,0},{8,4},{12,8},{16,12},{20,16},{24,20},{28,24},{32,28},{36,32}... | collective-permute-start | bytes 1179656 | tf_op jit(solution)/shard_map/ppermute | solution.py:16
  4.9 12.0 %copy-start.36 = (s32[1,128]{1,0:T(1,128)S(1)}, s32[1,128]{1,0:T(1,128)}, u32[]{:S(2)}) copy-start(s32[1,128]{1,0:T(1,128)} %param.15) | copy-start | bytes 1540
  4.9 12.0 %copy-start.35 = (f32[1,10,128]{2,0,1:T(1,128)S(1)}, f32[1,10,128]{2,0,1:T(1,128)}, u32[]{:S(2)}) copy-start(f32[1,10,128]{2,0,1:T(1,128)} %param.16) | copy-start | bytes 15364
  4.9 19.8 %collective-permute-start.1 = (f32[4,192,128]{2,1,0:T(8,128)}, f32[4,192,128]{2,1,0:T(8,128)}, u32[]{:S(2)}, u32[]{:S(2)}) collective-permute-start(f32[4,192,128]{2,1,0:T(8,128)} %get-tuple-element.133), channel_id=1, source_target_pairs={{0,4},{4,8},{8,12},{12,16},{16,20},{20,24},{24,28},{28,32},{32,36}... | collective-permute-start | bytes 1179656 | tf_op jit(solution)/shard_map/ppermute | solution.py:15
  9.9 262.3 %collective-permute-start.20 = (f32[4,192,128]{2,1,0:T(8,128)}, f32[4,192,128]{2,1,0:T(8,128)}, u32[]{:S(2)}, u32[]{:S(2)}) collective-permute-start(f32[4,192,128]{2,1,0:T(8,128)} %get-tuple-element.114), channel_id=1, source_target_pairs={{4,0},{8,4},{12,8},{16,12},{20,16},{24,20},{28,24},{32,28},{36,32}... | collective-permute-start | bytes 1179656 | tf_op jit(solution)/shard_map/ppermute | solution.py:16
  12.0 260.2 %collective-permute-start.21 = (f32[4,192,128]{2,1,0:T(8,128)}, f32[4,192,128]{2,1,0:T(8,128)}, u32[]{:S(2)}, u32[]{:S(2)}) collective-permute-start(f32[4,192,128]{2,1,0:T(8,128)} %get-tuple-element.113), channel_id=1, source_target_pairs={{0,4},{4,8},{8,12},{12,16},{16,20},{20,24},{24,28},{28,32},{32,36}... | collective-permute-start | bytes 1179656 | tf_op jit(solution)/shard_map/ppermute | solution.py:15
  22.0 42.3 %copy-start.32 = (s32[1024]{0:T(1024)}, s32[1024]{0:T(1024)S(1)}, u32[]{:S(2)}) copy-start(s32[1024]{0:T(1024)S(1)} %pad_clamp_fusion) | copy-start | bytes 12292
  27.8 23.0 %collective-permute-start.2 = (f32[4,192,128]{2,1,0:T(8,128)}, f32[4,192,128]{2,1,0:T(8,128)S(1)}, u32[]{:S(2)}, u32[]{:S(2)}) collective-permute-start(f32[4,192,128]{2,1,0:T(8,128)} %get-tuple-element.132), channel_id=1, source_target_pairs={{4,0},{8,4},{12,8},{16,12},{20,16},{24,20},{28,24},{32,28},{36,32}... | collective-permute-start | bytes 1179656 | tf_op jit(solution)/shard_map/ppermute | solution.py:16
  30.6 30.8 %collective-permute-start.3 = (f32[4,192,128]{2,1,0:T(8,128)S(1)}, f32[4,192,128]{2,1,0:T(8,128)}, u32[]{:S(2)}, u32[]{:S(2)}) collective-permute-start(f32[4,192,128]{2,1,0:T(8,128)S(1)} %get-tuple-element.131), channel_id=1, source_target_pairs={{0,4},{4,8},{8,12},{12,16},{16,20},{20,24},{24,28},{28,32},{32,36}... | collective-permute-start | bytes 1179656 | tf_op jit(solution)/shard_map/ppermute | solution.py:15
  66.9 14.8 %collective-permute-start.4 = (f32[4,192,128]{2,1,0:T(8,128)S(1)}, f32[4,192,128]{2,1,0:T(8,128)S(1)}, u32[]{:S(2)}, u32[]{:S(2)}) collective-permute-start(f32[4,192,128]{2,1,0:T(8,128)S(1)} %copy-done.31), channel_id=1, source_target_pairs={{4,0},{8,4},{12,8},{16,12},{20,16},{24,20},{28,24},{32,28},{36,32}... | collective-permute-start | bytes 1179656 | tf_op jit(solution)/shard_map/ppermute | solution.py:16
  69.1 19.6 %collective-permute-start.5 = (f32[4,192,128]{2,1,0:T(8,128)S(1)}, f32[4,192,128]{2,1,0:T(8,128)S(1)}, u32[]{:S(2)}, u32[]{:S(2)}) collective-permute-start(f32[4,192,128]{2,1,0:T(8,128)S(1)} %copy-done.25), channel_id=1, source_target_pairs={{0,4},{4,8},{8,12},{12,16},{16,20},{20,24},{24,28},{28,32},{32,36}... | collective-permute-start | bytes 1179656 | tf_op jit(solution)/shard_map/ppermute | solution.py:15
  92.6 14.8 %collective-permute-start.6 = (f32[4,192,128]{2,1,0:T(8,128)S(1)}, f32[4,192,128]{2,1,0:T(8,128)S(1)}, u32[]{:S(2)}, u32[]{:S(2)}) collective-permute-start(f32[4,192,128]{2,1,0:T(8,128)S(1)} %copy-done.27), channel_id=1, source_target_pairs={{4,0},{8,4},{12,8},{16,12},{20,16},{24,20},{28,24},{32,28},{36,32}... | collective-permute-start | bytes 1179656 | tf_op jit(solution)/shard_map/ppermute | solution.py:16
  94.8 18.3 %collective-permute-start.7 = (f32[4,192,128]{2,1,0:T(8,128)S(1)}, f32[4,192,128]{2,1,0:T(8,128)S(1)}, u32[]{:S(2)}, u32[]{:S(2)}) collective-permute-start(f32[4,192,128]{2,1,0:T(8,128)S(1)} %copy-done.20), channel_id=1, source_target_pairs={{0,4},{4,8},{8,12},{12,16},{16,20},{20,24},{24,28},{28,32},{32,36}... | collective-permute-start | bytes 1179656 | tf_op jit(solution)/shard_map/ppermute | solution.py:15
  117.0 14.8 %collective-permute-start.8 = (f32[4,192,128]{2,1,0:T(8,128)S(1)}, f32[4,192,128]{2,1,0:T(8,128)S(1)}, u32[]{:S(2)}, u32[]{:S(2)}) collective-permute-start(f32[4,192,128]{2,1,0:T(8,128)S(1)} %copy-done.28), channel_id=1, source_target_pairs={{4,0},{8,4},{12,8},{16,12},{20,16},{24,20},{28,24},{32,28},{36,32}... | collective-permute-start | bytes 1179656 | tf_op jit(solution)/shard_map/ppermute | solution.py:16
  119.2 17.2 %collective-permute-start.9 = (f32[4,192,128]{2,1,0:T(8,128)S(1)}, f32[4,192,128]{2,1,0:T(8,128)S(1)}, u32[]{:S(2)}, u32[]{:S(2)}) collective-permute-start(f32[4,192,128]{2,1,0:T(8,128)S(1)} %copy-done.21), channel_id=1, source_target_pairs={{0,4},{4,8},{8,12},{12,16},{16,20},{20,24},{24,28},{28,32},{32,36}... | collective-permute-start | bytes 1179656 | tf_op jit(solution)/shard_map/ppermute | solution.py:15
  136.6 10.6 %copy-start.1 = (f32[8,192,128]{2,1,0:T(8,128)}, f32[8,192,128]{2,1,0:T(8,128)S(1)}, u32[]{:S(2)}) copy-start(f32[8,192,128]{2,1,0:T(8,128)S(1)} %fusion.108) | copy-start | bytes 2359300
  140.4 14.8 %collective-permute-start.10 = (f32[4,192,128]{2,1,0:T(8,128)S(1)}, f32[4,192,128]{2,1,0:T(8,128)S(1)}, u32[]{:S(2)}, u32[]{:S(2)}) collective-permute-start(f32[4,192,128]{2,1,0:T(8,128)S(1)} %copy-done.29), channel_id=1, source_target_pairs={{4,0},{8,4},{12,8},{16,12},{20,16},{24,20},{28,24},{32,28},{36,32}... | collective-permute-start | bytes 1179656 | tf_op jit(solution)/shard_map/ppermute | solution.py:16
  142.5 20.5 %collective-permute-start.11 = (f32[4,192,128]{2,1,0:T(8,128)S(1)}, f32[4,192,128]{2,1,0:T(8,128)S(1)}, u32[]{:S(2)}, u32[]{:S(2)}) collective-permute-start(f32[4,192,128]{2,1,0:T(8,128)S(1)} %copy-done.22), channel_id=1, source_target_pairs={{0,4},{4,8},{8,12},{12,16},{16,20},{20,24},{24,28},{28,32},{32,36}... | collective-permute-start | bytes 1179656 | tf_op jit(solution)/shard_map/ppermute | solution.py:15
  166.6 15.1 %collective-permute-start.12 = (f32[4,192,128]{2,1,0:T(8,128)}, f32[4,192,128]{2,1,0:T(8,128)S(1)}, u32[]{:S(2)}, u32[]{:S(2)}) collective-permute-start(f32[4,192,128]{2,1,0:T(8,128)} %get-tuple-element.122), channel_id=1, source_target_pairs={{4,0},{8,4},{12,8},{16,12},{20,16},{24,20},{28,24},{32,28},{36,32}... | collective-permute-start | bytes 1179656 | tf_op jit(solution)/shard_map/ppermute | solution.py:16
  168.8 20.1 %collective-permute-start.13 = (f32[4,192,128]{2,1,0:T(8,128)}, f32[4,192,128]{2,1,0:T(8,128)S(1)}, u32[]{:S(2)}, u32[]{:S(2)}) collective-permute-start(f32[4,192,128]{2,1,0:T(8,128)} %get-tuple-element.121), channel_id=1, source_target_pairs={{0,4},{4,8},{8,12},{12,16},{16,20},{20,24},{24,28},{28,32},{32,36}... | collective-permute-start | bytes 1179656 | tf_op jit(solution)/shard_map/ppermute | solution.py:15
  192.8 14.8 %collective-permute-start.14 = (f32[4,192,128]{2,1,0:T(8,128)S(1)}, f32[4,192,128]{2,1,0:T(8,128)S(1)}, u32[]{:S(2)}, u32[]{:S(2)}) collective-permute-start(f32[4,192,128]{2,1,0:T(8,128)S(1)} %copy-done.30), channel_id=1, source_target_pairs={{4,0},{8,4},{12,8},{16,12},{20,16},{24,20},{28,24},{32,28},{36,32}... | collective-permute-start | bytes 1179656 | tf_op jit(solution)/shard_map/ppermute | solution.py:16
  195.0 18.3 %collective-permute-start.15 = (f32[4,192,128]{2,1,0:T(8,128)S(1)}, f32[4,192,128]{2,1,0:T(8,128)S(1)}, u32[]{:S(2)}, u32[]{:S(2)}) collective-permute-start(f32[4,192,128]{2,1,0:T(8,128)S(1)} %copy-done.23), channel_id=1, source_target_pairs={{0,4},{4,8},{8,12},{12,16},{16,20},{20,24},{24,28},{28,32},{32,36}... | collective-permute-start | bytes 1179656 | tf_op jit(solution)/shard_map/ppermute | solution.py:15
  217.3 14.8 %collective-permute-start.16 = (f32[4,192,128]{2,1,0:T(8,128)S(1)}, f32[4,192,128]{2,1,0:T(8,128)S(1)}, u32[]{:S(2)}, u32[]{:S(2)}) collective-permute-start(f32[4,192,128]{2,1,0:T(8,128)S(1)} %copy-done.26), channel_id=1, source_target_pairs={{4,0},{8,4},{12,8},{16,12},{20,16},{24,20},{28,24},{32,28},{36,32}... | collective-permute-start | bytes 1179656 | tf_op jit(solution)/shard_map/ppermute | solution.py:16
  219.5 17.2 %collective-permute-start.17 = (f32[4,192,128]{2,1,0:T(8,128)S(1)}, f32[4,192,128]{2,1,0:T(8,128)S(1)}, u32[]{:S(2)}, u32[]{:S(2)}) collective-permute-start(f32[4,192,128]{2,1,0:T(8,128)S(1)} %copy-done.19), channel_id=1, source_target_pairs={{0,4},{4,8},{8,12},{12,16},{16,20},{20,24},{24,28},{28,32},{32,36}... | collective-permute-start | bytes 1179656 | tf_op jit(solution)/shard_map/ppermute | solution.py:15
  240.6 14.8 %collective-permute-start.18 = (f32[4,192,128]{2,1,0:T(8,128)S(1)}, f32[4,192,128]{2,1,0:T(8,128)S(1)}, u32[]{:S(2)}, u32[]{:S(2)}) collective-permute-start(f32[4,192,128]{2,1,0:T(8,128)S(1)} %copy-done.24), channel_id=1, source_target_pairs={{4,0},{8,4},{12,8},{16,12},{20,16},{24,20},{28,24},{32,28},{36,32}... | collective-permute-start | bytes 1179656 | tf_op jit(solution)/shard_map/ppermute | solution.py:16
  242.6 20.5 %collective-permute-start.19 = (f32[4,192,128]{2,1,0:T(8,128)S(1)}, f32[4,192,128]{2,1,0:T(8,128)S(1)}, u32[]{:S(2)}, u32[]{:S(2)}) collective-permute-start(f32[4,192,128]{2,1,0:T(8,128)S(1)} %copy-done.18), channel_id=1, source_target_pairs={{0,4},{4,8},{8,12},{12,16},{16,20},{20,24},{24,28},{28,32},{32,36}... | collective-permute-start | bytes 1179656 | tf_op jit(solution)/shard_map/ppermute | solution.py:15
  250.9 12.4 %copy-start.33 = (s32[1024]{0:T(1024)S(1)}, s32[1024]{0:T(1024)}, u32[]{:S(2)}) copy-start(s32[1024]{0:T(1024)} %copy-done.32) | copy-start | bytes 12292
  278.8 14.8 %collective-permute-start.22 = (f32[4,192,128]{2,1,0:T(8,128)S(1)}, f32[4,192,128]{2,1,0:T(8,128)S(1)}, u32[]{:S(2)}, u32[]{:S(2)}) collective-permute-start(f32[4,192,128]{2,1,0:T(8,128)S(1)} %get-tuple-element.112), channel_id=1, source_target_pairs={{4,0},{8,4},{12,8},{16,12},{20,16},{24,20},{28,24},{32,28},{36,32}... | collective-permute-start | bytes 1179656 | tf_op jit(solution)/shard_map/ppermute | solution.py:16
  281.0 20.0 %collective-permute-start.23 = (f32[4,192,128]{2,1,0:T(8,128)S(1)}, f32[4,192,128]{2,1,0:T(8,128)S(1)}, u32[]{:S(2)}, u32[]{:S(2)}) collective-permute-start(f32[4,192,128]{2,1,0:T(8,128)S(1)} %get-tuple-element.111), channel_id=1, source_target_pairs={{0,4},{4,8},{8,12},{12,16},{16,20},{20,24},{24,28},{28,32},{32,36}... | collective-permute-start | bytes 1179656 | tf_op jit(solution)/shard_map/ppermute | solution.py:15
  303.3 14.8 %collective-permute-start.24 = (f32[4,192,128]{2,1,0:T(8,128)S(1)}, f32[4,192,128]{2,1,0:T(8,128)S(1)}, u32[]{:S(2)}, u32[]{:S(2)}) collective-permute-start(f32[4,192,128]{2,1,0:T(8,128)S(1)} %get-tuple-element.108), channel_id=1, source_target_pairs={{4,0},{8,4},{12,8},{16,12},{20,16},{24,20},{28,24},{32,28},{36,32}... | collective-permute-start | bytes 1179656 | tf_op jit(solution)/shard_map/ppermute | solution.py:16
  305.5 18.3 %collective-permute-start.25 = (f32[4,192,128]{2,1,0:T(8,128)S(1)}, f32[4,192,128]{2,1,0:T(8,128)S(1)}, u32[]{:S(2)}, u32[]{:S(2)}) collective-permute-start(f32[4,192,128]{2,1,0:T(8,128)S(1)} %get-tuple-element.107), channel_id=1, source_target_pairs={{0,4},{4,8},{8,12},{12,16},{16,20},{20,24},{24,28},{28,32},{32,36}... | collective-permute-start | bytes 1179656 | tf_op jit(solution)/shard_map/ppermute | solution.py:15
  326.1 14.8 %collective-permute-start.26 = (f32[4,192,128]{2,1,0:T(8,128)S(1)}, f32[4,192,128]{2,1,0:T(8,128)S(1)}, u32[]{:S(2)}, u32[]{:S(2)}) collective-permute-start(f32[4,192,128]{2,1,0:T(8,128)S(1)} %get-tuple-element.104), channel_id=1, source_target_pairs={{4,0},{8,4},{12,8},{16,12},{20,16},{24,20},{28,24},{32,28},{36,32}... | collective-permute-start | bytes 1179656 | tf_op jit(solution)/shard_map/ppermute | solution.py:16
  328.3 17.2 %collective-permute-start.27 = (f32[4,192,128]{2,1,0:T(8,128)S(1)}, f32[4,192,128]{2,1,0:T(8,128)S(1)}, u32[]{:S(2)}, u32[]{:S(2)}) collective-permute-start(f32[4,192,128]{2,1,0:T(8,128)S(1)} %get-tuple-element.103), channel_id=1, source_target_pairs={{0,4},{4,8},{8,12},{12,16},{16,20},{20,24},{24,28},{28,32},{32,36}... | collective-permute-start | bytes 1179656 | tf_op jit(solution)/shard_map/ppermute | solution.py:15
  347.7 14.8 %collective-permute-start.28 = (f32[4,192,128]{2,1,0:T(8,128)S(1)}, f32[4,192,128]{2,1,0:T(8,128)S(1)}, u32[]{:S(2)}, u32[]{:S(2)}) collective-permute-start(f32[4,192,128]{2,1,0:T(8,128)S(1)} %get-tuple-element.100), channel_id=1, source_target_pairs={{4,0},{8,4},{12,8},{16,12},{20,16},{24,20},{28,24},{32,28},{36,32}... | collective-permute-start | bytes 1179656 | tf_op jit(solution)/shard_map/ppermute | solution.py:16
  349.7 20.3 %collective-permute-start.29 = (f32[4,192,128]{2,1,0:T(8,128)S(1)}, f32[4,192,128]{2,1,0:T(8,128)S(1)}, u32[]{:S(2)}, u32[]{:S(2)}) collective-permute-start(f32[4,192,128]{2,1,0:T(8,128)S(1)} %get-tuple-element.99), channel_id=1, source_target_pairs={{0,4},{4,8},{8,12},{12,16},{16,20},{20,24},{24,28},{28,32},{32,36}... | collective-permute-start | bytes 1179656 | tf_op jit(solution)/shard_map/ppermute | solution.py:15
  372.2 14.8 %collective-permute-start.30 = (f32[4,192,128]{2,1,0:T(8,128)S(1)}, f32[4,192,128]{2,1,0:T(8,128)S(1)}, u32[]{:S(2)}, u32[]{:S(2)}) collective-permute-start(f32[4,192,128]{2,1,0:T(8,128)S(1)} %get-tuple-element.96), channel_id=1, source_target_pairs={{4,0},{8,4},{12,8},{16,12},{20,16},{24,20},{28,24},{32,28},{36,32}... | collective-permute-start | bytes 1179656 | tf_op jit(solution)/shard_map/ppermute | solution.py:16
  374.4 20.3 %collective-permute-start.31 = (f32[4,192,128]{2,1,0:T(8,128)S(1)}, f32[4,192,128]{2,1,0:T(8,128)S(1)}, u32[]{:S(2)}, u32[]{:S(2)}) collective-permute-start(f32[4,192,128]{2,1,0:T(8,128)S(1)} %get-tuple-element.95), channel_id=1, source_target_pairs={{0,4},{4,8},{8,12},{12,16},{16,20},{20,24},{24,28},{28,32},{32,36}... | collective-permute-start | bytes 1179656 | tf_op jit(solution)/shard_map/ppermute | solution.py:15
  397.0 14.8 %collective-permute-start.32 = (f32[4,192,128]{2,1,0:T(8,128)S(1)}, f32[4,192,128]{2,1,0:T(8,128)S(1)}, u32[]{:S(2)}, u32[]{:S(2)}) collective-permute-start(f32[4,192,128]{2,1,0:T(8,128)S(1)} %get-tuple-element.92), channel_id=1, source_target_pairs={{4,0},{8,4},{12,8},{16,12},{20,16},{24,20},{28,24},{32,28},{36,32}... | collective-permute-start | bytes 1179656 | tf_op jit(solution)/shard_map/ppermute | solution.py:16
  399.2 18.3 %collective-permute-start.33 = (f32[4,192,128]{2,1,0:T(8,128)S(1)}, f32[4,192,128]{2,1,0:T(8,128)S(1)}, u32[]{:S(2)}, u32[]{:S(2)}) collective-permute-start(f32[4,192,128]{2,1,0:T(8,128)S(1)} %get-tuple-element.91), channel_id=1, source_target_pairs={{0,4},{4,8},{8,12},{12,16},{16,20},{20,24},{24,28},{28,32},{32,36}... | collective-permute-start | bytes 1179656 | tf_op jit(solution)/shard_map/ppermute | solution.py:15
  419.8 14.8 %collective-permute-start.34 = (f32[4,192,128]{2,1,0:T(8,128)S(1)}, f32[4,192,128]{2,1,0:T(8,128)S(1)}, u32[]{:S(2)}, u32[]{:S(2)}) collective-permute-start(f32[4,192,128]{2,1,0:T(8,128)S(1)} %get-tuple-element.88), channel_id=1, source_target_pairs={{4,0},{8,4},{12,8},{16,12},{20,16},{24,20},{28,24},{32,28},{36,32}... | collective-permute-start | bytes 1179656 | tf_op jit(solution)/shard_map/ppermute | solution.py:16
  422.0 17.2 %collective-permute-start.35 = (f32[4,192,128]{2,1,0:T(8,128)S(1)}, f32[4,192,128]{2,1,0:T(8,128)S(1)}, u32[]{:S(2)}, u32[]{:S(2)}) collective-permute-start(f32[4,192,128]{2,1,0:T(8,128)S(1)} %get-tuple-element.87), channel_id=1, source_target_pairs={{0,4},{4,8},{8,12},{12,16},{16,20},{20,24},{24,28},{28,32},{32,36}... | collective-permute-start | bytes 1179656 | tf_op jit(solution)/shard_map/ppermute | solution.py:15
  441.5 14.8 %collective-permute-start.36 = (f32[4,192,128]{2,1,0:T(8,128)S(1)}, f32[4,192,128]{2,1,0:T(8,128)S(1)}, u32[]{:S(2)}, u32[]{:S(2)}) collective-permute-start(f32[4,192,128]{2,1,0:T(8,128)S(1)} %get-tuple-element.84), channel_id=1, source_target_pairs={{4,0},{8,4},{12,8},{16,12},{20,16},{24,20},{28,24},{32,28},{36,32}... | collective-permute-start | bytes 1179656 | tf_op jit(solution)/shard_map/ppermute | solution.py:16
  443.4 20.3 %collective-permute-start.37 = (f32[4,192,128]{2,1,0:T(8,128)S(1)}, f32[4,192,128]{2,1,0:T(8,128)S(1)}, u32[]{:S(2)}, u32[]{:S(2)}) collective-permute-start(f32[4,192,128]{2,1,0:T(8,128)S(1)} %get-tuple-element.83), channel_id=1, source_target_pairs={{0,4},{4,8},{8,12},{12,16},{16,20},{20,24},{24,28},{28,32},{32,36}... | collective-permute-start | bytes 1179656 | tf_op jit(solution)/shard_map/ppermute | solution.py:15
  465.9 14.8 %collective-permute-start.38 = (f32[4,192,128]{2,1,0:T(8,128)S(1)}, f32[4,192,128]{2,1,0:T(8,128)S(1)}, u32[]{:S(2)}, u32[]{:S(2)}) collective-permute-start(f32[4,192,128]{2,1,0:T(8,128)S(1)} %get-tuple-element.80), channel_id=1, source_target_pairs={{4,0},{8,4},{12,8},{16,12},{20,16},{24,20},{28,24},{32,28},{36,32}... | collective-permute-start | bytes 1179656 | tf_op jit(solution)/shard_map/ppermute | solution.py:16
  468.1 20.3 %collective-permute-start.39 = (f32[4,192,128]{2,1,0:T(8,128)S(1)}, f32[4,192,128]{2,1,0:T(8,128)S(1)}, u32[]{:S(2)}, u32[]{:S(2)}) collective-permute-start(f32[4,192,128]{2,1,0:T(8,128)S(1)} %get-tuple-element.79), channel_id=1, source_target_pairs={{0,4},{4,8},{8,12},{12,16},{16,20},{20,24},{24,28},{28,32},{32,36}... | collective-permute-start | bytes 1179656 | tf_op jit(solution)/shard_map/ppermute | solution.py:15
  475.7 13.1 %copy-start.13 = (f32[8,192,128]{2,1,0:T(8,128)S(1)}, f32[8,192,128]{2,1,0:T(8,128)}, u32[]{:S(2)}) copy-start(f32[8,192,128]{2,1,0:T(8,128)} %get-tuple-element.59) | copy-start | bytes 2359300
  489.0 3.6 collective-permute-start.40
  492.7 10.3 %collective-permute-start.41 = (f32[8,48,128]{2,1,0:T(8,128)S(1)}, f32[8,48,128]{2,1,0:T(8,128)S(1)}, u32[]{:S(2)}, u32[]{:S(2)}) collective-permute-start(f32[8,48,128]{2,1,0:T(8,128)S(1)} %dynamic-slice_bitcast_fusion), channel_id=1, source_target_pairs={{0,2},{1,3},{2,0},{3,1},{4,6},{5,7},{6,4},{7,5},{8,10},{9,11},{10,... | collective-permute-start | bytes 589832 | tf_op jit(solution)/shard_map/ppermute | solution.py:143
  (32 other events, 145.6 us)

commit v4 on v2

--- a/solution.py
+++ b/solution.py
@@ -104,12 +104,24 @@
     source_index = jnp.where(inside, local_sources, 0)
     pulses = wavelet[0]
 
+    lanes = extent_z
+    row_ids = lax.broadcasted_iota(jnp.int32, (steps, block_cells // lanes, pulses.shape[1]), 1)
+    by_row = jnp.where(
+        row_ids == (source_index // lanes)[None, None, :],
+        jnp.where(inside, pulses, 0.0)[:, None, :],
+        0.0,
+    ).reshape(-1, pulses.shape[1])
+    lane_ids = lax.broadcasted_iota(jnp.int32, (pulses.shape[1], lanes), 1)
+    by_lane = (lane_ids == (source_index % lanes)[:, None]).astype(jnp.float32)
+    sources_all = jnp.dot(by_row, by_lane, precision=lax.Precision.HIGHEST).reshape(
+        (steps,) + velocity.shape
+    )
+
     current, former = wave_now[0], wave_prev[0]
     accelerations = []
     traces = []
     for t in range(steps):
-        injected = place_cells(velocity.shape, source_index, jnp.where(inside, pulses[t], 0.0))
-        latest = step(current, former, courant_sq, injected)
+        latest = step(current, former, courant_sq, sources_all[t])
         accelerations.append(lax.optimization_barrier(latest - 2.0 * current + former))
         traces.append(sample_cells(latest, receiver_cells))
         current, former = latest, current

time: 500 us -> 509 us (1.018)
  the two profiles are of different devices: /device:TPU:454 before, /device:TPU:464 now
where the time goes in v4:
time: 509 us; the launch traced here: 499 us
  waiting for transfers between devices  184 us (36%)
  starting transfers between devices  153 us (30%)
  other arithmetic  102 us (20%)
  local copies, waits for them, and re-layouts  34.9 us (7%)
  matrix products  23 us (5%)
    ppermute x20, waiting for transfers between devices, exchange_edges(): low = lax.ppermute(block[block.shape[0] - RADIUS:], 'space', forward)  113 us
    ppermute x20, starting transfers between devices, exchange_edges(): high = lax.ppermute(block[:RADIUS], 'space', backward)  94.7 us
    ppermute x20, waiting for transfers between devices, exchange_edges(): high = lax.ppermute(block[:RADIUS], 'space', backward)  63.9 us
    ppermute x20, starting transfers between devices, exchange_edges(): low = lax.ppermute(block[block.shape[0] - RADIUS:], 'space', forward)  51.6 us
    add x10, other arithmetic, per_device(): latest - 2.0 * current + former  35 us
    add x11, other arithmetic, step(): 2.0 * current - former + courant_sq * inner_laplace(current) + injected  30.8 us
    add x20, other arithmetic, step(): base + courant_sq * edge_terms(low, high, current.shape[0])  23.7 us
    dot_general x10, matrix products, place_cells(): placed = jnp.dot(by_row, by_lane, precision=lax.Precision.HIGHEST)  19.3 us
  transfers between devices with their start and end apart: 42, of which 36 were waited for; matrix products, arithmetic and copies ran while one was open for 30% of the time, Pallas kernels for 0%

profile of v4, /device:TPU:464, one launch (start us, length us, event | category | flops | bytes accessed | tf_op | source)
XLA Modules:
  0.0 499.3 jit_solution(6940816095950502092)
XLA Ops:
  10.0 4.2 collective-permute-start.20
  16.4 8.3 %bitcast_select_fusion = f32[15360,128]{1,0:T(8,128)S(1)} fusion(f32[10,128]{1,0:T(8,128)S(1)} %bitcast_select_fusion.1, s32[128]{0:T(128)S(1)} %and_select_fusion.1, s32[15360]{0:T(1024)S(1)} %iota.44), kind=kLoop, calls=%fused_computation.490 | loop fusion | flops 3932160 | bytes 7931392 | tf_op jit(solution)/shard_map/jit(_where)/select_n | solution.py:109
  24.7 3.7 fusion.942
  39.2 4.7 collective-permute-start.2
  46.0 4.7 bitcast_add_fusion
  55.1 5.6 %collective-permute-done.3 = f32[4,192,128]{2,1,0:T(8,128)} collective-permute-done((f32[4,192,128]{2,1,0:T(8,128)S(1)}, f32[4,192,128]{2,1,0:T(8,128)}, u32[]{:S(2)}, u32[]{:S(2)}) %collective-permute-start.3) | collective-permute-done | bytes 393248 | tf_op jit(solution)/shard_map/ppermute | solution.py:15
  69.5 3.7 subtract_add_fusion
  77.9 9.5 %collective-permute-done.5 = f32[4,192,128]{2,1,0:T(8,128)} collective-permute-done((f32[4,192,128]{2,1,0:T(8,128)}, f32[4,192,128]{2,1,0:T(8,128)}, u32[]{:S(2)}, u32[]{:S(2)}) %collective-permute-start.5) | collective-permute-done | bytes 393248 | tf_op jit(solution)/shard_map/ppermute | solution.py:15
  90.3 9.0 %collective-permute-start.6 = (f32[4,192,128]{2,1,0:T(8,128)}, f32[4,192,128]{2,1,0:T(8,128)}, u32[]{:S(2)}, u32[]{:S(2)}) collective-permute-start(f32[4,192,128]{2,1,0:T(8,128)} %get-tuple-element.98), channel_id=1, source_target_pairs={{4,0},{8,4},{12,8},{16,12},{20,16},{24,20},{28,24},{32,28},{36,32}... | collective-permute-start | bytes 1179656 | tf_op jit(solution)/shard_map/ppermute | solution.py:16
  101.5 3.7 subtract_add_fusion.1
  109.2 7.6 %collective-permute-done.7 = f32[4,192,128]{2,1,0:T(8,128)} collective-permute-done((f32[4,192,128]{2,1,0:T(8,128)}, f32[4,192,128]{2,1,0:T(8,128)}, u32[]{:S(2)}, u32[]{:S(2)}) %collective-permute-start.7) | collective-permute-done | bytes 393248 | tf_op jit(solution)/shard_map/ppermute | solution.py:15
  119.7 3.7 collective-permute-start.8
  134.0 7.0 %collective-permute-done.9 = f32[4,192,128]{2,1,0:T(8,128)} collective-permute-done((f32[4,192,128]{2,1,0:T(8,128)}, f32[4,192,128]{2,1,0:T(8,128)}, u32[]{:S(2)}, u32[]{:S(2)}) %collective-permute-start.9) | collective-permute-done | bytes 393248 | tf_op jit(solution)/shard_map/ppermute | solution.py:15
  158.1 4.8 collective-permute-done.11
  167.9 3.9 collective-permute-start.13
  171.8 3.7 subtract_add_fusion.4
  186.7 9.1 %collective-permute-start.14 = (f32[4,192,128]{2,1,0:T(8,128)}, f32[4,192,128]{2,1,0:T(8,128)}, u32[]{:S(2)}, u32[]{:S(2)}) collective-permute-start(f32[4,192,128]{2,1,0:T(8,128)} %get-tuple-element.90), channel_id=1, source_target_pairs={{4,0},{8,4},{12,8},{16,12},{20,16},{24,20},{28,24},{32,28},{36,32}... | collective-permute-start | bytes 1179656 | tf_op jit(solution)/shard_map/ppermute | solution.py:16
  205.7 7.6 %collective-permute-done.15 = f32[4,192,128]{2,1,0:T(8,128)} collective-permute-done((f32[4,192,128]{2,1,0:T(8,128)}, f32[4,192,128]{2,1,0:T(8,128)}, u32[]{:S(2)}, u32[]{:S(2)}) %collective-permute-start.15) | collective-permute-done | bytes 393248 | tf_op jit(solution)/shard_map/ppermute | solution.py:15
  216.3 3.7 collective-permute-start.16
  222.5 3.7 subtract_add_fusion.6
  230.5 7.0 %collective-permute-done.17 = f32[4,192,128]{2,1,0:T(8,128)} collective-permute-done((f32[4,192,128]{2,1,0:T(8,128)}, f32[4,192,128]{2,1,0:T(8,128)}, u32[]{:S(2)}, u32[]{:S(2)}) %collective-permute-start.17) | collective-permute-done | bytes 393248 | tf_op jit(solution)/shard_map/ppermute | solution.py:15
  246.3 3.7 subtract_add_fusion.7
  254.7 4.8 collective-permute-done.19
  274.8 3.9 collective-permute-start.23
  308.8 5.3 %collective-permute-done.24 = f32[4,192,128]{2,1,0:T(8,128)S(1)} collective-permute-done((f32[4,192,128]{2,1,0:T(8,128)S(1)}, f32[4,192,128]{2,1,0:T(8,128)S(1)}, u32[]{:S(2)}, u32[]{:S(2)}) %collective-permute-start.24) | collective-permute-done | bytes 393248 | tf_op jit(solution)/shard_map/ppermute | solution.py:16
  314.0 7.8 %collective-permute-done.25 = f32[4,192,128]{2,1,0:T(8,128)S(1)} collective-permute-done((f32[4,192,128]{2,1,0:T(8,128)S(1)}, f32[4,192,128]{2,1,0:T(8,128)S(1)}, u32[]{:S(2)}, u32[]{:S(2)}) %collective-permute-start.25) | collective-permute-done | bytes 393248 | tf_op jit(solution)/shard_map/ppermute | solution.py:15
  322.1 4.5 collective-permute-start.26
  331.4 4.8 collective-permute-done.26
  336.2 7.0 %collective-permute-done.27 = f32[4,192,128]{2,1,0:T(8,128)S(1)} collective-permute-done((f32[4,192,128]{2,1,0:T(8,128)S(1)}, f32[4,192,128]{2,1,0:T(8,128)S(1)}, u32[]{:S(2)}, u32[]{:S(2)}) %collective-permute-start.27) | collective-permute-done | bytes 393248 | tf_op jit(solution)/shard_map/ppermute | solution.py:15
  343.5 14.9 %collective-permute-start.28 = (f32[4,192,128]{2,1,0:T(8,128)S(1)}, f32[4,192,128]{2,1,0:T(8,128)S(1)}, u32[]{:S(2)}, u32[]{:S(2)}) collective-permute-start(f32[4,192,128]{2,1,0:T(8,128)S(1)} %get-tuple-element.70), channel_id=1, source_target_pairs={{4,0},{8,4},{12,8},{16,12},{20,16},{24,20},{28,24},{32,28},{36,32}... | collective-permute-start | bytes 1179656 | tf_op jit(solution)/shard_map/ppermute | solution.py:16
  363.2 4.8 collective-permute-done.28
  368.0 7.6 %collective-permute-done.29 = f32[4,192,128]{2,1,0:T(8,128)S(1)} collective-permute-done((f32[4,192,128]{2,1,0:T(8,128)S(1)}, f32[4,192,128]{2,1,0:T(8,128)S(1)}, u32[]{:S(2)}, u32[]{:S(2)}) %collective-permute-start.29) | collective-permute-done | bytes 393248 | tf_op jit(solution)/shard_map/ppermute | solution.py:15
  376.0 5.7 %collective-permute-start.30 = (f32[4,192,128]{2,1,0:T(8,128)S(1)}, f32[4,192,128]{2,1,0:T(8,128)S(1)}, u32[]{:S(2)}, u32[]{:S(2)}) collective-permute-start(f32[4,192,128]{2,1,0:T(8,128)S(1)} %get-tuple-element.66), channel_id=1, source_target_pairs={{4,0},{8,4},{12,8},{16,12},{20,16},{24,20},{28,24},{32,28},{36,32}... | collective-permute-start | bytes 1179656 | tf_op jit(solution)/shard_map/ppermute | solution.py:16
  386.4 4.8 collective-permute-done.30
  391.2 7.6 %collective-permute-done.31 = f32[4,192,128]{2,1,0:T(8,128)S(1)} collective-permute-done((f32[4,192,128]{2,1,0:T(8,128)S(1)}, f32[4,192,128]{2,1,0:T(8,128)S(1)}, u32[]{:S(2)}, u32[]{:S(2)}) %collective-permute-start.31) | collective-permute-done | bytes 393248 | tf_op jit(solution)/shard_map/ppermute | solution.py:15
  399.1 5.3 %collective-permute-start.32 = (f32[4,192,128]{2,1,0:T(8,128)S(1)}, f32[4,192,128]{2,1,0:T(8,128)S(1)}, u32[]{:S(2)}, u32[]{:S(2)}) collective-permute-start(f32[4,192,128]{2,1,0:T(8,128)S(1)} %get-tuple-element.62), channel_id=1, source_target_pairs={{4,0},{8,4},{12,8},{16,12},{20,16},{24,20},{28,24},{32,28},{36,32}... | collective-permute-start | bytes 1179656 | tf_op jit(solution)/shard_map/ppermute | solution.py:16
  409.4 4.5 collective-permute-done.32
  413.9 6.7 %collective-permute-done.33 = f32[4,192,128]{2,1,0:T(8,128)S(1)} collective-permute-done((f32[4,192,128]{2,1,0:T(8,128)S(1)}, f32[4,192,128]{2,1,0:T(8,128)S(1)}, u32[]{:S(2)}, u32[]{:S(2)}) %collective-permute-start.33) | collective-permute-done | bytes 393248 | tf_op jit(solution)/shard_map/ppermute | solution.py:15
  429.6 5.3 %collective-permute-done.34 = f32[4,192,128]{2,1,0:T(8,128)S(1)} collective-permute-done((f32[4,192,128]{2,1,0:T(8,128)S(1)}, f32[4,192,128]{2,1,0:T(8,128)S(1)}, u32[]{:S(2)}, u32[]{:S(2)}) %collective-permute-start.34) | collective-permute-done | bytes 393248 | tf_op jit(solution)/shard_map/ppermute | solution.py:16
  434.9 3.8 collective-permute-done.35
  439.1 4.1 collective-permute-start.36
  447.9 5.1 %collective-permute-done.36 = f32[4,192,128]{2,1,0:T(8,128)S(1)} collective-permute-done((f32[4,192,128]{2,1,0:T(8,128)S(1)}, f32[4,192,128]{2,1,0:T(8,128)S(1)}, u32[]{:S(2)}, u32[]{:S(2)}) %collective-permute-start.36) | collective-permute-done | bytes 393248 | tf_op jit(solution)/shard_map/ppermute | solution.py:16
  453.0 7.3 %collective-permute-done.37 = f32[4,192,128]{2,1,0:T(8,128)S(1)} collective-permute-done((f32[4,192,128]{2,1,0:T(8,128)S(1)}, f32[4,192,128]{2,1,0:T(8,128)S(1)}, u32[]{:S(2)}, u32[]{:S(2)}) %collective-permute-start.37) | collective-permute-done | bytes 393248 | tf_op jit(solution)/shard_map/ppermute | solution.py:15
  460.7 5.7 %collective-permute-start.38 = (f32[4,192,128]{2,1,0:T(8,128)S(1)}, f32[4,192,128]{2,1,0:T(8,128)S(1)}, u32[]{:S(2)}, u32[]{:S(2)}) collective-permute-start(f32[4,192,128]{2,1,0:T(8,128)S(1)} %get-tuple-element.50), channel_id=1, source_target_pairs={{4,0},{8,4},{12,8},{16,12},{20,16},{24,20},{28,24},{32,28},{36,32}... | collective-permute-start | bytes 1179656 | tf_op jit(solution)/shard_map/ppermute | solution.py:16
  471.3 4.7 collective-permute-done.38
  475.9 7.6 %collective-permute-done.39 = f32[4,192,128]{2,1,0:T(8,128)S(1)} collective-permute-done((f32[4,192,128]{2,1,0:T(8,128)S(1)}, f32[4,192,128]{2,1,0:T(8,128)S(1)}, u32[]{:S(2)}, u32[]{:S(2)}) %collective-permute-start.39) | collective-permute-done | bytes 393248 | tf_op jit(solution)/shard_map/ppermute | solution.py:15
  487.8 4.7 collective-permute-start.41
  492.5 5.7 %collective-permute-done.41 = f32[8,48,128]{2,1,0:T(8,128)S(1)} collective-permute-done((f32[8,48,128]{2,1,0:T(8,128)S(1)}, f32[8,48,128]{2,1,0:T(8,128)S(1)}, u32[]{:S(2)}, u32[]{:S(2)}) %collective-permute-start.41) | collective-permute-done | bytes 196640 | tf_op jit(solution)/shard_map/ppermute | solution.py:153
  (222 shorter events, 220.3 us)
Async XLA Ops:
  2.1 34.8 %collective-permute-start = (f32[4,192,128]{2,1,0:T(8,128)}, f32[4,192,128]{2,1,0:T(8,128)S(1)}, u32[]{:S(2)}, u32[]{:S(2)}) collective-permute-start(f32[4,192,128]{2,1,0:T(8,128)} %get-tuple-element.104), channel_id=1, source_target_pairs={{4,0},{8,4},{12,8},{16,12},{20,16},{24,20},{28,24},{32,28},{36,32}... | collective-permute-start | bytes 1179656 | tf_op jit(solution)/shard_map/ppermute | solution.py:16
  5.4 31.6 %collective-permute-start.1 = (f32[4,192,128]{2,1,0:T(8,128)}, f32[4,192,128]{2,1,0:T(8,128)}, u32[]{:S(2)}, u32[]{:S(2)}) collective-permute-start(f32[4,192,128]{2,1,0:T(8,128)} %get-tuple-element.103), channel_id=1, source_target_pairs={{0,4},{4,8},{8,12},{12,16},{16,20},{20,24},{24,28},{28,32},{32,36}... | collective-permute-start | bytes 1179656 | tf_op jit(solution)/shard_map/ppermute | solution.py:15
  10.0 260.8 %collective-permute-start.20 = (f32[4,192,128]{2,1,0:T(8,128)}, f32[4,192,128]{2,1,0:T(8,128)}, u32[]{:S(2)}, u32[]{:S(2)}) collective-permute-start(f32[4,192,128]{2,1,0:T(8,128)} %get-tuple-element.84), channel_id=1, source_target_pairs={{4,0},{8,4},{12,8},{16,12},{20,16},{24,20},{28,24},{32,28},{36,32}... | collective-permute-start | bytes 1179656 | tf_op jit(solution)/shard_map/ppermute | solution.py:16
  14.2 256.7 %collective-permute-start.21 = (f32[4,192,128]{2,1,0:T(8,128)}, f32[4,192,128]{2,1,0:T(8,128)}, u32[]{:S(2)}, u32[]{:S(2)}) collective-permute-start(f32[4,192,128]{2,1,0:T(8,128)} %get-tuple-element.83), channel_id=1, source_target_pairs={{0,4},{4,8},{8,12},{12,16},{16,20},{20,24},{24,28},{28,32},{32,36}... | collective-permute-start | bytes 1179656 | tf_op jit(solution)/shard_map/ppermute | solution.py:15
  35.5 37.7 %copy-start.26 = (s32[1024]{0:T(1024)}, s32[1024]{0:T(1024)S(1)}, u32[]{:S(2)}) copy-start(s32[1024]{0:T(1024)S(1)} %pad_clamp_fusion) | copy-start | bytes 12292
  39.2 15.0 %collective-permute-start.2 = (f32[4,192,128]{2,1,0:T(8,128)}, f32[4,192,128]{2,1,0:T(8,128)S(1)}, u32[]{:S(2)}, u32[]{:S(2)}) collective-permute-start(f32[4,192,128]{2,1,0:T(8,128)} %get-tuple-element.102), channel_id=1, source_target_pairs={{4,0},{8,4},{12,8},{16,12},{20,16},{24,20},{28,24},{32,28},{36,32}... | collective-permute-start | bytes 1179656 | tf_op jit(solution)/shard_map/ppermute | solution.py:16
  43.9 16.7 %collective-permute-start.3 = (f32[4,192,128]{2,1,0:T(8,128)S(1)}, f32[4,192,128]{2,1,0:T(8,128)}, u32[]{:S(2)}, u32[]{:S(2)}) collective-permute-start(f32[4,192,128]{2,1,0:T(8,128)S(1)} %get-tuple-element.101), channel_id=1, source_target_pairs={{0,4},{4,8},{8,12},{12,16},{16,20},{20,24},{24,28},{28,32},{32,36}... | collective-permute-start | bytes 1179656 | tf_op jit(solution)/shard_map/ppermute | solution.py:15
  63.7 14.2 %collective-permute-start.4 = (f32[4,192,128]{2,1,0:T(8,128)}, f32[4,192,128]{2,1,0:T(8,128)}, u32[]{:S(2)}, u32[]{:S(2)}) collective-permute-start(f32[4,192,128]{2,1,0:T(8,128)} %get-tuple-element.100), channel_id=1, source_target_pairs={{4,0},{8,4},{12,8},{16,12},{20,16},{24,20},{28,24},{32,28},{36,32}... | collective-permute-start | bytes 1179656 | tf_op jit(solution)/shard_map/ppermute | solution.py:16
  67.2 20.2 %collective-permute-start.5 = (f32[4,192,128]{2,1,0:T(8,128)}, f32[4,192,128]{2,1,0:T(8,128)}, u32[]{:S(2)}, u32[]{:S(2)}) collective-permute-start(f32[4,192,128]{2,1,0:T(8,128)} %get-tuple-element.99), channel_id=1, source_target_pairs={{0,4},{4,8},{8,12},{12,16},{16,20},{20,24},{24,28},{28,32},{32,36}... | collective-permute-start | bytes 1179656 | tf_op jit(solution)/shard_map/ppermute | solution.py:15
  74.8 26.7 %copy-start.22 = (f32[1536,128]{1,0:T(8,128)S(1)}, f32[1536,128]{1,0:T(8,128)}, u32[]{:S(2)}) copy-start(f32[1536,128]{1,0:T(8,128)} %get-tuple-element.25) | copy-start | bytes 2359300
  90.3 18.9 %collective-permute-start.6 = (f32[4,192,128]{2,1,0:T(8,128)}, f32[4,192,128]{2,1,0:T(8,128)}, u32[]{:S(2)}, u32[]{:S(2)}) collective-permute-start(f32[4,192,128]{2,1,0:T(8,128)} %get-tuple-element.98), channel_id=1, source_target_pairs={{4,0},{8,4},{12,8},{16,12},{20,16},{24,20},{28,24},{32,28},{36,32}... | collective-permute-start | bytes 1179656 | tf_op jit(solution)/shard_map/ppermute | solution.py:16
  99.3 17.5 %collective-permute-start.7 = (f32[4,192,128]{2,1,0:T(8,128)}, f32[4,192,128]{2,1,0:T(8,128)}, u32[]{:S(2)}, u32[]{:S(2)}) collective-permute-start(f32[4,192,128]{2,1,0:T(8,128)} %get-tuple-element.97), channel_id=1, source_target_pairs={{0,4},{4,8},{8,12},{12,16},{16,20},{20,24},{24,28},{28,32},{32,36}... | collective-permute-start | bytes 1179656 | tf_op jit(solution)/shard_map/ppermute | solution.py:15
  119.7 14.2 %collective-permute-start.8 = (f32[4,192,128]{2,1,0:T(8,128)}, f32[4,192,128]{2,1,0:T(8,128)}, u32[]{:S(2)}, u32[]{:S(2)}) collective-permute-start(f32[4,192,128]{2,1,0:T(8,128)} %get-tuple-element.96), channel_id=1, source_target_pairs={{4,0},{8,4},{12,8},{16,12},{20,16},{24,20},{28,24},{32,28},{36,32}... | collective-permute-start | bytes 1179656 | tf_op jit(solution)/shard_map/ppermute | solution.py:16
  123.5 17.5 %collective-permute-start.9 = (f32[4,192,128]{2,1,0:T(8,128)}, f32[4,192,128]{2,1,0:T(8,128)}, u32[]{:S(2)}, u32[]{:S(2)}) collective-permute-start(f32[4,192,128]{2,1,0:T(8,128)} %get-tuple-element.95), channel_id=1, source_target_pairs={{0,4},{4,8},{8,12},{12,16},{16,20},{20,24},{24,28},{28,32},{32,36}... | collective-permute-start | bytes 1179656 | tf_op jit(solution)/shard_map/ppermute | solution.py:15
  143.9 14.2 %collective-permute-start.10 = (f32[4,192,128]{2,1,0:T(8,128)}, f32[4,192,128]{2,1,0:T(8,128)}, u32[]{:S(2)}, u32[]{:S(2)}) collective-permute-start(f32[4,192,128]{2,1,0:T(8,128)} %get-tuple-element.94), channel_id=1, source_target_pairs={{4,0},{8,4},{12,8},{16,12},{20,16},{24,20},{28,24},{32,28},{36,32}... | collective-permute-start | bytes 1179656 | tf_op jit(solution)/shard_map/ppermute | solution.py:16
  146.1 16.9 %collective-permute-start.11 = (f32[4,192,128]{2,1,0:T(8,128)}, f32[4,192,128]{2,1,0:T(8,128)}, u32[]{:S(2)}, u32[]{:S(2)}) collective-permute-start(f32[4,192,128]{2,1,0:T(8,128)} %get-tuple-element.93), channel_id=1, source_target_pairs={{0,4},{4,8},{8,12},{12,16},{16,20},{20,24},{24,28},{28,32},{32,36}... | collective-permute-start | bytes 1179656 | tf_op jit(solution)/shard_map/ppermute | solution.py:15
  165.0 32.8 %copy-start.1 = (f32[8,192,128]{2,1,0:T(8,128)}, f32[8,192,128]{2,1,0:T(8,128)S(1)}, u32[]{:S(2)}) copy-start(f32[8,192,128]{2,1,0:T(8,128)S(1)} %fusion.121) | copy-start | bytes 2359300
  166.0 14.2 %collective-permute-start.12 = (f32[4,192,128]{2,1,0:T(8,128)}, f32[4,192,128]{2,1,0:T(8,128)}, u32[]{:S(2)}, u32[]{:S(2)}) collective-permute-start(f32[4,192,128]{2,1,0:T(8,128)} %get-tuple-element.92), channel_id=1, source_target_pairs={{4,0},{8,4},{12,8},{16,12},{20,16},{24,20},{28,24},{32,28},{36,32}... | collective-permute-start | bytes 1179656 | tf_op jit(solution)/shard_map/ppermute | solution.py:16
  167.9 15.8 %collective-permute-start.13 = (f32[4,192,128]{2,1,0:T(8,128)}, f32[4,192,128]{2,1,0:T(8,128)}, u32[]{:S(2)}, u32[]{:S(2)}) collective-permute-start(f32[4,192,128]{2,1,0:T(8,128)} %get-tuple-element.91), channel_id=1, source_target_pairs={{0,4},{4,8},{8,12},{12,16},{16,20},{20,24},{24,28},{28,32},{32,36}... | collective-permute-start | bytes 1179656 | tf_op jit(solution)/shard_map/ppermute | solution.py:15
  177.3 20.5 %copy-start.18 = (f32[1536,128]{1,0:T(8,128)S(1)}, f32[1536,128]{1,0:T(8,128)}, u32[]{:S(2)}) copy-start(f32[1536,128]{1,0:T(8,128)} %get-tuple-element.21) | copy-start | bytes 2359300
  186.7 19.0 %collective-permute-start.14 = (f32[4,192,128]{2,1,0:T(8,128)}, f32[4,192,128]{2,1,0:T(8,128)}, u32[]{:S(2)}, u32[]{:S(2)}) collective-permute-start(f32[4,192,128]{2,1,0:T(8,128)} %get-tuple-element.90), channel_id=1, source_target_pairs={{4,0},{8,4},{12,8},{16,12},{20,16},{24,20},{28,24},{32,28},{36,32}... | collective-permute-start | bytes 1179656 | tf_op jit(solution)/shard_map/ppermute | solution.py:16
  195.8 17.5 %collective-permute-start.15 = (f32[4,192,128]{2,1,0:T(8,128)}, f32[4,192,128]{2,1,0:T(8,128)}, u32[]{:S(2)}, u32[]{:S(2)}) collective-permute-start(f32[4,192,128]{2,1,0:T(8,128)} %get-tuple-element.89), channel_id=1, source_target_pairs={{0,4},{4,8},{8,12},{12,16},{16,20},{20,24},{24,28},{28,32},{32,36}... | collective-permute-start | bytes 1179656 | tf_op jit(solution)/shard_map/ppermute | solution.py:15
  201.4 21.1 %copy-start.17 = (f32[1536,128]{1,0:T(8,128)S(1)}, f32[1536,128]{1,0:T(8,128)}, u32[]{:S(2)}) copy-start(f32[1536,128]{1,0:T(8,128)} %get-tuple-element.20) | copy-start | bytes 2359300
  216.3 14.2 %collective-permute-start.16 = (f32[4,192,128]{2,1,0:T(8,128)}, f32[4,192,128]{2,1,0:T(8,128)}, u32[]{:S(2)}, u32[]{:S(2)}) collective-permute-start(f32[4,192,128]{2,1,0:T(8,128)} %get-tuple-element.88), channel_id=1, source_target_pairs={{4,0},{8,4},{12,8},{16,12},{20,16},{24,20},{28,24},{32,28},{36,32}... | collective-permute-start | bytes 1179656 | tf_op jit(solution)/shard_map/ppermute | solution.py:16
  220.0 17.5 %collective-permute-start.17 = (f32[4,192,128]{2,1,0:T(8,128)}, f32[4,192,128]{2,1,0:T(8,128)}, u32[]{:S(2)}, u32[]{:S(2)}) collective-permute-start(f32[4,192,128]{2,1,0:T(8,128)} %get-tuple-element.87), channel_id=1, source_target_pairs={{0,4},{4,8},{8,12},{12,16},{16,20},{20,24},{24,28},{28,32},{32,36}... | collective-permute-start | bytes 1179656 | tf_op jit(solution)/shard_map/ppermute | solution.py:15
  240.4 14.2 %collective-permute-start.18 = (f32[4,192,128]{2,1,0:T(8,128)}, f32[4,192,128]{2,1,0:T(8,128)}, u32[]{:S(2)}, u32[]{:S(2)}) collective-permute-start(f32[4,192,128]{2,1,0:T(8,128)} %get-tuple-element.86), channel_id=1, source_target_pairs={{4,0},{8,4},{12,8},{16,12},{20,16},{24,20},{28,24},{32,28},{36,32}... | collective-permute-start | bytes 1179656 | tf_op jit(solution)/shard_map/ppermute | solution.py:16
  242.6 16.9 %collective-permute-start.19 = (f32[4,192,128]{2,1,0:T(8,128)}, f32[4,192,128]{2,1,0:T(8,128)}, u32[]{:S(2)}, u32[]{:S(2)}) collective-permute-start(f32[4,192,128]{2,1,0:T(8,128)} %get-tuple-element.85), channel_id=1, source_target_pairs={{0,4},{4,8},{8,12},{12,16},{16,20},{20,24},{24,28},{28,32},{32,36}... | collective-permute-start | bytes 1179656 | tf_op jit(solution)/shard_map/ppermute | solution.py:15
  272.8 26.3 %collective-permute-start.22 = (f32[4,192,128]{2,1,0:T(8,128)S(1)}, f32[4,192,128]{2,1,0:T(8,128)S(1)}, u32[]{:S(2)}, u32[]{:S(2)}) collective-permute-start(f32[4,192,128]{2,1,0:T(8,128)S(1)} %get-tuple-element.82), channel_id=1, source_target_pairs={{4,0},{8,4},{12,8},{16,12},{20,16},{24,20},{28,24},{32,28},{36,32}... | collective-permute-start | bytes 1179656 | tf_op jit(solution)/shard_map/ppermute | solution.py:16
  274.8 24.4 %collective-permute-start.23 = (f32[4,192,128]{2,1,0:T(8,128)S(1)}, f32[4,192,128]{2,1,0:T(8,128)S(1)}, u32[]{:S(2)}, u32[]{:S(2)}) collective-permute-start(f32[4,192,128]{2,1,0:T(8,128)S(1)} %get-tuple-element.81), channel_id=1, source_target_pairs={{0,4},{4,8},{8,12},{12,16},{16,20},{20,24},{24,28},{28,32},{32,36}... | collective-permute-start | bytes 1179656 | tf_op jit(solution)/shard_map/ppermute | solution.py:15
  299.5 14.6 %collective-permute-start.24 = (f32[4,192,128]{2,1,0:T(8,128)S(1)}, f32[4,192,128]{2,1,0:T(8,128)S(1)}, u32[]{:S(2)}, u32[]{:S(2)}) collective-permute-start(f32[4,192,128]{2,1,0:T(8,128)S(1)} %get-tuple-element.78), channel_id=1, source_target_pairs={{4,0},{8,4},{12,8},{16,12},{20,16},{24,20},{28,24},{32,28},{36,32}... | collective-permute-start | bytes 1179656 | tf_op jit(solution)/shard_map/ppermute | solution.py:16
  302.3 19.5 %collective-permute-start.25 = (f32[4,192,128]{2,1,0:T(8,128)S(1)}, f32[4,192,128]{2,1,0:T(8,128)S(1)}, u32[]{:S(2)}, u32[]{:S(2)}) collective-permute-start(f32[4,192,128]{2,1,0:T(8,128)S(1)} %get-tuple-element.77), channel_id=1, source_target_pairs={{0,4},{4,8},{8,12},{12,16},{16,20},{20,24},{24,28},{28,32},{32,36}... | collective-permute-start | bytes 1179656 | tf_op jit(solution)/shard_map/ppermute | solution.py:15
  322.1 14.1 %collective-permute-start.26 = (f32[4,192,128]{2,1,0:T(8,128)S(1)}, f32[4,192,128]{2,1,0:T(8,128)S(1)}, u32[]{:S(2)}, u32[]{:S(2)}) collective-permute-start(f32[4,192,128]{2,1,0:T(8,128)S(1)} %get-tuple-element.74), channel_id=1, source_target_pairs={{4,0},{8,4},{12,8},{16,12},{20,16},{24,20},{28,24},{32,28},{36,32}... | collective-permute-start | bytes 1179656 | tf_op jit(solution)/shard_map/ppermute | solution.py:16
  326.6 16.5 %collective-permute-start.27 = (f32[4,192,128]{2,1,0:T(8,128)S(1)}, f32[4,192,128]{2,1,0:T(8,128)S(1)}, u32[]{:S(2)}, u32[]{:S(2)}) collective-permute-start(f32[4,192,128]{2,1,0:T(8,128)S(1)} %get-tuple-element.73), channel_id=1, source_target_pairs={{0,4},{4,8},{8,12},{12,16},{16,20},{20,24},{24,28},{28,32},{32,36}... | collective-permute-start | bytes 1179656 | tf_op jit(solution)/shard_map/ppermute | solution.py:15
  331.4 29.0 %copy-start.10 = (f32[8,192,128]{2,1,0:T(8,128)S(1)}, f32[8,192,128]{2,1,0:T(8,128)}, u32[]{:S(2)}) copy-start(f32[8,192,128]{2,1,0:T(8,128)} %get-tuple-element.43) | copy-start | bytes 2359300
  343.5 24.5 %collective-permute-start.28 = (f32[4,192,128]{2,1,0:T(8,128)S(1)}, f32[4,192,128]{2,1,0:T(8,128)S(1)}, u32[]{:S(2)}, u32[]{:S(2)}) collective-permute-start(f32[4,192,128]{2,1,0:T(8,128)S(1)} %get-tuple-element.70), channel_id=1, source_target_pairs={{4,0},{8,4},{12,8},{16,12},{20,16},{24,20},{28,24},{32,28},{36,32}... | collective-permute-start | bytes 1179656 | tf_op jit(solution)/shard_map/ppermute | solution.py:16
  358.4 17.2 %collective-permute-start.29 = (f32[4,192,128]{2,1,0:T(8,128)S(1)}, f32[4,192,128]{2,1,0:T(8,128)S(1)}, u32[]{:S(2)}, u32[]{:S(2)}) collective-permute-start(f32[4,192,128]{2,1,0:T(8,128)S(1)} %get-tuple-element.69), channel_id=1, source_target_pairs={{0,4},{4,8},{8,12},{12,16},{16,20},{20,24},{24,28},{28,32},{32,36}... | collective-permute-start | bytes 1179656 | tf_op jit(solution)/shard_map/ppermute | solution.py:15
  376.0 15.2 %collective-permute-start.30 = (f32[4,192,128]{2,1,0:T(8,128)S(1)}, f32[4,192,128]{2,1,0:T(8,128)S(1)}, u32[]{:S(2)}, u32[]{:S(2)}) collective-permute-start(f32[4,192,128]{2,1,0:T(8,128)S(1)} %get-tuple-element.66), channel_id=1, source_target_pairs={{4,0},{8,4},{12,8},{16,12},{20,16},{24,20},{28,24},{32,28},{36,32}... | collective-permute-start | bytes 1179656 | tf_op jit(solution)/shard_map/ppermute | solution.py:16
  381.6 17.2 %collective-permute-start.31 = (f32[4,192,128]{2,1,0:T(8,128)S(1)}, f32[4,192,128]{2,1,0:T(8,128)S(1)}, u32[]{:S(2)}, u32[]{:S(2)}) collective-permute-start(f32[4,192,128]{2,1,0:T(8,128)S(1)} %get-tuple-element.65), channel_id=1, source_target_pairs={{0,4},{4,8},{8,12},{12,16},{16,20},{20,24},{24,28},{28,32},{32,36}... | collective-permute-start | bytes 1179656 | tf_op jit(solution)/shard_map/ppermute | solution.py:15
  399.1 14.8 %collective-permute-start.32 = (f32[4,192,128]{2,1,0:T(8,128)S(1)}, f32[4,192,128]{2,1,0:T(8,128)S(1)}, u32[]{:S(2)}, u32[]{:S(2)}) collective-permute-start(f32[4,192,128]{2,1,0:T(8,128)S(1)} %get-tuple-element.62), channel_id=1, source_target_pairs={{4,0},{8,4},{12,8},{16,12},{20,16},{24,20},{28,24},{32,28},{36,32}... | collective-permute-start | bytes 1179656 | tf_op jit(solution)/shard_map/ppermute | solution.py:16
  404.4 16.2 %collective-permute-start.33 = (f32[4,192,128]{2,1,0:T(8,128)S(1)}, f32[4,192,128]{2,1,0:T(8,128)S(1)}, u32[]{:S(2)}, u32[]{:S(2)}) collective-permute-start(f32[4,192,128]{2,1,0:T(8,128)S(1)} %get-tuple-element.61), channel_id=1, source_target_pairs={{0,4},{4,8},{8,12},{12,16},{16,20},{20,24},{24,28},{28,32},{32,36}... | collective-permute-start | bytes 1179656 | tf_op jit(solution)/shard_map/ppermute | solution.py:15
  421.0 13.9 %collective-permute-start.34 = (f32[4,192,128]{2,1,0:T(8,128)S(1)}, f32[4,192,128]{2,1,0:T(8,128)S(1)}, u32[]{:S(2)}, u32[]{:S(2)}) collective-permute-start(f32[4,192,128]{2,1,0:T(8,128)S(1)} %get-tuple-element.58), channel_id=1, source_target_pairs={{4,0},{8,4},{12,8},{16,12},{20,16},{24,20},{28,24},{32,28},{36,32}... | collective-permute-start | bytes 1179656 | tf_op jit(solution)/shard_map/ppermute | solution.py:16
  423.2 15.6 %collective-permute-start.35 = (f32[4,192,128]{2,1,0:T(8,128)S(1)}, f32[4,192,128]{2,1,0:T(8,128)S(1)}, u32[]{:S(2)}, u32[]{:S(2)}) collective-permute-start(f32[4,192,128]{2,1,0:T(8,128)S(1)} %get-tuple-element.57), channel_id=1, source_target_pairs={{0,4},{4,8},{8,12},{12,16},{16,20},{20,24},{24,28},{28,32},{32,36}... | collective-permute-start | bytes 1179656 | tf_op jit(solution)/shard_map/ppermute | solution.py:15
  439.1 13.9 %collective-permute-start.36 = (f32[4,192,128]{2,1,0:T(8,128)S(1)}, f32[4,192,128]{2,1,0:T(8,128)S(1)}, u32[]{:S(2)}, u32[]{:S(2)}) collective-permute-start(f32[4,192,128]{2,1,0:T(8,128)S(1)} %get-tuple-element.54), channel_id=1, source_target_pairs={{4,0},{8,4},{12,8},{16,12},{20,16},{24,20},{28,24},{32,28},{36,32}... | collective-permute-start | bytes 1179656 | tf_op jit(solution)/shard_map/ppermute | solution.py:16
  443.2 17.2 %collective-permute-start.37 = (f32[4,192,128]{2,1,0:T(8,128)S(1)}, f32[4,192,128]{2,1,0:T(8,128)S(1)}, u32[]{:S(2)}, u32[]{:S(2)}) collective-permute-start(f32[4,192,128]{2,1,0:T(8,128)S(1)} %get-tuple-element.53), channel_id=1, source_target_pairs={{0,4},{4,8},{8,12},{12,16},{16,20},{20,24},{24,28},{28,32},{32,36}... | collective-permute-start | bytes 1179656 | tf_op jit(solution)/shard_map/ppermute | solution.py:15
  460.7 15.2 %collective-permute-start.38 = (f32[4,192,128]{2,1,0:T(8,128)S(1)}, f32[4,192,128]{2,1,0:T(8,128)S(1)}, u32[]{:S(2)}, u32[]{:S(2)}) collective-permute-start(f32[4,192,128]{2,1,0:T(8,128)S(1)} %get-tuple-element.50), channel_id=1, source_target_pairs={{4,0},{8,4},{12,8},{16,12},{20,16},{24,20},{28,24},{32,28},{36,32}... | collective-permute-start | bytes 1179656 | tf_op jit(solution)/shard_map/ppermute | solution.py:16
  466.4 17.2 %collective-permute-start.39 = (f32[4,192,128]{2,1,0:T(8,128)S(1)}, f32[4,192,128]{2,1,0:T(8,128)S(1)}, u32[]{:S(2)}, u32[]{:S(2)}) collective-permute-start(f32[4,192,128]{2,1,0:T(8,128)S(1)} %get-tuple-element.49), channel_id=1, source_target_pairs={{0,4},{4,8},{8,12},{12,16},{16,20},{20,24},{24,28},{28,32},{32,36}... | collective-permute-start | bytes 1179656 | tf_op jit(solution)/shard_map/ppermute | solution.py:15
  484.1 3.6 collective-permute-start.40
  487.8 10.3 %collective-permute-start.41 = (f32[8,48,128]{2,1,0:T(8,128)S(1)}, f32[8,48,128]{2,1,0:T(8,128)S(1)}, u32[]{:S(2)}, u32[]{:S(2)}) collective-permute-start(f32[8,48,128]{2,1,0:T(8,128)S(1)} %dynamic-slice_bitcast_fusion), channel_id=1, source_target_pairs={{0,2},{1,3},{2,0},{3,1},{4,6},{5,7},{6,4},{7,5},{8,10},{9,11},{10,... | collective-permute-start | bytes 589832 | tf_op jit(solution)/shard_map/ppermute | solution.py:153
  (34 other events, 336.5 us)

commit v5 on v2

--- a/solution.py
+++ b/solution.py
@@ -108,6 +108,8 @@
     accelerations = []
     traces = []
     for t in range(steps):
+        if t == steps - 1:
+            last_start = current
         injected = place_cells(velocity.shape, source_index, jnp.where(inside, pulses[t], 0.0))
         latest = step(current, former, courant_sq, injected)
         accelerations.append(lax.optimization_barrier(latest - 2.0 * current + former))
@@ -119,7 +121,8 @@
     )
     misfit = [(traces[t] - observed[0, t]) * live_slots for t in range(steps)]
 
-    following, furthest = adjoint_now[0], adjoint_prev[0]
+    following, _ = lax.optimization_barrier((adjoint_now[0], last_start))
+    furthest = adjoint_prev[0]
     imaging = jnp.zeros_like(velocity)
     for t in reversed(range(steps)):
         injected = place_cells(velocity.shape, receiver_cells, misfit[t])

time: 500 us -> 498 us (level)
  the two profiles are of different devices: /device:TPU:454 before, /device:TPU:106 now
where the time goes in v5:
time: 498 us; the launch traced here: 489 us
  waiting for transfers between devices  178 us (36%)
  starting transfers between devices  153 us (31%)
  other arithmetic  93.3 us (19%)
  matrix products  32.9 us (7%)
  local copies, waits for them, and re-layouts  29.4 us (6%)
    ppermute x20, waiting for transfers between devices, exchange_edges(): low = lax.ppermute(block[block.shape[0] - RADIUS:], 'space', forward)  107 us
    ppermute x20, starting transfers between devices, exchange_edges(): low = lax.ppermute(block[block.shape[0] - RADIUS:], 'space', forward)  96.8 us
    ppermute x20, waiting for transfers between devices, exchange_edges(): high = lax.ppermute(block[:RADIUS], 'space', backward)  63.5 us
    ppermute x20, starting transfers between devices, exchange_edges(): high = lax.ppermute(block[:RADIUS], 'space', backward)  49.9 us
    add x10, other arithmetic, per_device(): latest - 2.0 * current + former  34 us
    dot_general x20, matrix products, place_cells(): placed = jnp.dot(by_row, by_lane, precision=lax.Precision.HIGHEST)  32.9 us
    add x11, other arithmetic, step(): 2.0 * current - former + courant_sq * inner_laplace(current) + injected  31.8 us
    add x20, other arithmetic, step(): base + courant_sq * edge_terms(low, high, current.shape[0])  23.3 us
  transfers between devices with their start and end apart: 42, of which 34 were waited for; matrix products, arithmetic and copies ran while one was open for 25% of the time, Pallas kernels for 0%

profile of v5, /device:TPU:106, one launch (start us, length us, event | category | flops | bytes accessed | tf_op | source)
XLA Modules:
  0.0 488.8 jit_solution(10936700300533776117)
XLA Ops:
  4.5 4.3 collective-permute-start.1
  32.9 4.8 collective-permute-start.3
  37.7 3.7 bitcast_add_fusion
  46.1 5.7 %collective-permute-done.3 = f32[4,192,128]{2,1,0:T(8,128)} collective-permute-done((f32[4,192,128]{2,1,0:T(8,128)}, f32[4,192,128]{2,1,0:T(8,128)}, u32[]{:S(2)}, u32[]{:S(2)}) %collective-permute-start.3) | collective-permute-done | bytes 393248 | tf_op jit(solution)/shard_map/ppermute | solution.py:15
  58.1 3.7 collective-permute-start.5
  69.9 10.9 %collective-permute-done.5 = f32[4,192,128]{2,1,0:T(8,128)} collective-permute-done((f32[4,192,128]{2,1,0:T(8,128)}, f32[4,192,128]{2,1,0:T(8,128)}, u32[]{:S(2)}, u32[]{:S(2)}) %collective-permute-start.5) | collective-permute-done | bytes 393248 | tf_op jit(solution)/shard_map/ppermute | solution.py:15
  86.0 4.5 collective-permute-start.7
  90.6 3.7 subtract_add_fusion.1
  99.0 8.0 %collective-permute-done.7 = f32[4,192,128]{2,1,0:T(8,128)} collective-permute-done((f32[4,192,128]{2,1,0:T(8,128)}, f32[4,192,128]{2,1,0:T(8,128)}, u32[]{:S(2)}, u32[]{:S(2)}) %collective-permute-start.7) | collective-permute-done | bytes 393248 | tf_op jit(solution)/shard_map/ppermute | solution.py:15
  112.1 4.5 collective-permute-start.9
  125.1 5.7 %collective-permute-done.9 = f32[4,192,128]{2,1,0:T(8,128)} collective-permute-done((f32[4,192,128]{2,1,0:T(8,128)}, f32[4,192,128]{2,1,0:T(8,128)}, u32[]{:S(2)}, u32[]{:S(2)}) %collective-permute-start.9) | collective-permute-done | bytes 393248 | tf_op jit(solution)/shard_map/ppermute | solution.py:15
  136.0 4.5 collective-permute-start.11
  148.9 5.7 %collective-permute-done.11 = f32[4,192,128]{2,1,0:T(8,128)} collective-permute-done((f32[4,192,128]{2,1,0:T(8,128)}, f32[4,192,128]{2,1,0:T(8,128)}, u32[]{:S(2)}, u32[]{:S(2)}) %collective-permute-start.11) | collective-permute-done | bytes 393248 | tf_op jit(solution)/shard_map/ppermute | solution.py:15
  159.8 4.5 collective-permute-start.13
  172.7 4.6 collective-permute-done.13
  182.4 15.2 %collective-permute-start.15 = (f32[4,192,128]{2,1,0:T(8,128)}, f32[4,192,128]{2,1,0:T(8,128)}, u32[]{:S(2)}, u32[]{:S(2)}) collective-permute-start(f32[4,192,128]{2,1,0:T(8,128)} %get-tuple-element.81), channel_id=1, source_target_pairs={{0,4},{4,8},{8,12},{12,16},{16,20},{20,24},{24,28},{28,32},{32,36}... | collective-permute-start | bytes 1179656 | tf_op jit(solution)/shard_map/ppermute | solution.py:15
  208.4 3.8 collective-permute-start.17
  221.3 6.8 %collective-permute-done.17 = f32[4,192,128]{2,1,0:T(8,128)} collective-permute-done((f32[4,192,128]{2,1,0:T(8,128)S(1)}, f32[4,192,128]{2,1,0:T(8,128)}, u32[]{:S(2)}, u32[]{:S(2)}) %collective-permute-start.17) | collective-permute-done | bytes 393248 | tf_op jit(solution)/shard_map/ppermute | solution.py:15
  233.2 4.5 collective-permute-start.19
  246.8 4.0 collective-permute-start.21
  250.8 4.6 collective-permute-done.19
  273.2 4.5 collective-permute-start.23
  298.8 5.0 %collective-permute-start.24 = (f32[4,192,128]{2,1,0:T(8,128)S(1)}, f32[4,192,128]{2,1,0:T(8,128)S(1)}, u32[]{:S(2)}, u32[]{:S(2)}) collective-permute-start(f32[4,192,128]{2,1,0:T(8,128)S(1)} %get-tuple-element.70), channel_id=1, source_target_pairs={{4,0},{8,4},{12,8},{16,12},{20,16},{24,20},{28,24},{32,28},{36,32}... | collective-permute-start | bytes 1179656 | tf_op jit(solution)/shard_map/ppermute | solution.py:16
  308.6 5.1 %collective-permute-done.24 = f32[4,192,128]{2,1,0:T(8,128)S(1)} collective-permute-done((f32[4,192,128]{2,1,0:T(8,128)S(1)}, f32[4,192,128]{2,1,0:T(8,128)S(1)}, u32[]{:S(2)}, u32[]{:S(2)}) %collective-permute-start.24) | collective-permute-done | bytes 393248 | tf_op jit(solution)/shard_map/ppermute | solution.py:16
  313.7 9.8 %collective-permute-done.25 = f32[4,192,128]{2,1,0:T(8,128)S(1)} collective-permute-done((f32[4,192,128]{2,1,0:T(8,128)S(1)}, f32[4,192,128]{2,1,0:T(8,128)S(1)}, u32[]{:S(2)}, u32[]{:S(2)}) %collective-permute-start.25) | collective-permute-done | bytes 393248 | tf_op jit(solution)/shard_map/ppermute | solution.py:15
  326.2 4.5 collective-permute-start.27
  333.5 5.3 %collective-permute-done.26 = f32[4,192,128]{2,1,0:T(8,128)S(1)} collective-permute-done((f32[4,192,128]{2,1,0:T(8,128)S(1)}, f32[4,192,128]{2,1,0:T(8,128)S(1)}, u32[]{:S(2)}, u32[]{:S(2)}) %collective-permute-start.26) | collective-permute-done | bytes 393248 | tf_op jit(solution)/shard_map/ppermute | solution.py:16
  338.8 7.0 %collective-permute-done.27 = f32[4,192,128]{2,1,0:T(8,128)S(1)} collective-permute-done((f32[4,192,128]{2,1,0:T(8,128)S(1)}, f32[4,192,128]{2,1,0:T(8,128)S(1)}, u32[]{:S(2)}, u32[]{:S(2)}) %collective-permute-start.27) | collective-permute-done | bytes 393248 | tf_op jit(solution)/shard_map/ppermute | solution.py:15
  348.5 4.5 collective-permute-start.29
  355.9 5.3 %collective-permute-done.28 = f32[4,192,128]{2,1,0:T(8,128)S(1)} collective-permute-done((f32[4,192,128]{2,1,0:T(8,128)S(1)}, f32[4,192,128]{2,1,0:T(8,128)S(1)}, u32[]{:S(2)}, u32[]{:S(2)}) %collective-permute-start.28) | collective-permute-done | bytes 393248 | tf_op jit(solution)/shard_map/ppermute | solution.py:16
  361.1 5.1 %collective-permute-done.29 = f32[4,192,128]{2,1,0:T(8,128)S(1)} collective-permute-done((f32[4,192,128]{2,1,0:T(8,128)S(1)}, f32[4,192,128]{2,1,0:T(8,128)S(1)}, u32[]{:S(2)}, u32[]{:S(2)}) %collective-permute-start.29) | collective-permute-done | bytes 393248 | tf_op jit(solution)/shard_map/ppermute | solution.py:15
  368.9 4.5 collective-permute-start.31
  376.3 5.3 %collective-permute-done.30 = f32[4,192,128]{2,1,0:T(8,128)S(1)} collective-permute-done((f32[4,192,128]{2,1,0:T(8,128)S(1)}, f32[4,192,128]{2,1,0:T(8,128)S(1)}, u32[]{:S(2)}, u32[]{:S(2)}) %collective-permute-start.30) | collective-permute-done | bytes 393248 | tf_op jit(solution)/shard_map/ppermute | solution.py:16
  381.5 5.2 %collective-permute-done.31 = f32[4,192,128]{2,1,0:T(8,128)S(1)} collective-permute-done((f32[4,192,128]{2,1,0:T(8,128)S(1)}, f32[4,192,128]{2,1,0:T(8,128)S(1)}, u32[]{:S(2)}, u32[]{:S(2)}) %collective-permute-start.31) | collective-permute-done | bytes 393248 | tf_op jit(solution)/shard_map/ppermute | solution.py:15
  389.4 4.5 collective-permute-start.33
  397.0 5.1 %collective-permute-done.32 = f32[4,192,128]{2,1,0:T(8,128)S(1)} collective-permute-done((f32[4,192,128]{2,1,0:T(8,128)S(1)}, f32[4,192,128]{2,1,0:T(8,128)S(1)}, u32[]{:S(2)}, u32[]{:S(2)}) %collective-permute-start.32) | collective-permute-done | bytes 393248 | tf_op jit(solution)/shard_map/ppermute | solution.py:16
  402.1 6.9 %collective-permute-done.33 = f32[4,192,128]{2,1,0:T(8,128)S(1)} collective-permute-done((f32[4,192,128]{2,1,0:T(8,128)S(1)}, f32[4,192,128]{2,1,0:T(8,128)S(1)}, u32[]{:S(2)}, u32[]{:S(2)}) %collective-permute-start.33) | collective-permute-done | bytes 393248 | tf_op jit(solution)/shard_map/ppermute | solution.py:15
  411.6 4.5 collective-permute-start.35
  419.0 5.3 %collective-permute-done.34 = f32[4,192,128]{2,1,0:T(8,128)S(1)} collective-permute-done((f32[4,192,128]{2,1,0:T(8,128)S(1)}, f32[4,192,128]{2,1,0:T(8,128)S(1)}, u32[]{:S(2)}, u32[]{:S(2)}) %collective-permute-start.34) | collective-permute-done | bytes 393248 | tf_op jit(solution)/shard_map/ppermute | solution.py:16
  424.3 8.1 %collective-permute-done.35 = f32[4,192,128]{2,1,0:T(8,128)S(1)} collective-permute-done((f32[4,192,128]{2,1,0:T(8,128)S(1)}, f32[4,192,128]{2,1,0:T(8,128)S(1)}, u32[]{:S(2)}, u32[]{:S(2)}) %collective-permute-start.35) | collective-permute-done | bytes 393248 | tf_op jit(solution)/shard_map/ppermute | solution.py:15
  435.0 4.5 collective-permute-start.37
  442.4 5.3 %collective-permute-done.36 = f32[4,192,128]{2,1,0:T(8,128)S(1)} collective-permute-done((f32[4,192,128]{2,1,0:T(8,128)S(1)}, f32[4,192,128]{2,1,0:T(8,128)S(1)}, u32[]{:S(2)}, u32[]{:S(2)}) %collective-permute-start.36) | collective-permute-done | bytes 393248 | tf_op jit(solution)/shard_map/ppermute | solution.py:16
  447.7 5.1 %collective-permute-done.37 = f32[4,192,128]{2,1,0:T(8,128)S(1)} collective-permute-done((f32[4,192,128]{2,1,0:T(8,128)S(1)}, f32[4,192,128]{2,1,0:T(8,128)S(1)}, u32[]{:S(2)}, u32[]{:S(2)}) %collective-permute-start.37) | collective-permute-done | bytes 393248 | tf_op jit(solution)/shard_map/ppermute | solution.py:15
  455.4 4.5 collective-permute-start.39
  463.0 5.1 %collective-permute-done.38 = f32[4,192,128]{2,1,0:T(8,128)S(1)} collective-permute-done((f32[4,192,128]{2,1,0:T(8,128)S(1)}, f32[4,192,128]{2,1,0:T(8,128)S(1)}, u32[]{:S(2)}, u32[]{:S(2)}) %collective-permute-start.38) | collective-permute-done | bytes 393248 | tf_op jit(solution)/shard_map/ppermute | solution.py:16
  468.1 5.2 %collective-permute-done.39 = f32[4,192,128]{2,1,0:T(8,128)S(1)} collective-permute-done((f32[4,192,128]{2,1,0:T(8,128)S(1)}, f32[4,192,128]{2,1,0:T(8,128)S(1)}, u32[]{:S(2)}, u32[]{:S(2)}) %collective-permute-start.39) | collective-permute-done | bytes 393248 | tf_op jit(solution)/shard_map/ppermute | solution.py:15
  477.5 4.0 collective-permute-start.41
  481.5 6.3 %collective-permute-done.41 = f32[8,48,128]{2,1,0:T(8,128)S(1)} collective-permute-done((f32[8,48,128]{2,1,0:T(8,128)S(1)}, f32[8,48,128]{2,1,0:T(8,128)S(1)}, u32[]{:S(2)}, u32[]{:S(2)}) %collective-permute-start.41) | collective-permute-done | bytes 196640 | tf_op jit(solution)/shard_map/ppermute | solution.py:144
  (251 shorter events, 222.8 us)
Async XLA Ops:
  0.0 8.8 %copy-start.49 = (s32[1,128]{1,0:T(1,128)S(1)}, s32[1,128]{1,0:T(1,128)}, u32[]{:S(2)}) copy-start(s32[1,128]{1,0:T(1,128)} %param.15) | copy-start | bytes 1540
  0.0 8.8 %copy-start.48 = (f32[1,10,128]{2,0,1:T(1,128)S(1)}, f32[1,10,128]{2,0,1:T(1,128)}, u32[]{:S(2)}) copy-start(f32[1,10,128]{2,0,1:T(1,128)} %param.16) | copy-start | bytes 15364
  2.1 26.4 %collective-permute-start = (f32[4,192,128]{2,1,0:T(8,128)}, f32[4,192,128]{2,1,0:T(8,128)S(1)}, u32[]{:S(2)}, u32[]{:S(2)}) collective-permute-start(f32[4,192,128]{2,1,0:T(8,128)} %get-tuple-element.96), channel_id=1, source_target_pairs={{4,0},{8,4},{12,8},{16,12},{20,16},{24,20},{28,24},{32,28},{36,32}... | collective-permute-start | bytes 1179656 | tf_op jit(solution)/shard_map/ppermute | solution.py:16
  4.5 23.9 %collective-permute-start.1 = (f32[4,192,128]{2,1,0:T(8,128)}, f32[4,192,128]{2,1,0:T(8,128)}, u32[]{:S(2)}, u32[]{:S(2)}) collective-permute-start(f32[4,192,128]{2,1,0:T(8,128)} %get-tuple-element.95), channel_id=1, source_target_pairs={{0,4},{4,8},{8,12},{12,16},{16,20},{20,24},{24,28},{28,32},{32,36}... | collective-permute-start | bytes 1179656 | tf_op jit(solution)/shard_map/ppermute | solution.py:15
  31.0 15.2 %collective-permute-start.2 = (f32[4,192,128]{2,1,0:T(8,128)}, f32[4,192,128]{2,1,0:T(8,128)}, u32[]{:S(2)}, u32[]{:S(2)}) collective-permute-start(f32[4,192,128]{2,1,0:T(8,128)} %get-tuple-element.94), channel_id=1, source_target_pairs={{4,0},{8,4},{12,8},{16,12},{20,16},{24,20},{28,24},{32,28},{36,32}... | collective-permute-start | bytes 1179656 | tf_op jit(solution)/shard_map/ppermute | solution.py:16
  32.9 18.9 %collective-permute-start.3 = (f32[4,192,128]{2,1,0:T(8,128)}, f32[4,192,128]{2,1,0:T(8,128)}, u32[]{:S(2)}, u32[]{:S(2)}) collective-permute-start(f32[4,192,128]{2,1,0:T(8,128)} %get-tuple-element.93), channel_id=1, source_target_pairs={{0,4},{4,8},{8,12},{12,16},{16,20},{20,24},{24,28},{28,32},{32,36}... | collective-permute-start | bytes 1179656 | tf_op jit(solution)/shard_map/ppermute | solution.py:15
  54.8 15.1 %collective-permute-start.4 = (f32[4,192,128]{2,1,0:T(8,128)}, f32[4,192,128]{2,1,0:T(8,128)}, u32[]{:S(2)}, u32[]{:S(2)}) collective-permute-start(f32[4,192,128]{2,1,0:T(8,128)} %get-tuple-element.92), channel_id=1, source_target_pairs={{4,0},{8,4},{12,8},{16,12},{20,16},{24,20},{28,24},{32,28},{36,32}... | collective-permute-start | bytes 1179656 | tf_op jit(solution)/shard_map/ppermute | solution.py:16
  58.1 22.7 %collective-permute-start.5 = (f32[4,192,128]{2,1,0:T(8,128)}, f32[4,192,128]{2,1,0:T(8,128)}, u32[]{:S(2)}, u32[]{:S(2)}) collective-permute-start(f32[4,192,128]{2,1,0:T(8,128)} %get-tuple-element.91), channel_id=1, source_target_pairs={{0,4},{4,8},{8,12},{12,16},{16,20},{20,24},{24,28},{28,32},{32,36}... | collective-permute-start | bytes 1179656 | tf_op jit(solution)/shard_map/ppermute | solution.py:15
  83.8 15.1 %collective-permute-start.6 = (f32[4,192,128]{2,1,0:T(8,128)}, f32[4,192,128]{2,1,0:T(8,128)}, u32[]{:S(2)}, u32[]{:S(2)}) collective-permute-start(f32[4,192,128]{2,1,0:T(8,128)} %get-tuple-element.90), channel_id=1, source_target_pairs={{4,0},{8,4},{12,8},{16,12},{20,16},{24,20},{28,24},{32,28},{36,32}... | collective-permute-start | bytes 1179656 | tf_op jit(solution)/shard_map/ppermute | solution.py:16
  86.0 20.9 %collective-permute-start.7 = (f32[4,192,128]{2,1,0:T(8,128)}, f32[4,192,128]{2,1,0:T(8,128)}, u32[]{:S(2)}, u32[]{:S(2)}) collective-permute-start(f32[4,192,128]{2,1,0:T(8,128)} %get-tuple-element.89), channel_id=1, source_target_pairs={{0,4},{4,8},{8,12},{12,16},{16,20},{20,24},{24,28},{28,32},{32,36}... | collective-permute-start | bytes 1179656 | tf_op jit(solution)/shard_map/ppermute | solution.py:15
  109.9 15.1 %collective-permute-start.8 = (f32[4,192,128]{2,1,0:T(8,128)}, f32[4,192,128]{2,1,0:T(8,128)}, u32[]{:S(2)}, u32[]{:S(2)}) collective-permute-start(f32[4,192,128]{2,1,0:T(8,128)} %get-tuple-element.88), channel_id=1, source_target_pairs={{4,0},{8,4},{12,8},{16,12},{20,16},{24,20},{28,24},{32,28},{36,32}... | collective-permute-start | bytes 1179656 | tf_op jit(solution)/shard_map/ppermute | solution.py:16
  112.1 18.6 %collective-permute-start.9 = (f32[4,192,128]{2,1,0:T(8,128)}, f32[4,192,128]{2,1,0:T(8,128)}, u32[]{:S(2)}, u32[]{:S(2)}) collective-permute-start(f32[4,192,128]{2,1,0:T(8,128)} %get-tuple-element.87), channel_id=1, source_target_pairs={{0,4},{4,8},{8,12},{12,16},{16,20},{20,24},{24,28},{28,32},{32,36}... | collective-permute-start | bytes 1179656 | tf_op jit(solution)/shard_map/ppermute | solution.py:15
  133.8 15.1 %collective-permute-start.10 = (f32[4,192,128]{2,1,0:T(8,128)}, f32[4,192,128]{2,1,0:T(8,128)}, u32[]{:S(2)}, u32[]{:S(2)}) collective-permute-start(f32[4,192,128]{2,1,0:T(8,128)} %get-tuple-element.86), channel_id=1, source_target_pairs={{4,0},{8,4},{12,8},{16,12},{20,16},{24,20},{28,24},{32,28},{36,32}... | collective-permute-start | bytes 1179656 | tf_op jit(solution)/shard_map/ppermute | solution.py:16
  136.0 18.6 %collective-permute-start.11 = (f32[4,192,128]{2,1,0:T(8,128)}, f32[4,192,128]{2,1,0:T(8,128)}, u32[]{:S(2)}, u32[]{:S(2)}) collective-permute-start(f32[4,192,128]{2,1,0:T(8,128)} %get-tuple-element.85), channel_id=1, source_target_pairs={{0,4},{4,8},{8,12},{12,16},{16,20},{20,24},{24,28},{28,32},{32,36}... | collective-permute-start | bytes 1179656 | tf_op jit(solution)/shard_map/ppermute | solution.py:15
  156.6 41.0 %copy-start.1 = (f32[8,192,128]{2,1,0:T(8,128)}, f32[8,192,128]{2,1,0:T(8,128)S(1)}, u32[]{:S(2)}) copy-start(f32[8,192,128]{2,1,0:T(8,128)S(1)} %fusion.121) | copy-start | bytes 2359300
  157.6 15.1 %collective-permute-start.12 = (f32[4,192,128]{2,1,0:T(8,128)}, f32[4,192,128]{2,1,0:T(8,128)}, u32[]{:S(2)}, u32[]{:S(2)}) collective-permute-start(f32[4,192,128]{2,1,0:T(8,128)} %get-tuple-element.84), channel_id=1, source_target_pairs={{4,0},{8,4},{12,8},{16,12},{20,16},{24,20},{28,24},{32,28},{36,32}... | collective-permute-start | bytes 1179656 | tf_op jit(solution)/shard_map/ppermute | solution.py:16
  159.8 17.5 %collective-permute-start.13 = (f32[4,192,128]{2,1,0:T(8,128)}, f32[4,192,128]{2,1,0:T(8,128)}, u32[]{:S(2)}, u32[]{:S(2)}) collective-permute-start(f32[4,192,128]{2,1,0:T(8,128)} %get-tuple-element.83), channel_id=1, source_target_pairs={{0,4},{4,8},{8,12},{12,16},{16,20},{20,24},{24,28},{28,32},{32,36}... | collective-permute-start | bytes 1179656 | tf_op jit(solution)/shard_map/ppermute | solution.py:15
  179.3 18.3 %copy-start.16 = (f32[1536,128]{1,0:T(8,128)S(1)}, f32[1536,128]{1,0:T(8,128)}, u32[]{:S(2)}) copy-start(f32[1536,128]{1,0:T(8,128)} %fusion.934) | copy-start | bytes 2359300
  180.2 22.7 %collective-permute-start.14 = (f32[4,192,128]{2,1,0:T(8,128)}, f32[4,192,128]{2,1,0:T(8,128)}, u32[]{:S(2)}, u32[]{:S(2)}) collective-permute-start(f32[4,192,128]{2,1,0:T(8,128)} %get-tuple-element.82), channel_id=1, source_target_pairs={{4,0},{8,4},{12,8},{16,12},{20,16},{24,20},{28,24},{32,28},{36,32}... | collective-permute-start | bytes 1179656 | tf_op jit(solution)/shard_map/ppermute | solution.py:16
  182.4 20.5 %collective-permute-start.15 = (f32[4,192,128]{2,1,0:T(8,128)}, f32[4,192,128]{2,1,0:T(8,128)}, u32[]{:S(2)}, u32[]{:S(2)}) collective-permute-start(f32[4,192,128]{2,1,0:T(8,128)} %get-tuple-element.81), channel_id=1, source_target_pairs={{0,4},{4,8},{8,12},{12,16},{16,20},{20,24},{24,28},{28,32},{32,36}... | collective-permute-start | bytes 1179656 | tf_op jit(solution)/shard_map/ppermute | solution.py:15
  205.5 15.0 %collective-permute-start.16 = (f32[4,192,128]{2,1,0:T(8,128)}, f32[4,192,128]{2,1,0:T(8,128)S(1)}, u32[]{:S(2)}, u32[]{:S(2)}) collective-permute-start(f32[4,192,128]{2,1,0:T(8,128)} %get-tuple-element.80), channel_id=1, source_target_pairs={{4,0},{8,4},{12,8},{16,12},{20,16},{24,20},{28,24},{32,28},{36,32}... | collective-permute-start | bytes 1179656 | tf_op jit(solution)/shard_map/ppermute | solution.py:16
  208.4 19.7 %collective-permute-start.17 = (f32[4,192,128]{2,1,0:T(8,128)S(1)}, f32[4,192,128]{2,1,0:T(8,128)}, u32[]{:S(2)}, u32[]{:S(2)}) collective-permute-start(f32[4,192,128]{2,1,0:T(8,128)S(1)} %get-tuple-element.79), channel_id=1, source_target_pairs={{0,4},{4,8},{8,12},{12,16},{16,20},{20,24},{24,28},{28,32},{32,36}... | collective-permute-start | bytes 1179656 | tf_op jit(solution)/shard_map/ppermute | solution.py:15
  231.1 19.8 %collective-permute-start.18 = (f32[4,192,128]{2,1,0:T(8,128)}, f32[4,192,128]{2,1,0:T(8,128)}, u32[]{:S(2)}, u32[]{:S(2)}) collective-permute-start(f32[4,192,128]{2,1,0:T(8,128)} %get-tuple-element.78), channel_id=1, source_target_pairs={{4,0},{8,4},{12,8},{16,12},{20,16},{24,20},{28,24},{32,28},{36,32}... | collective-permute-start | bytes 1179656 | tf_op jit(solution)/shard_map/ppermute | solution.py:16
  233.2 22.2 %collective-permute-start.19 = (f32[4,192,128]{2,1,0:T(8,128)}, f32[4,192,128]{2,1,0:T(8,128)}, u32[]{:S(2)}, u32[]{:S(2)}) collective-permute-start(f32[4,192,128]{2,1,0:T(8,128)} %get-tuple-element.77), channel_id=1, source_target_pairs={{0,4},{4,8},{8,12},{12,16},{16,20},{20,24},{24,28},{28,32},{32,36}... | collective-permute-start | bytes 1179656 | tf_op jit(solution)/shard_map/ppermute | solution.py:15
  243.1 12.3 %copy-start.25 = (f32[8,192,128]{2,1,0:T(8,128)S(1)}, f32[8,192,128]{2,1,0:T(8,128)}, u32[]{:S(2)}) copy-start(f32[8,192,128]{2,1,0:T(8,128)} %get-tuple-element.38) | copy-start | bytes 2359300
  244.1 22.7 %collective-permute-start.20 = (f32[4,192,128]{2,1,0:T(8,128)}, f32[4,192,128]{2,1,0:T(8,128)}, u32[]{:S(2)}, u32[]{:S(2)}) collective-permute-start(f32[4,192,128]{2,1,0:T(8,128)} %get-tuple-element.76), channel_id=1, source_target_pairs={{4,0},{8,4},{12,8},{16,12},{20,16},{24,20},{28,24},{32,28},{36,32}... | collective-permute-start | bytes 1179656 | tf_op jit(solution)/shard_map/ppermute | solution.py:16
  246.8 22.3 %collective-permute-start.21 = (f32[4,192,128]{2,1,0:T(8,128)}, f32[4,192,128]{2,1,0:T(8,128)}, u32[]{:S(2)}, u32[]{:S(2)}) collective-permute-start(f32[4,192,128]{2,1,0:T(8,128)} %get-tuple-element.75), channel_id=1, source_target_pairs={{0,4},{4,8},{8,12},{12,16},{16,20},{20,24},{24,28},{28,32},{32,36}... | collective-permute-start | bytes 1179656 | tf_op jit(solution)/shard_map/ppermute | solution.py:15
  271.0 27.5 %collective-permute-start.22 = (f32[4,192,128]{2,1,0:T(8,128)S(1)}, f32[4,192,128]{2,1,0:T(8,128)S(1)}, u32[]{:S(2)}, u32[]{:S(2)}) collective-permute-start(f32[4,192,128]{2,1,0:T(8,128)S(1)} %get-tuple-element.74), channel_id=1, source_target_pairs={{4,0},{8,4},{12,8},{16,12},{20,16},{24,20},{28,24},{32,28},{36,32}... | collective-permute-start | bytes 1179656 | tf_op jit(solution)/shard_map/ppermute | solution.py:16
  273.2 25.3 %collective-permute-start.23 = (f32[4,192,128]{2,1,0:T(8,128)S(1)}, f32[4,192,128]{2,1,0:T(8,128)S(1)}, u32[]{:S(2)}, u32[]{:S(2)}) collective-permute-start(f32[4,192,128]{2,1,0:T(8,128)S(1)} %get-tuple-element.73), channel_id=1, source_target_pairs={{0,4},{4,8},{8,12},{12,16},{16,20},{20,24},{24,28},{28,32},{32,36}... | collective-permute-start | bytes 1179656 | tf_op jit(solution)/shard_map/ppermute | solution.py:15
  298.8 14.9 %collective-permute-start.24 = (f32[4,192,128]{2,1,0:T(8,128)S(1)}, f32[4,192,128]{2,1,0:T(8,128)S(1)}, u32[]{:S(2)}, u32[]{:S(2)}) collective-permute-start(f32[4,192,128]{2,1,0:T(8,128)S(1)} %get-tuple-element.70), channel_id=1, source_target_pairs={{4,0},{8,4},{12,8},{16,12},{20,16},{24,20},{28,24},{32,28},{36,32}... | collective-permute-start | bytes 1179656 | tf_op jit(solution)/shard_map/ppermute | solution.py:16
  303.8 19.7 %collective-permute-start.25 = (f32[4,192,128]{2,1,0:T(8,128)S(1)}, f32[4,192,128]{2,1,0:T(8,128)S(1)}, u32[]{:S(2)}, u32[]{:S(2)}) collective-permute-start(f32[4,192,128]{2,1,0:T(8,128)S(1)} %get-tuple-element.69), channel_id=1, source_target_pairs={{0,4},{4,8},{8,12},{12,16},{16,20},{20,24},{24,28},{28,32},{32,36}... | collective-permute-start | bytes 1179656 | tf_op jit(solution)/shard_map/ppermute | solution.py:15
  323.8 15.0 %collective-permute-start.26 = (f32[4,192,128]{2,1,0:T(8,128)S(1)}, f32[4,192,128]{2,1,0:T(8,128)S(1)}, u32[]{:S(2)}, u32[]{:S(2)}) collective-permute-start(f32[4,192,128]{2,1,0:T(8,128)S(1)} %get-tuple-element.66), channel_id=1, source_target_pairs={{4,0},{8,4},{12,8},{16,12},{20,16},{24,20},{28,24},{32,28},{36,32}... | collective-permute-start | bytes 1179656 | tf_op jit(solution)/shard_map/ppermute | solution.py:16
  326.2 19.7 %collective-permute-start.27 = (f32[4,192,128]{2,1,0:T(8,128)S(1)}, f32[4,192,128]{2,1,0:T(8,128)S(1)}, u32[]{:S(2)}, u32[]{:S(2)}) collective-permute-start(f32[4,192,128]{2,1,0:T(8,128)S(1)} %get-tuple-element.65), channel_id=1, source_target_pairs={{0,4},{4,8},{8,12},{12,16},{16,20},{20,24},{24,28},{28,32},{32,36}... | collective-permute-start | bytes 1179656 | tf_op jit(solution)/shard_map/ppermute | solution.py:15
  346.2 15.0 %collective-permute-start.28 = (f32[4,192,128]{2,1,0:T(8,128)S(1)}, f32[4,192,128]{2,1,0:T(8,128)S(1)}, u32[]{:S(2)}, u32[]{:S(2)}) collective-permute-start(f32[4,192,128]{2,1,0:T(8,128)S(1)} %get-tuple-element.62), channel_id=1, source_target_pairs={{4,0},{8,4},{12,8},{16,12},{20,16},{24,20},{28,24},{32,28},{36,32}... | collective-permute-start | bytes 1179656 | tf_op jit(solution)/shard_map/ppermute | solution.py:16
  348.5 17.7 %collective-permute-start.29 = (f32[4,192,128]{2,1,0:T(8,128)S(1)}, f32[4,192,128]{2,1,0:T(8,128)S(1)}, u32[]{:S(2)}, u32[]{:S(2)}) collective-permute-start(f32[4,192,128]{2,1,0:T(8,128)S(1)} %get-tuple-element.61), channel_id=1, source_target_pairs={{0,4},{4,8},{8,12},{12,16},{16,20},{20,24},{24,28},{28,32},{32,36}... | collective-permute-start | bytes 1179656 | tf_op jit(solution)/shard_map/ppermute | solution.py:15
  366.6 15.0 %collective-permute-start.30 = (f32[4,192,128]{2,1,0:T(8,128)S(1)}, f32[4,192,128]{2,1,0:T(8,128)S(1)}, u32[]{:S(2)}, u32[]{:S(2)}) collective-permute-start(f32[4,192,128]{2,1,0:T(8,128)S(1)} %get-tuple-element.58), channel_id=1, source_target_pairs={{4,0},{8,4},{12,8},{16,12},{20,16},{24,20},{28,24},{32,28},{36,32}... | collective-permute-start | bytes 1179656 | tf_op jit(solution)/shard_map/ppermute | solution.py:16
  368.9 17.8 %collective-permute-start.31 = (f32[4,192,128]{2,1,0:T(8,128)S(1)}, f32[4,192,128]{2,1,0:T(8,128)S(1)}, u32[]{:S(2)}, u32[]{:S(2)}) collective-permute-start(f32[4,192,128]{2,1,0:T(8,128)S(1)} %get-tuple-element.57), channel_id=1, source_target_pairs={{0,4},{4,8},{8,12},{12,16},{16,20},{20,24},{24,28},{28,32},{32,36}... | collective-permute-start | bytes 1179656 | tf_op jit(solution)/shard_map/ppermute | solution.py:15
  387.1 15.0 %collective-permute-start.32 = (f32[4,192,128]{2,1,0:T(8,128)S(1)}, f32[4,192,128]{2,1,0:T(8,128)S(1)}, u32[]{:S(2)}, u32[]{:S(2)}) collective-permute-start(f32[4,192,128]{2,1,0:T(8,128)S(1)} %get-tuple-element.54), channel_id=1, source_target_pairs={{4,0},{8,4},{12,8},{16,12},{20,16},{24,20},{28,24},{32,28},{36,32}... | collective-permute-start | bytes 1179656 | tf_op jit(solution)/shard_map/ppermute | solution.py:16
  389.4 19.5 %collective-permute-start.33 = (f32[4,192,128]{2,1,0:T(8,128)S(1)}, f32[4,192,128]{2,1,0:T(8,128)S(1)}, u32[]{:S(2)}, u32[]{:S(2)}) collective-permute-start(f32[4,192,128]{2,1,0:T(8,128)S(1)} %get-tuple-element.53), channel_id=1, source_target_pairs={{0,4},{4,8},{8,12},{12,16},{16,20},{20,24},{24,28},{28,32},{32,36}... | collective-permute-start | bytes 1179656 | tf_op jit(solution)/shard_map/ppermute | solution.py:15
  409.3 15.0 %collective-permute-start.34 = (f32[4,192,128]{2,1,0:T(8,128)S(1)}, f32[4,192,128]{2,1,0:T(8,128)S(1)}, u32[]{:S(2)}, u32[]{:S(2)}) collective-permute-start(f32[4,192,128]{2,1,0:T(8,128)S(1)} %get-tuple-element.50), channel_id=1, source_target_pairs={{4,0},{8,4},{12,8},{16,12},{20,16},{24,20},{28,24},{32,28},{36,32}... | collective-permute-start | bytes 1179656 | tf_op jit(solution)/shard_map/ppermute | solution.py:16
  411.6 20.7 %collective-permute-start.35 = (f32[4,192,128]{2,1,0:T(8,128)S(1)}, f32[4,192,128]{2,1,0:T(8,128)S(1)}, u32[]{:S(2)}, u32[]{:S(2)}) collective-permute-start(f32[4,192,128]{2,1,0:T(8,128)S(1)} %get-tuple-element.49), channel_id=1, source_target_pairs={{0,4},{4,8},{8,12},{12,16},{16,20},{20,24},{24,28},{28,32},{32,36}... | collective-permute-start | bytes 1179656 | tf_op jit(solution)/shard_map/ppermute | solution.py:15
  432.7 15.0 %collective-permute-start.36 = (f32[4,192,128]{2,1,0:T(8,128)S(1)}, f32[4,192,128]{2,1,0:T(8,128)S(1)}, u32[]{:S(2)}, u32[]{:S(2)}) collective-permute-start(f32[4,192,128]{2,1,0:T(8,128)S(1)} %get-tuple-element.46), channel_id=1, source_target_pairs={{4,0},{8,4},{12,8},{16,12},{20,16},{24,20},{28,24},{32,28},{36,32}... | collective-permute-start | bytes 1179656 | tf_op jit(solution)/shard_map/ppermute | solution.py:16
  435.0 17.7 %collective-permute-start.37 = (f32[4,192,128]{2,1,0:T(8,128)S(1)}, f32[4,192,128]{2,1,0:T(8,128)S(1)}, u32[]{:S(2)}, u32[]{:S(2)}) collective-permute-start(f32[4,192,128]{2,1,0:T(8,128)S(1)} %get-tuple-element.45), channel_id=1, source_target_pairs={{0,4},{4,8},{8,12},{12,16},{16,20},{20,24},{24,28},{28,32},{32,36}... | collective-permute-start | bytes 1179656 | tf_op jit(solution)/shard_map/ppermute | solution.py:15
  453.1 15.0 %collective-permute-start.38 = (f32[4,192,128]{2,1,0:T(8,128)S(1)}, f32[4,192,128]{2,1,0:T(8,128)S(1)}, u32[]{:S(2)}, u32[]{:S(2)}) collective-permute-start(f32[4,192,128]{2,1,0:T(8,128)S(1)} %get-tuple-element.42), channel_id=1, source_target_pairs={{4,0},{8,4},{12,8},{16,12},{20,16},{24,20},{28,24},{32,28},{36,32}... | collective-permute-start | bytes 1179656 | tf_op jit(solution)/shard_map/ppermute | solution.py:16
  455.4 17.8 %collective-permute-start.39 = (f32[4,192,128]{2,1,0:T(8,128)S(1)}, f32[4,192,128]{2,1,0:T(8,128)S(1)}, u32[]{:S(2)}, u32[]{:S(2)}) collective-permute-start(f32[4,192,128]{2,1,0:T(8,128)S(1)} %get-tuple-element.41), channel_id=1, source_target_pairs={{0,4},{4,8},{8,12},{12,16},{16,20},{20,24},{24,28},{28,32},{32,36}... | collective-permute-start | bytes 1179656 | tf_op jit(solution)/shard_map/ppermute | solution.py:15
  462.9 10.6 %copy-start.13 = (f32[8,192,128]{2,1,0:T(8,128)S(1)}, f32[8,192,128]{2,1,0:T(8,128)}, u32[]{:S(2)}) copy-start(f32[8,192,128]{2,1,0:T(8,128)} %get-tuple-element.21) | copy-start | bytes 2359300
  473.8 3.6 collective-permute-start.40
  477.5 10.3 %collective-permute-start.41 = (f32[8,48,128]{2,1,0:T(8,128)S(1)}, f32[8,48,128]{2,1,0:T(8,128)S(1)}, u32[]{:S(2)}, u32[]{:S(2)}) collective-permute-start(f32[8,48,128]{2,1,0:T(8,128)S(1)} %dynamic-slice_bitcast_fusion), channel_id=1, source_target_pairs={{0,2},{1,3},{2,0},{3,1},{4,6},{5,7},{6,4},{7,5},{8,10},{9,11},{10,... | collective-permute-start | bytes 589832 | tf_op jit(solution)/shard_map/ppermute | solution.py:144
  (46 other events, 190.5 us)
